TPU v7x, 32 devices: a whole 2x2x4 slice. The times are simulated.
32 devices in a mesh: replica: 2 (over y), shard: 16 (over z, x, core).
Axes of the slice: x: 2, y: 2, z: 4, core: 2. Of those that a mesh axis runs over, the one named last changes fastest.
Arguments:
- inputs: bfloat16 [2, 2, 2048, 2048], P('replica', None, 'shard'), may hold values from -6 to 6
- cotangent: bfloat16 [2, 2, 2048, 2048], P('replica', None, 'shard'), may hold values from -6 to 6
- lengths: int32 [2, 2, 4], P('replica'), may hold values from 1 to 1024, 2048 in all within a row
- padding: int32 [2, 2, 2048], P('replica', None, 'shard'), may hold values 0 or 1
- attention_norm_gain: bfloat16 [2048], P('shard'), may hold values from 0.5 to 1.5
- joint_projection_weight: bfloat16 [2048, 3072], P('shard'), may hold values from -0.125 to 0.125
- adapter_down_factors: bfloat16 [2048, 24], P('shard'), may hold values from -0.125 to 0.125
- adapter_up_factors: bfloat16 [8, 3072], P(None, 'shard'), may hold values from -0.59765625 to 0.59765625
- output_weight: bfloat16 [2048, 2048], P('shard'), may hold values from -0.75 to 0.75
- adapter_output_down: bfloat16 [2048, 8], P('shard'), may hold values from -0.75 to 0.75
- adapter_output_upper: bfloat16 [8, 2048], P(None, 'shard'), may hold values from -1.796875 to 1.796875
- feature_query_map: bfloat16 [2048, 64], P('shard'), may hold values from -0.75 to 0.75
- feature_key_map: bfloat16 [512, 64], P('shard'), may hold values from -0.75 to 0.75
- feedforward_norm_gain: bfloat16 [2048], P('shard'), may hold values from 0.5 to 1.5
- gate_up_weight: bfloat16 [2048, 16384], P('shard'), may hold values from -0.125 to 0.125
- down_weight: bfloat16 [8192, 2048], P('shard'), may hold values from -0.0625 to 0.0625
Outputs:
- output: bfloat16 [2, 2, 2048, 2048], P('replica', None, 'shard')
- grad_inputs: bfloat16 [2, 2, 2048, 2048], P('replica', None, 'shard')
- grad_norm_attn: float32 [2048], P('shard')
- grad_w_qkv: float32 [2048, 3072], P('shard')
- grad_lora_down: float32 [2048, 24], P('shard')
- grad_lora_up: float32 [8, 3072], P(None, 'shard')
- grad_w_out: float32 [2048, 2048], P('shard')
- grad_lora_out_down: float32 [2048, 8], P('shard')
- grad_lora_out_up: float32 [8, 2048], P(None, 'shard')
- grad_feat_query: float32 [2048, 64], P('shard')
- grad_feat_key: float32 [512, 64], P('shard')
- grad_norm_ffn: float32 [2048], P('shard')
- grad_w_gate_up: float32 [2048, 16384], P('shard')
- grad_w_down: float32 [8192, 2048], P('shard')
Inputs may be any that keep to these rules, and one draw needn't show every extreme that they name: Each row of lengths sums to 2048, and its largest entry is 1024.
All inputs are finite; a program needn't handle non-finite values. No bound on the sum of `padding` on one device may be relied on, other than what follows from the above.
Results may differ from a plain program's by a relative error of at most 0.015.
The roundings to bfloat16 on the way count: a program that leaves them out, or rounds other values in their place, can miss the bound.
Values may be sent and summed in bfloat16 or wider, within the bound.
No kernel may reach another device: no remote copies, remote signals or barrier semaphores. Data moves between devices by JAX's collectives and lax.ppermute only.
A program may use at most 576 MiB of HBM per device.

v0:
```python
import math

import jax
import jax.numpy as jnp
from jax import lax
from jax.sharding import PartitionSpec as P

MODEL_WIDTH = 2048
HEADS = 32
KV_HEADS = 8
HEAD_DIM = 64
FF = 8192
ADAPTER_RANK = 8
WINDOW = 64


HIGHEST = lax.Precision.HIGHEST
NORM_EPS = 1e-05
ADAPTER_SCALE = 2.0
ROPE_BASE = 500000.0


def from_behind(shard, axis, by):
    peers = lax.axis_size(axis)
    pairs = [(i, i + by) for i in range(peers) if 0 <= i + by < peers]
    return lax.ppermute(shard, axis, pairs)


def entering(shard, axis, combine, identity):
    peers, place = (lax.axis_size(axis), lax.axis_index(axis))
    everything = jax.tree.map(
        lambda part, kind: lax.all_gather(part.astype(kind), axis),
        shard,
        (jnp.bfloat16, jnp.bfloat16, jnp.bfloat16),
    )
    start = jax.tree.map(
        lambda part, zero: jnp.broadcast_to(jnp.asarray(zero, part.dtype), part.shape),
        shard,
        identity,
    )

    def hop(k, before):
        reached = k < place
        new = combine(
            before, jax.tree.map(lambda part, own: part[k].astype(own.dtype), everything, shard)
        )
        return jax.tree.map(lambda a, b: jnp.where(reached, a, b), new, before)

    return lax.fori_loop(0, peers, hop, start)


def prefix(shard, axis, join, neutral):
    count = lax.axis_size(axis)
    place = lax.axis_index(axis)
    ahead = count - 1 - place
    gathered = jax.tree.map(
        lambda a, kind: lax.all_gather(a.astype(kind), axis),
        shard,
        jax.tree.map(lambda a: jnp.bfloat16 if a.dtype == jnp.float32 else a.dtype, shard),
    )
    state = jax.tree.map(lambda a, e: jnp.zeros_like(a) + jnp.asarray(e, a.dtype), shard, neutral)

    def one(hop, state):
        source = count - 1 - hop
        return join(
            state,
            jax.tree.map(
                lambda a, own: lax.dynamic_index_in_dim(a, source, 0, False).astype(own.dtype),
                gathered,
                shard,
            ),
        )

    return lax.fori_loop(0, ahead, one, state)


def shortened(shard):
    return jax.tree.map(lambda a: a.astype(jnp.bfloat16) if a.dtype == jnp.float32 else a, shard)


def forward_product(left, right):
    return jnp.dot(left, right, preferred_element_type=jnp.float32)


def contract_row_pairs(left, right):
    return lax.dot_general(
        left, right, (((0,), (0,)), ((), ())), preferred_element_type=jnp.float32
    )


def contract_columns(left, right):
    return lax.dot_general(
        left, right, (((1,), (1,)), ((), ())), preferred_element_type=jnp.float32
    )


def rotate(values, doc_place, head_count, sign_factor):
    half_dim = HEAD_DIM // 2
    frequency = ROPE_BASE ** (-(jnp.arange(half_dim, dtype=jnp.float32) * 2.0) / HEAD_DIM)
    angles = doc_place.astype(jnp.float32)[:, None] * frequency[None, :]
    cosine = jnp.cos(angles)[:, None, :]
    sine_part = sign_factor * jnp.sin(angles)[:, None, :]
    shaped = values.reshape(values.shape[0], head_count, HEAD_DIM)
    first_half = shaped[..., :half_dim]
    second = shaped[..., half_dim:]
    turned = jnp.concatenate(
        [first_half * cosine - second * sine_part, second * cosine + first_half * sine_part],
        axis=-1,
    )
    return turned.reshape(values.shape[0], head_count * HEAD_DIM)


def feature_map(values, weight, head_count):
    shaped = values.reshape(values.shape[0], head_count, HEAD_DIM)
    table = weight.reshape(head_count, HEAD_DIM, HEAD_DIM)
    mixed = jnp.einsum("rhi,hij->rhj", shaped, table, preferred_element_type=jnp.float32)
    return jnp.concatenate(
        [jax.nn.softmax(mixed, axis=-1), jax.nn.softmax(-mixed, axis=-1)], axis=-1
    )


def attend(
    queries,
    keys_ext,
    values_ext,
    seg_query,
    seg_ext,
    live_query,
    live_ext,
    state_sum,
    state_norm,
    state_tag,
    feature_query_map,
    feature_key_map,
):
    row_count = queries.shape[0]
    extent = keys_ext.shape[0]
    window = extent - row_count
    groups = HEADS // KV_HEADS
    query_heads = queries.astype(jnp.bfloat16).reshape(row_count, KV_HEADS, groups, HEAD_DIM)
    key_heads = keys_ext.astype(jnp.bfloat16).reshape(extent, KV_HEADS, HEAD_DIM)
    value_heads = values_ext.reshape(extent, KV_HEADS, HEAD_DIM)
    scores = jnp.einsum(
        "rkgd,jkd->kgrj", query_heads, key_heads, preferred_element_type=jnp.float32
    ) / math.sqrt(HEAD_DIM)
    offset = jnp.arange(row_count)[:, None] + window - jnp.arange(extent)[None, :]
    same_doc = seg_query[:, None] == seg_ext[None, :]
    live_key = live_ext[None, :] > 0
    in_window = (offset >= 0) & (offset < window) & same_doc & (live_key | (offset == 0))
    in_linear = (offset >= window) & same_doc & live_key
    row_top = jnp.max(jnp.where(in_window, scores, -1e30), axis=-1, keepdims=True)
    window_exp = jnp.exp(jnp.where(in_window, scores - row_top, -1e30))
    phi_query = feature_map(queries, feature_query_map, HEADS).reshape(
        row_count, KV_HEADS, groups, 2 * HEAD_DIM
    )
    phi_key = feature_map(keys_ext, feature_key_map, KV_HEADS)
    linear = jnp.einsum("rkgf,jkf->kgrj", phi_query, phi_key, precision=HIGHEST) * in_linear
    far_scale = jnp.exp(-row_top)
    weights = window_exp + far_scale * linear
    numerator = jnp.einsum("kgrj,jkd->kgrd", weights, value_heads, precision=HIGHEST)
    denominator = jnp.sum(weights, axis=-1)
    use_state = (seg_query == state_tag).astype(jnp.float32)
    carried = jnp.einsum("rkgf,kfd->kgrd", phi_query, state_sum, precision=HIGHEST)
    carried_norm = jnp.einsum("rkgf,kf->kgr", phi_query, state_norm, precision=HIGHEST)
    numerator = numerator + far_scale * use_state[:, None] * carried
    denominator = denominator + far_scale[..., 0] * use_state * carried_norm
    result = numerator / denominator[..., None] * live_query[:, None]
    return jnp.transpose(result, (2, 0, 1, 3)).reshape(row_count, HEADS * HEAD_DIM)


def state_terms(key_rows, value_rows, seg_rows, live_rows, state_tag, feature_key_map):
    phi_key = feature_map(key_rows, feature_key_map, KV_HEADS)
    chosen = ((seg_rows == state_tag) & (live_rows > 0)).astype(jnp.float32)
    phi_key = phi_key * chosen[:, None, None]
    value_heads = value_rows.reshape(value_rows.shape[0], KV_HEADS, HEAD_DIM)
    return (
        jnp.einsum("jkf,jkd->kfd", phi_key, value_heads, precision=HIGHEST),
        jnp.sum(phi_key, axis=0),
    )


def keep_latest(earlier, later):
    newest = jnp.maximum(earlier[2], later[2])
    take_early = (earlier[2] == newest).astype(jnp.float32)[0]
    take_late = (later[2] == newest).astype(jnp.float32)[0]
    return (
        earlier[0] * take_early + later[0] * take_late,
        earlier[1] * take_early + later[1] * take_late,
        newest,
    )


def keep_earliest(earlier, later):
    oldest = jnp.minimum(earlier[2], later[2])
    take_early = (earlier[2] == oldest).astype(jnp.float32)[0]
    take_late = (later[2] == oldest).astype(jnp.float32)[0]
    return (
        earlier[0] * take_early + later[0] * take_late,
        earlier[1] * take_early + later[1] * take_late,
        oldest,
    )


def gather_attention(shards):
    return (
        lax.all_gather(shards[0], "shard", axis=0, tiled=True),
        lax.all_gather(shards[1], "shard", axis=0, tiled=True),
        lax.all_gather(shards[2], "shard", axis=0, tiled=True),
        lax.all_gather(shards[3], "shard", axis=1, tiled=True),
        lax.all_gather(shards[4], "shard", axis=0, tiled=True),
        lax.all_gather(shards[5], "shard", axis=0, tiled=True),
        lax.all_gather(shards[6], "shard", axis=1, tiled=True),
        lax.all_gather(shards[7], "shard", axis=0, tiled=True),
        lax.all_gather(shards[8], "shard", axis=0, tiled=True),
    )


def gather_feedforward(shards):
    return (
        lax.all_gather(shards[0], "shard", axis=0, tiled=True),
        lax.all_gather(shards[1], "shard", axis=0, tiled=True),
        lax.all_gather(shards[2], "shard", axis=0, tiled=True),
    )


def ffn_sums_joined(acted, ffn_grad, normed_two, gate_up_grad):
    down_part = lax.psum_scatter(
        contract_row_pairs(acted, ffn_grad), "shard", scatter_dimension=0, tiled=True
    )
    gate_part = lax.psum_scatter(
        contract_row_pairs(normed_two, gate_up_grad), "shard", scatter_dimension=0, tiled=True
    )
    return (gate_part, down_part)


def per_device(
    inputs,
    cotangent,
    lengths,
    padding,
    attention_norm_gain,
    joint_projection_weight,
    adapter_down_factors,
    adapter_up_factors,
    output_weight,
    adapter_output_down,
    adapter_output_upper,
    feature_query_map,
    feature_key_map,
    feedforward_norm_gain,
    gate_up_weight,
    down_weight,
):
    micro_count = inputs.shape[1]
    tok_rows = inputs.shape[2]
    key_value_width = KV_HEADS * HEAD_DIM
    first_place = lax.axis_index("shard") * tok_rows
    attention_shards = (
        attention_norm_gain,
        joint_projection_weight,
        adapter_down_factors,
        adapter_up_factors,
        output_weight,
        adapter_output_down,
        adapter_output_upper,
        feature_query_map,
        feature_key_map,
    )
    feedforward_shards = (feedforward_norm_gain, gate_up_weight, down_weight)
    outputs = []
    input_grads = []
    attn_totals = ()
    ffn_totals = ()
    acted_list = []
    ffn_grad_list = []
    normed_two_list = []
    gate_grad_list = []
    for micro_index in range(micro_count):
        attention_full = gather_attention(attention_shards)
        feedforward_full = gather_feedforward(feedforward_shards)
        (
            gain_attn,
            merged_joint_weight,
            full_down,
            merged_up_factor,
            merged_output_weight,
            full_out_down,
            merged_output_up,
            full_featq,
            full_featk,
        ) = attention_full
        gain_ffn, full_gate_up, full_down_proj = feedforward_full
        activ = inputs[0, micro_index].astype(jnp.float32)
        live_own = padding[0, micro_index]
        doc_lengths = lengths[0, micro_index]
        doc_ends = jnp.cumsum(doc_lengths)
        places = first_place - WINDOW + jnp.arange(tok_rows + WINDOW, dtype=jnp.int32)
        finished = doc_ends[None, :] <= places[:, None]
        seg_ext = jnp.sum(finished.astype(jnp.int32), axis=1)
        doc_place = places - jnp.sum(jnp.where(finished, doc_lengths[None, :], 0), axis=1)
        seg_own = seg_ext[WINDOW:]
        place_own = doc_place[WINDOW:]
        gain_one = gain_attn.astype(jnp.float32)
        inv_one = lax.rsqrt(jnp.mean(activ * activ, axis=-1, keepdims=True) + NORM_EPS)
        normalized_input = (activ * inv_one * gain_one).astype(jnp.bfloat16)
        adapter_delta = forward_product(normalized_input, full_down).astype(jnp.bfloat16)
        adapter_products = jnp.concatenate(
            [
                forward_product(adapter_delta[:, :ADAPTER_RANK], merged_up_factor[:, :MODEL_WIDTH]),
                forward_product(
                    adapter_delta[:, ADAPTER_RANK : 2 * ADAPTER_RANK],
                    merged_up_factor[:, MODEL_WIDTH : MODEL_WIDTH + key_value_width],
                ),
                forward_product(
                    adapter_delta[:, 2 * ADAPTER_RANK :],
                    merged_up_factor[:, MODEL_WIDTH + key_value_width :],
                ),
            ],
            axis=1,
        )
        projected_rows = (
            forward_product(normalized_input, merged_joint_weight)
            + ADAPTER_SCALE * adapter_products
        )
        queries = rotate(projected_rows[:, :MODEL_WIDTH], place_own, HEADS, 1.0).astype(
            jnp.bfloat16
        )
        keys = rotate(
            projected_rows[:, MODEL_WIDTH : MODEL_WIDTH + key_value_width], place_own, KV_HEADS, 1.0
        ).astype(jnp.bfloat16)
        values = projected_rows[:, MODEL_WIDTH + key_value_width :].astype(jnp.bfloat16)
        live_tail = live_own[tok_rows - WINDOW :].astype(jnp.bfloat16)
        halo_k, halo_v, halo_live = from_behind(
            (keys[tok_rows - WINDOW :], values[tok_rows - WINDOW :], live_tail), "shard", 1
        )
        keys_ext = jnp.concatenate([halo_k, keys], axis=0).astype(jnp.float32)
        values_ext = jnp.concatenate([halo_v, values], axis=0).astype(jnp.float32)
        live_ext = jnp.concatenate(
            [halo_live.astype(jnp.float32), live_own.astype(jnp.float32)], axis=0
        )
        live_query = live_own.astype(jnp.float32)
        featq_full = full_featq.astype(jnp.float32)
        featk_full = full_featk.astype(jnp.float32)
        own_tag = seg_ext[tok_rows - 1]

        def contribute(key_rows, value_rows, featk_rows):
            return state_terms(
                key_rows, value_rows, seg_ext[:tok_rows], live_ext[:tok_rows], own_tag, featk_rows
            )

        (add_sum, add_norm), contribute_pull = jax.vjp(
            contribute, keys_ext[:tok_rows], values_ext[:tok_rows], featk_full
        )
        tag_value = own_tag.astype(jnp.float32).reshape(1)
        start_state = (
            jnp.zeros_like(add_sum),
            jnp.zeros_like(add_norm),
            jnp.full((1,), -1.0, jnp.float32),
        )
        prev_sum, prev_norm, prev_tag = entering(
            (add_sum, add_norm, tag_value), "shard", keep_latest, start_state
        )

        def local_attention(
            query_vals, key_vals, value_vals, state_sum, state_norm, featq_vals, featk_vals
        ):
            return attend(
                query_vals,
                key_vals,
                value_vals,
                seg_own,
                seg_ext,
                live_query,
                live_ext,
                state_sum,
                state_norm,
                prev_tag[0],
                featq_vals,
                featk_vals,
            )

        heads_out, attention_pull = jax.vjp(
            local_attention,
            queries.astype(jnp.float32),
            keys_ext,
            values_ext,
            prev_sum,
            prev_norm,
            featq_full,
            featk_full,
        )
        lowrank_heads = heads_out.astype(jnp.bfloat16)
        adapter_output_delta = forward_product(lowrank_heads, full_out_down).astype(jnp.bfloat16)
        branch_value = forward_product(
            lowrank_heads, merged_output_weight
        ) + ADAPTER_SCALE * forward_product(adapter_output_delta, merged_output_up)
        hidden = activ + branch_value
        gain_two = gain_ffn.astype(jnp.float32)
        inv_two = lax.rsqrt(jnp.mean(hidden * hidden, axis=-1, keepdims=True) + NORM_EPS)
        normed_two = (hidden * inv_two * gain_two).astype(jnp.bfloat16)
        gate_up = forward_product(normed_two, full_gate_up)
        gate = gate_up[:, :FF]
        upward = gate_up[:, FF:]
        sigmoid_gate = jax.nn.sigmoid(gate)
        swish = gate * sigmoid_gate
        acted = (swish * upward).astype(jnp.bfloat16)
        result = hidden + forward_product(acted, full_down_proj)
        outputs.append(result.astype(jnp.bfloat16))
        (
            gain_attn,
            merged_joint_weight,
            full_down,
            merged_up_factor,
            merged_output_weight,
            full_out_down,
            merged_output_up,
            full_featq,
            full_featk,
        ) = gather_attention(attention_shards)
        gain_ffn, full_gate_up, full_down_proj = gather_feedforward(feedforward_shards)
        upstream = cotangent[0, micro_index].astype(jnp.float32)
        ffn_grad = upstream.astype(jnp.bfloat16)
        acted_grad = contract_columns(ffn_grad, full_down_proj)
        swish_slope = sigmoid_gate * (1.0 + gate * (1.0 - sigmoid_gate))
        gate_up_grad = jnp.concatenate(
            [acted_grad * upward * swish_slope, acted_grad * swish], axis=1
        ).astype(jnp.bfloat16)
        acted_list.append(acted)
        ffn_grad_list.append(ffn_grad)
        normed_two_list.append(normed_two)
        gate_grad_list.append(gate_up_grad)
        normed_two_grad = contract_columns(gate_up_grad, full_gate_up)
        gain_two_term = jnp.sum(normed_two_grad * hidden * inv_two, axis=0)
        hidden_grad = (
            upstream
            + gain_two * inv_two * normed_two_grad
            - hidden
            * inv_two**3
            * jnp.mean(hidden * gain_two * normed_two_grad, axis=-1, keepdims=True)
        )
        branch_gradient = hidden_grad.astype(jnp.bfloat16)
        out_term = contract_row_pairs(lowrank_heads, branch_gradient)
        output_up_product = ADAPTER_SCALE * contract_row_pairs(
            adapter_output_delta, branch_gradient
        )
        adapter_output_grad = (
            ADAPTER_SCALE * contract_columns(branch_gradient, merged_output_up)
        ).astype(jnp.bfloat16)
        out_down_term = contract_row_pairs(lowrank_heads, adapter_output_grad)
        heads_grad = contract_columns(branch_gradient, merged_output_weight) + contract_columns(
            adapter_output_grad, full_out_down
        )
        (
            query_grad,
            key_grad_ext,
            value_grad_ext,
            prev_sum_grad,
            prev_norm_grad,
            featq_grad,
            featk_grad,
        ) = attention_pull(heads_grad)
        end_state = (
            jnp.zeros_like(prev_sum_grad),
            jnp.zeros_like(prev_norm_grad),
            jnp.full((1,), 1000000000.0, jnp.float32),
        )
        back_sum, back_norm, back_tag = prefix(
            (prev_sum_grad, prev_norm_grad, prev_tag), "shard", keep_earliest, end_state
        )
        matched = (back_tag[0] == tag_value[0]).astype(jnp.float32)
        key_more, value_more, featk_more = contribute_pull(
            (back_sum * matched, back_norm * matched)
        )
        tail_zeros = jnp.zeros((WINDOW, key_value_width), jnp.float32)
        key_grad_ext = key_grad_ext + jnp.concatenate([key_more, tail_zeros], axis=0)
        value_grad_ext = value_grad_ext + jnp.concatenate([value_more, tail_zeros], axis=0)
        sent_keys, sent_values = (
            from_behind(key_grad_ext[:WINDOW].astype(jnp.bfloat16), "shard", -1).astype(
                jnp.float32
            ),
            from_behind(value_grad_ext[:WINDOW].astype(jnp.bfloat16), "shard", -1).astype(
                jnp.float32
            ),
        )
        head_zeros = jnp.zeros((tok_rows - WINDOW, key_value_width), jnp.float32)
        key_grad = key_grad_ext[WINDOW:] + jnp.concatenate([head_zeros, sent_keys], axis=0)
        value_grad = value_grad_ext[WINDOW:] + jnp.concatenate([head_zeros, sent_values], axis=0)
        query_lin = rotate(query_grad, place_own, HEADS, -1.0)
        key_lin = rotate(key_grad, place_own, KV_HEADS, -1.0)
        proj_grad = jnp.concatenate([query_lin, key_lin, value_grad], axis=1).astype(jnp.bfloat16)
        qkv_term = contract_row_pairs(normalized_input, proj_grad)
        adapter_up_product = ADAPTER_SCALE * jnp.concatenate(
            [
                contract_row_pairs(adapter_delta[:, :ADAPTER_RANK], proj_grad[:, :MODEL_WIDTH]),
                contract_row_pairs(
                    adapter_delta[:, ADAPTER_RANK : 2 * ADAPTER_RANK],
                    proj_grad[:, MODEL_WIDTH : MODEL_WIDTH + key_value_width],
                ),
                contract_row_pairs(
                    adapter_delta[:, 2 * ADAPTER_RANK :],
                    proj_grad[:, MODEL_WIDTH + key_value_width :],
                ),
            ],
            axis=1,
        )
        adapter_delta_grad = (
            ADAPTER_SCALE
            * jnp.concatenate(
                [
                    contract_columns(proj_grad[:, :MODEL_WIDTH], merged_up_factor[:, :MODEL_WIDTH]),
                    contract_columns(
                        proj_grad[:, MODEL_WIDTH : MODEL_WIDTH + key_value_width],
                        merged_up_factor[:, MODEL_WIDTH : MODEL_WIDTH + key_value_width],
                    ),
                    contract_columns(
                        proj_grad[:, MODEL_WIDTH + key_value_width :],
                        merged_up_factor[:, MODEL_WIDTH + key_value_width :],
                    ),
                ],
                axis=1,
            )
        ).astype(jnp.bfloat16)
        adapter_down_product = contract_row_pairs(normalized_input, adapter_delta_grad)
        normed_grad = contract_columns(proj_grad, merged_joint_weight) + contract_columns(
            adapter_delta_grad, full_down
        )
        gain_one_term = jnp.sum(normed_grad * activ * inv_one, axis=0)
        input_grad = (
            hidden_grad
            + gain_one * inv_one * normed_grad
            - activ * inv_one**3 * jnp.mean(activ * gain_one * normed_grad, axis=-1, keepdims=True)
        )
        input_grads.append(input_grad.astype(jnp.bfloat16))
        micro_terms = (
            gain_one_term,
            qkv_term,
            adapter_down_product,
            adapter_up_product,
            out_term,
            out_down_term,
            output_up_product,
            featq_grad,
            featk_grad + featk_more,
            gain_two_term,
        )
        if micro_index == 0:
            attn_totals = micro_terms
        else:
            attn_totals = tuple(
                (
                    earlier_sum + newer_sum
                    for earlier_sum, newer_sum in zip(attn_totals, micro_terms)
                )
            )
    ffn_totals = ffn_sums_joined(
        jnp.concatenate(acted_list, axis=0),
        jnp.concatenate(ffn_grad_list, axis=0),
        jnp.concatenate(normed_two_list, axis=0),
        jnp.concatenate(gate_grad_list, axis=0),
    )
    scattered = (
        lax.psum_scatter(attn_totals[0], "shard", scatter_dimension=0, tiled=True),
        lax.psum_scatter(attn_totals[1], "shard", scatter_dimension=0, tiled=True),
        lax.psum_scatter(attn_totals[2], "shard", scatter_dimension=0, tiled=True),
        lax.psum_scatter(attn_totals[3], "shard", scatter_dimension=1, tiled=True),
        lax.psum_scatter(attn_totals[4], "shard", scatter_dimension=0, tiled=True),
        lax.psum_scatter(attn_totals[5], "shard", scatter_dimension=0, tiled=True),
        lax.psum_scatter(attn_totals[6], "shard", scatter_dimension=1, tiled=True),
        lax.psum_scatter(attn_totals[7], "shard", scatter_dimension=0, tiled=True),
        lax.psum_scatter(attn_totals[8], "shard", scatter_dimension=0, tiled=True),
        lax.psum_scatter(attn_totals[9], "shard", scatter_dimension=0, tiled=True),
    )
    totals = tuple(scattered) + tuple(ffn_totals)
    summed = jax.tree.map(
        lambda part: part.astype(jnp.float32), lax.psum(shortened(totals), "replica")
    )
    return (
        jnp.stack(outputs)[None],
        jnp.stack(input_grads)[None],
        summed[0],
        summed[1],
        summed[2],
        summed[3],
        summed[4],
        summed[5],
        summed[6],
        summed[7],
        summed[8],
        summed[9],
        summed[10],
        summed[11],
    )


def solution(mesh):
    placed = (
        P("replica", None, "shard", None),
        P("replica", None, "shard", None),
        P("replica", None, None),
        P("replica", None, "shard"),
        P("shard"),
        P("shard", None),
        P("shard", None),
        P(None, "shard"),
        P("shard", None),
        P("shard", None),
        P(None, "shard"),
        P("shard", None),
        P("shard", None),
        P("shard"),
        P("shard", None),
        P("shard", None),
    )
    return jax.shard_map(
        per_device,
        mesh=mesh,
        in_specs=placed,
        out_specs=(
            P("replica", None, "shard", None),
            P("replica", None, "shard", None),
            P("shard"),
            P("shard", None),
            P("shard", None),
            P(None, "shard"),
            P("shard", None),
            P("shard", None),
            P(None, "shard"),
            P("shard", None),
            P("shard", None),
            P("shard"),
            P("shard", None),
            P("shard", None),
        ),
        check_vma=False,
    )
```

profile of v0, /device:TPU:0, one launch (start us, length us, event | category | flops | bytes accessed | tf_op | source)
XLA Modules:
  0.0 3947.1 jit_solution(9617640561688964021)
XLA Ops:
  173.8 30.8 all-reduce.16
  267.4 21.5 all_gather.145
  405.3 109.4 %while.71 = (s32[]{:T(128)}, f32[8,128,64]{2,1,0:T(8,128)}, f32[8,128]{1,0:T(8,128)}, f32[1]{0:T(128)}, s32[]{:T(128)}, /*index=5*/bf16[16,1]{0,1:T(2,128)(2,1)}...) while((s32[]{:T(128)}, f32[8,128,64]{2,1,0:T(8,128)}, ...), condition=%wide.region_41.42_spmd.clone, body=%wide.region_40.41_spmd.clone.sunk | while | flops 399370 | bytes 1190100 | solution.py:49
  516.0 109.4 %while.70 = (s32[]{:T(128)}, f32[8,128,64]{2,1,0:T(8,128)}, f32[8,128]{1,0:T(8,128)}, f32[1]{0:T(128)}, s32[]{:T(128)}, /*index=5*/bf16[16,1]{0,1:T(2,128)(2,1)}...) while((s32[]{:T(128)}, f32[8,128,64]{2,1,0:T(8,128)}, ...), condition=%wide.region_19.20_spmd.clone, body=%wide.region_18.19_spmd.clone.sunk | while | flops 399370 | bytes 1190100 | solution.py:49
  648.7 27.3 fusion.354
  676.0 119.0 %all-gather.28.cloned.1.call-done = bf16[8192,2048]{1,0:T(8,128)(2,1)} async-done(((bf16[512,2048]{1,0:T(8,128)(2,1)}), bf16[8192,2048]{1,0:T(8,128)(2,1)}) %all-gather.28.cloned.1.call-update) | async-done | bytes 33554448 | tf_op jit(solution)/shard_map/all_gather | solution.py:222
  816.3 30.9 multiply_reduce_fusion.3
  847.3 27.2 fusion.358
  874.5 21.4 multiply_convert_fusion.1
  895.9 30.4 multiply_reduce_fusion.2
  997.0 33.9 all-reduce.15
  1119.3 49.1 %while.69 = (s32[]{:T(128)}, f32[8,128,64]{2,1,0:T(8,128)S(1)}, f32[8,128]{1,0:T(8,128)S(1)}, f32[1]{0:T(128)}, s32[]{:T(128)}, /*index=5*/bf16[16,1]{0,1:T(2,12...) while((s32[]{:T(128)}, f32[8,128,64]{2,1,0:T(8,128)S(1)}, ...), condition=%wide.region_70.71_spmd, body=%wide.region_69.70_spmd.sunk | while | flops 266251 | bytes 1190135 | solution.py:74
  1176.6 58.8 %while.68 = (s32[]{:T(128)}, f32[8,128,64]{2,1,0:T(8,128)S(1)}, f32[8,128]{1,0:T(8,128)S(1)}, f32[1]{0:T(128)}, s32[]{:T(128)}, /*index=5*/bf16[16,1]{0,1:T(2,12...) while((s32[]{:T(128)}, f32[8,128,64]{2,1,0:T(8,128)S(1)}, ...), condition=%wide.region_55.56_spmd, body=%wide.region_54.55_spmd.sunk | while | flops 266251 | bytes 1190135 | solution.py:74
  1274.3 38.1 fusion.32
  1313.6 48.4 %fusion.16 = f32[2048,16384]{1,0:T(8,128)} fusion(bf16[128,8192]{1,0:T(8,128)(2,1)} %get-tuple-element.845, bf16[128,8192]{1,0:T(8,128)(2,1)} %get-tuple-element.844, bf16[128,8192]{1,0:T(8,128)(2,1)} %get-tuple-element.843, bf16[128,8192]{1,0:T(8,128)(2,1)} %get-tuple-element.842, bf16[128,2048]{1,0:T(8,128)(2,1)S(1)} %copy-done.72, ...), kind=kOutput, calls=%fused_computation.34 | convolution fusion | flops 17215520768 | bytes 143654912 | tf_op jit(solution)/shard_map/dot_general | solution.py:86
  1392.0 124.8 %reduce-scatter.13.cloned.1.call-done = f32[128,3072]{1,0:T(8,128)} async-done(((f32[2048,3072]{1,0:T(8,128)}), f32[128,3072]{1,0:T(8,128)}) %reduce-scatter.13.cloned.1.call-update) | async-done | bytes 1572880 | tf_op jit(solution)/shard_map/reduce_scatter | solution.py:563
  1519.1 637.5 %reduce-scatter.29.cloned.1.call-done = f32[512,2048]{1,0:T(8,128)} async-done(((f32[8192,2048]{1,0:T(8,128)}), f32[512,2048]{1,0:T(8,128)}) %reduce-scatter.29.cloned.1.call-update) | async-done | bytes 4194320 | tf_op jit(solution)/shard_map/reduce_scatter | solution.py:227
  2160.5 1236.0 %reduce-scatter.27.cloned.1.call-done = f32[128,16384]{1,0:T(8,128)} async-done(((f32[2048,16384]{1,0:T(8,128)}), f32[128,16384]{1,0:T(8,128)}) %reduce-scatter.27.cloned.1.call-update) | async-done | bytes 8388624 | tf_op jit(solution)/shard_map/reduce_scatter | solution.py:230
  3452.1 53.3 %reduce-scatter.21.cloned.1.call-done = f32[8,128]{1,0:T(8,128)} async-done(((f32[8,2048]{1,0:T(8,128)}), f32[8,128]{1,0:T(8,128)}) %reduce-scatter.21.cloned.1.call-update) | async-done | bytes 4112 | tf_op jit(solution)/shard_map/reduce_scatter | solution.py:568
  3506.7 57.6 %reduce-scatter.23.cloned.1.call-done = f32[128,64]{0,1:T(8,128)} async-done(((f32[2048,64]{0,1:T(8,128)}), f32[128,64]{0,1:T(8,128)}) %reduce-scatter.23.cloned.1.call-update) | async-done | bytes 32784 | tf_op jit(solution)/shard_map/reduce_scatter | solution.py:569
  3585.9 57.6 %all-reduce.14 = (bf16[2048]{0:T(1024)(128)(2,1)S(1)}, bf16[2048]{0:T(1024)(128)(2,1)S(1)}) all-reduce(f32[2048]{0:T(1024)S(1)} %add.526, f32[2048]{0:T(1024)S(1)} %add.539), channel_id=12, replica_groups=mesh['replica'=2,'shard'=16] {'shard'}, use_global_device_ids=true, to_apply=%region_76.77.clone | all-reduce | flops 4096 | bytes 24576
  3647.7 37.8 reduce-scatter.31.cloned.1.call-done
  3686.5 55.1 %reduce-scatter.15.cloned.1.call-done = f32[128,24]{0,1:T(8,128)} async-done(((f32[2048,24]{0,1:T(8,128)}), f32[128,24]{0,1:T(8,128)}) %reduce-scatter.15.cloned.1.call-update) | async-done | bytes 12304 | tf_op jit(solution)/shard_map/reduce_scatter | solution.py:564
  3755.4 171.1 %all-reduce.21.cloned.1.call-done = (bf16[128,3072]{1,0:T(8,128)(2,1)}, bf16[128,2048]{1,0:T(8,128)(2,1)}, bf16[128,16384]{1,0:T(8,128)(2,1)}, bf16[512,2048]{1,0:T(8,128)(2,1)}) async-done(((bf16[128,3072]{1,0:T(8,128)(2,1)}, bf16[128,2048]{1,0:T(8,128)(2,1)}, bf16[128,16384]{1,0:T(8,128)(2,1)}, bf16[512,2048]{1,0:T(8,128)(2,1)}), (bf16[128,3072]{1,0:T(8,128)(2,1)}, bf16[128,2048]{1,0:T(8,128)(2,1)}, ...) | async-done | bytes 7602192 | tf_op jit(solution)/shard_map/psum | solution.py:575
  (1318 shorter events, 983.2 us)
Async XLA Ops:
  7.2 109.1 %all-gather.22.cloned.1.call-start = ((), (), s32[]{:S(2)}) async-start(), calls=%async_computation.10 | async-start | bytes 13369344 | tf_op jit(solution)/shard_map/all_gather | solution.py:207
  7.9 397.4 %all-gather.32.cloned.1.call-start = ((), (), s32[]{:S(2)}) async-start(), calls=%async_computation.24 | async-start | bytes 2228224 | tf_op jit(solution)/shard_map/all_gather | solution.py:32
  9.2 130.9 %collective-permute-start = (bf16[64]{0:T(256)(128)(2,1)}, bf16[64]{0:T(256)(128)(2,1)}, u32[]{:S(2)}, u32[]{:S(2)}) collective-permute-start(bf16[64]{0:T(256)(128)(2,1)} %get-tuple-element.916), channel_id=1, source_target_pairs={{0,1},{1,2},{2,3},{3,4},{4,5},{5,6},{6,7},{7,8},{8,9},{9,10},{10,1... | collective-permute-start | bytes 392 | tf_op jit(solution)/shard_map/ppermute | solution.py:26
  12.2 91.5 %collective-permute-start.3 = (bf16[64]{0:T(256)(128)(2,1)S(1)}, bf16[64]{0:T(256)(128)(2,1)S(1)}, u32[]{:S(2)}, u32[]{:S(2)}) collective-permute-start(bf16[64]{0:T(256)(128)(2,1)S(1)} %get-tuple-element.917), channel_id=1, source_target_pairs={{0,1},{1,2},{2,3},{3,4},{4,5},{5,6},{6,7},{7,8},{8,9},{9,10},{10,1... | collective-permute-start | bytes 392 | tf_op jit(solution)/shard_map/ppermute | solution.py:26
  136.8 379.1 %all-gather.30.cloned.1.call-start = ((), (), s32[]{:S(2)}) async-start(), calls=%async_computation.23 | async-start | bytes 2228224 | tf_op jit(solution)/shard_map/all_gather | solution.py:32
  152.5 8.4 collective-permute-start.1
  167.7 467.1 %all-gather.24.cloned.1.call-start = ((), (), s32[]{:S(2)}) async-start(), calls=%async_computation.11 | async-start | bytes 8912896 | tf_op jit(solution)/shard_map/all_gather | solution.py:210
  168.3 479.7 %all-gather.26.cloned.1.call-start = ((), (), s32[]{:S(2)}) async-start(), calls=%async_computation.12 | async-start | bytes 71303168 | tf_op jit(solution)/shard_map/all_gather | solution.py:221
  168.9 626.2 %all-gather.28.cloned.1.call-start = ((), (), s32[]{:S(2)}) async-start(), calls=%async_computation.13 | async-start | bytes 35651584 | tf_op jit(solution)/shard_map/all_gather | solution.py:222
  169.5 949.8 %all-gather.36.cloned.1.call-start = ((), (), s32[]{:S(2)}) async-start(), calls=%async_computation.26 | async-start | bytes 2228224 | tf_op jit(solution)/shard_map/all_gather | solution.py:57
  953.2 223.3 %all-gather.34.cloned.1.call-start = ((), (), s32[]{:S(2)}) async-start(), calls=%async_computation.25 | async-start | bytes 2228224 | tf_op jit(solution)/shard_map/all_gather | solution.py:57
  974.3 415.6 %reduce-scatter.17.cloned.1.call-start = ((), (), s32[]{:S(2)}) async-start(), calls=%async_computation.16 | async-start | bytes 17825792 | tf_op jit(solution)/shard_map/reduce_scatter | solution.py:566
  993.5 523.2 %reduce-scatter.13.cloned.1.call-start = ((), (), s32[]{:S(2)}) async-start(), calls=%async_computation.14 | async-start | bytes 26738688 | tf_op jit(solution)/shard_map/reduce_scatter | solution.py:563
  1171.4 73.0 %collective-permute-start.9 = (bf16[64,512]{0,1:T(8,128)(2,1)}, bf16[64,512]{0,1:T(8,128)(2,1)}, u32[]{:S(2)}, u32[]{:S(2)}) collective-permute-start(bf16[64,512]{0,1:T(8,128)(2,1)} %slice.586), channel_id=1, source_target_pairs={{1,0},{2,1},{3,2},{4,3},{5,4},{6,5},{7,6},{8,7},{9,8},{10,9},{11,1... | collective-permute-start | bytes 196616 | tf_op jit(solution)/shard_map/ppermute | solution.py:26
  1175.2 66.5 %collective-permute-start.8 = (bf16[64,512]{0,1:T(8,128)(2,1)}, bf16[64,512]{0,1:T(8,128)(2,1)}, u32[]{:S(2)}, u32[]{:S(2)}) collective-permute-start(bf16[64,512]{0,1:T(8,128)(2,1)} %slice.587), channel_id=1, source_target_pairs={{1,0},{2,1},{3,2},{4,3},{5,4},{6,5},{7,6},{8,7},{9,8},{10,9},{11,1... | collective-permute-start | bytes 196616 | tf_op jit(solution)/shard_map/ppermute | solution.py:26
  1272.2 884.5 %reduce-scatter.29.cloned.1.call-start = ((), (), s32[]{:S(2)}) async-start(), calls=%async_computation.22 | async-start | bytes 71303168 | tf_op jit(solution)/shard_map/reduce_scatter | solution.py:227
  1312.5 2084.0 %reduce-scatter.27.cloned.1.call-start = ((), (), s32[]{:S(2)}) async-start(), calls=%async_computation.21 | async-start | bytes 142606336 | tf_op jit(solution)/shard_map/reduce_scatter | solution.py:230
  1362.1 2088.8 %reduce-scatter.19.cloned.1.call-start = ((), (), s32[]{:S(2)}) async-start(), calls=%async_computation.17 | async-start | bytes 69632 | tf_op jit(solution)/shard_map/reduce_scatter | solution.py:567
  1374.0 2131.4 %reduce-scatter.21.cloned.1.call-start = ((), (), s32[]{:S(2)}) async-start(), calls=%async_computation.18 | async-start | bytes 69632 | tf_op jit(solution)/shard_map/reduce_scatter | solution.py:568
  1374.8 2189.4 %reduce-scatter.23.cloned.1.call-start = ((), (), s32[]{:S(2)}) async-start(), calls=%async_computation.19 | async-start | bytes 557056 | tf_op jit(solution)/shard_map/reduce_scatter | solution.py:569
  1378.1 2268.9 %reduce-scatter.25.cloned.1.call-start = ((), (), s32[]{:S(2)}) async-start(), calls=%async_computation.20 | async-start | bytes 278528 | tf_op jit(solution)/shard_map/reduce_scatter | solution.py:570
  1382.7 2302.9 %reduce-scatter.31.cloned.1.call-start = ((), (), s32[]{:S(2)}) async-start(), calls=%async_computation.27 | async-start | bytes 1671168
  1387.8 2353.8 %reduce-scatter.15.cloned.1.call-start = ((), (), s32[]{:S(2)}) async-start(), calls=%async_computation.15 | async-start | bytes 208896 | tf_op jit(solution)/shard_map/reduce_scatter | solution.py:564
  1389.2 2537.2 %all-reduce.21.cloned.1.call-start = ((), (), s32[]{:S(2)}) async-start(), calls=%async_computation.28 | async-start | bytes 15204352 | tf_op jit(solution)/shard_map/psum | solution.py:575
  (303 other events, 4805.1 us)
Sparse Core Ops, SparseCore 0:
  10.3 105.9 all-gather.21
  136.9 42.6 all-gather.31
  181.8 41.0 all-gather.29
  224.9 73.9 all-gather.23
  300.4 324.7 all-gather.25
  626.6 168.4 all-gather.27
  953.3 41.2 all-gather.35
  996.8 40.1 all-gather.33
  1041.1 182.2 reduce-scatter.16
  1272.3 244.3 reduce-scatter.12
  1521.0 635.6 reduce-scatter.28
  2160.8 1235.6 reduce-scatter.26
  3399.9 50.9 reduce-scatter.18
  3454.5 50.9 reduce-scatter.20
  3509.4 54.8 reduce-scatter.22
  3568.1 54.3 reduce-scatter.24
  3627.0 58.4 reduce-scatter.30
  3688.9 52.6 reduce-scatter.14
  3744.8 181.6 all-reduce.20
where the time goes:
time: 3960 us; the launch traced here: 3950 us
  waiting for transfers between devices  2530 us (64%)
  matrix products  512 us (13%)
  blocking collectives  366 us (9%)
  other arithmetic  238 us (6%)
  local copies, waits for them, and re-layouts  178 us (4%)
  loops' own time  83.2 us (2%)
    reduce_scatter x1, waiting for transfers between devices, ffn_sums_joined(): lax.psum_scatter(contract_row_pairs(normed_two, gate_up_grad), 'shard', s...  1240 us
    reduce_scatter x1, waiting for transfers between devices, ffn_sums_joined(): lax.psum_scatter(contract_row_pairs(acted, ffn_grad), 'shard', scatter_di...  638 us
    psum x1, waiting for transfers between devices, per_device(): lax.psum(shortened(totals), 'replica')  171 us
    dot_general x20, matrix products, contract_columns(): lax.dot_general(left, right, (((1,), (1,)), ((), ())), preferred_element_...  142 us
    dot_general x18, matrix products, contract_row_pairs(): lax.dot_general(left, right, (((0,), (0,)), ((), ())), preferred_element_...  133 us
    reduce_scatter x1, waiting for transfers between devices, per_device(): lax.psum_scatter(attn_totals[1], 'shard', scatter_dimension=0, tiled=True)  125 us
    unnamed x3, blocking collectives  122 us
    all_gather x1, waiting for transfers between devices, gather_feedforward(): lax.all_gather(shards[2], 'shard', axis=0, tiled=True)  119 us
  transfers between devices with their start and end apart: 29, of which 13 were waited for; matrix products, arithmetic and copies ran while one was open for 19% of the time, Pallas kernels for 0%

commit v1 on v0

v1 whole, which is shorter than its diff:
```python
import jax
import jax.numpy as jnp
from jax import lax
from jax.experimental import pallas as pl
from jax.experimental.pallas import tpu as pltpu
from jax.sharding import Mesh, PartitionSpec as P

D = 2048
HEADS = 32
KV = 8
HD = 64
FF = 8192
RANK = 8
WINDOW = 64
MAXLEN = 1024
KVW = KV * HD
COLS = D + 2 * KVW
GROUP = HEADS // KV
NORM_EPS = 1e-05
SCALE = 2.0
ROPE_BASE = 500000.0
SROWS = 80
PACK = 256
bf16 = jnp.bfloat16
f32 = jnp.float32


def mm(a, b):
    return jnp.dot(a, b, preferred_element_type=f32)


def mm_t(a, b):
    return lax.dot_general(a, b, (((1,), (1,)), ((), ())), preferred_element_type=f32)


def t_mm(a, b):
    return lax.dot_general(a, b, (((0,), (0,)), ((), ())), preferred_element_type=f32)


def swap(a, axis):
    return lax.ppermute(a, axis, [(0, 1), (1, 0)])


def line_gather(block):
    nz, z = lax.axis_size("z"), lax.axis_index("z")
    rights, lefts = [block], [block]
    for k in range(1, nz):
        rights.append(
            lax.ppermute(rights[-1], "z", [(i, i + 1) for i in range(k - 1, nz - 1)])
        )
        lefts.append(lax.ppermute(lefts[-1], "z", [(i, i - 1) for i in range(1, nz - k + 1)]))
    return [block] + [jnp.where(z >= k, rights[k], lefts[nz - k]) for k in range(1, nz)]


def line_scatter(blocks):
    nz = lax.axis_size("z")
    right = left = None
    for s in range(1, nz):
        up, down = blocks[s].astype(f32), blocks[nz - s].astype(f32)
        if right is not None:
            up, down = up + right.astype(f32), down + left.astype(f32)
        right = lax.ppermute(
            up.astype(bf16), "z", [(i, i + 1) for i in range(min(s, nz - 1))]
        )
        left = lax.ppermute(
            down.astype(bf16), "z", [(i, i - 1) for i in range(max(nz - s, 1), nz)]
        )
    return blocks[0].astype(f32) + right.astype(f32) + left.astype(f32)


def gather_rows(block):
    nz = lax.axis_size("z")
    z, x, c = lax.axis_index("z"), lax.axis_index("x"), lax.axis_index("c")
    rows, cols = block.shape
    half = jnp.zeros((nz, 2, rows, cols), block.dtype)
    for k, part in enumerate(line_gather(block)):
        at = lax.rem(z - k + nz, nz)
        half = lax.dynamic_update_slice(half, part[None, None], (at, x, 0, 0))
        half = lax.dynamic_update_slice(half, swap(part, "x")[None, None], (at, 1 - x, 0, 0))
    other = swap(half, "c")
    first = jnp.where(c == 0, half, other)
    second = jnp.where(c == 0, other, half)
    return jnp.stack([first, second], axis=2).reshape(nz * 4 * rows, cols)


def scatter_rows(total):
    nz = lax.axis_size("z")
    z, x, c = lax.axis_index("z"), lax.axis_index("x"), lax.axis_index("c")
    rows, cols = total.shape
    r = rows // (4 * nz)
    t = total.reshape(nz, 2, 2, r, cols)
    pick = lambda a, i, dim: lax.dynamic_index_in_dim(a, i, dim, False)
    mine, theirs = pick(t, c, 2), pick(t, 1 - c, 2)
    t = (mine.astype(f32) + swap(theirs, "c").astype(f32)).astype(bf16)
    mine, theirs = pick(t, x, 1), pick(t, 1 - x, 1)
    t = (mine.astype(f32) + swap(theirs, "x").astype(f32)).astype(bf16)
    return line_scatter([pick(t, lax.rem(z - k + nz, nz), 0) for k in range(nz)])


def both_replicas(part):
    low = part.astype(bf16)
    return low.astype(f32) + swap(low, "r").astype(f32)


def gather_tokens(block):
    out = []
    for part in line_gather(block):
        out += [part, swap(part, "c")]
    return jnp.concatenate(out, axis=0)


def scatter_tokens(total):
    nz = lax.axis_size("z")
    t = total.reshape(nz, 2, total.shape[0] // (2 * nz), total.shape[1])
    t = (t[:, 0].astype(f32) + swap(t[:, 1], "c").astype(f32)).astype(bf16)
    return line_scatter([t[k] for k in range(nz)])


def gather_gate_up(weight):
    nz = lax.axis_size("z")
    z, x, c = lax.axis_index("z"), lax.axis_index("x"), lax.axis_index("c")
    rows = weight.shape[0]
    loc = FF // (4 * nz)
    out = jnp.zeros((nz, 2, 2, rows, 4 * loc), weight.dtype)
    for k in range(nz):
        to = lax.rem(z + k, nz)
        part = jnp.concatenate(
            [
                lax.dynamic_slice(weight, (0, g * FF + to * 4 * loc), (rows, 4 * loc))
                for g in range(2)
            ],
            axis=1,
        )
        if k:
            part = lax.ppermute(part, "z", [(i, (i + k) % nz) for i in range(nz)])
        at = lax.rem(z - k + nz, nz)

        def columns(core):
            return jnp.concatenate(
                [
                    lax.dynamic_slice(part, (0, j * 2 * loc + core * loc), (rows, loc))
                    for j in range(4)
                ],
                axis=1,
            )

        mine = columns(c)
        theirs = swap(columns(1 - c), "c")
        pair = jnp.stack([jnp.where(c == 0, mine, theirs), jnp.where(c == 0, theirs, mine)])
        out = lax.dynamic_update_slice(out, pair[None, None], (at, x, 0, 0, 0))
        out = lax.dynamic_update_slice(
            out, swap(pair, "x")[None, None], (at, 1 - x, 0, 0, 0)
        )
    return out.reshape(nz * 4 * rows, 4 * loc)


def scatter_gate_up(total):
    nz = lax.axis_size("z")
    z, x, c = lax.axis_index("z"), lax.axis_index("x"), lax.axis_index("c")
    rows, loc = total.shape[0] // (4 * nz), total.shape[1] // 4
    pick = lambda a, i, dim: lax.dynamic_index_in_dim(a, i, dim, False)
    t = total.reshape(nz, 2, 2, rows, 4 * loc)
    t = (
        pick(t, x, 1).astype(f32) + swap(pick(t, 1 - x, 1), "x").astype(f32)
    ).astype(bf16)
    mine, theirs = pick(t, c, 1), swap(pick(t, 1 - c, 1), "c")
    first, second = jnp.where(c == 0, mine, theirs), jnp.where(c == 0, theirs, mine)
    pieces = []
    for j in range(4):
        pieces += [first[:, :, j * loc : (j + 1) * loc], second[:, :, j * loc : (j + 1) * loc]]
    t = jnp.concatenate(pieces, axis=2)
    out = jnp.zeros((rows, 2 * FF), bf16)
    for k in range(nz):
        part = pick(t, lax.rem(z + k, nz), 0)
        if k:
            part = lax.ppermute(part, "z", [(i, (i + k) % nz) for i in range(nz)])
        at = lax.rem(z - k + nz, nz)
        for g in range(2):
            out = lax.dynamic_update_slice(
                out, part[:, g * 4 * loc : (g + 1) * 4 * loc], (0, g * FF + at * 4 * loc)
            )
    return out


def turn(v, cosine, sine):
    lane = lax.broadcasted_iota(jnp.int32, v.shape, 1)
    low_half = (lane & 63) < 32
    other = jnp.where(low_half, pltpu.roll(v, 96, 1), pltpu.roll(v, 32, 1))
    return v * cosine + other * sine


def rope_kernel(v_ref, cos_ref, sin_ref, o_ref, *, turned):
    j = pl.program_id(0)

    @pl.when(j < turned)
    def _():
        for s in range(4):
            at = slice(s * 128, (s + 1) * 128)
            o_ref[:, at] = turn(v_ref[:, at], cos_ref[...], sin_ref[...]).astype(bf16)

    @pl.when(j >= turned)
    def _():
        o_ref[...] = v_ref[...].astype(bf16)


def rope(values, cosine, sine, turned):
    rows, cols = values.shape
    full = pl.BlockSpec((rows, 128), lambda j: (0, 0))
    return pl.pallas_call(
        lambda *refs: rope_kernel(*refs, turned=turned),
        out_shape=jax.ShapeDtypeStruct((rows, cols), bf16),
        grid=(cols // 512,),
        in_specs=[pl.BlockSpec((rows, 512), lambda j: (0, j)), full, full],
        out_specs=pl.BlockSpec((rows, 512), lambda j: (0, j)),
        cost_estimate=pl.CostEstimate(
            flops=6 * rows * cols, bytes_accessed=6 * rows * cols, transcendentals=0
        ),
        name="rope",
    )(values, cosine, sine)


def halves(shape):
    return lax.broadcasted_iota(jnp.int32, shape, 1) < 64


def feature(z2):
    first = halves(z2.shape)
    top = jnp.max(jnp.where(first, z2, -jnp.inf), axis=1, keepdims=True)
    low = jnp.max(jnp.where(first, -jnp.inf, z2), axis=1, keepdims=True)
    e = jnp.exp(z2 - jnp.where(first, top, low))
    s1 = jnp.sum(jnp.where(first, e, 0.0), axis=1, keepdims=True)
    s2 = jnp.sum(jnp.where(first, 0.0, e), axis=1, keepdims=True)
    return e * jnp.where(first, 1.0 / s1, 1.0 / s2)


def feature_grad(phi, dphi):
    first = halves(phi.shape)
    t = phi * dphi
    s1 = jnp.sum(jnp.where(first, t, 0.0), axis=1, keepdims=True)
    s2 = jnp.sum(jnp.where(first, 0.0, t), axis=1, keepdims=True)
    return t - phi * jnp.where(first, s1, s2)


def with_one(v):
    wide = jnp.concatenate([v, jnp.zeros_like(v)], axis=1)
    lane = lax.broadcasted_iota(jnp.int32, wide.shape, 1)
    return jnp.where(lane == 64, jnp.ones_like(wide), wide)


def tile(a):
    return jnp.concatenate([a] * GROUP, axis=0)


def attention_masks(row_ref, col_ref):
    rows, extent = row_ref.shape[0], col_ref.shape[1]
    offset = (
        lax.broadcasted_iota(jnp.int32, (rows, extent), 0)
        + WINDOW
        - lax.broadcasted_iota(jnp.int32, (rows, extent), 1)
    )
    same = row_ref[:, 0:1] == col_ref[0:1, :]
    live = col_ref[1:2, :] > 0
    window = (offset >= 0) & (offset < WINDOW) & same & (live | (offset == 0))
    far = (offset >= WINDOW) & same & live
    return tile(window.astype(f32)) > 0, tile(far.astype(f32)) > 0


def head_forward(q_ref, k, v, st, wq_ref, wk, hh, window, far, use):
    rows = q_ref.shape[0]
    qs = [q_ref[:, (hh * GROUP + i) * HD : (hh * GROUP + i + 1) * HD] for i in range(GROUP)]
    q4 = jnp.concatenate(qs, axis=0)
    s = mm_t(q4, k) * 0.125
    s = jnp.where(window, s, -1e30)
    top = jnp.max(s, axis=1, keepdims=True)
    p = jnp.exp(s - top)
    e = jnp.exp(-top)
    phi = feature(
        jnp.concatenate([mm(qs[i], wq_ref[hh * GROUP + i]) for i in range(GROUP)], axis=0)
    )
    phik = feature(mm(k, wk))
    phi_b, phik_b = phi.astype(bf16), phik.astype(bf16)
    a_b = (p + e * jnp.where(far, mm_t(phi_b, phik_b), 0.0)).astype(bf16)
    va = with_one(v)
    stp = jnp.concatenate([st, jnp.zeros((128 - SROWS, 128), bf16)], axis=0)
    eu = e * use
    nd = mm(a_b, va) + eu * mm_t(phi_b, stp)
    return qs, q4, p, e, eu, phi, phi_b, phik, phik_b, a_b, va, stp, nd


def attend_kernel(q_ref, k_ref, v_ref, st_ref, wq_ref, wk_ref, row_ref, col_ref, o_ref):
    rows = q_ref.shape[0]
    window, far = attention_masks(row_ref, col_ref)
    use, live = tile(row_ref[:, 1:2]), tile(row_ref[:, 2:3])
    for hh in range(2):
        at = slice(hh * HD, (hh + 1) * HD)
        nd = head_forward(
            q_ref, k_ref[:, at], v_ref[:, at], st_ref[hh], wq_ref, wk_ref[hh], hh, window, far, use
        )[-1]
        out = (nd[:, :HD] * (live / nd[:, HD : HD + 1])).astype(bf16)
        for i in range(GROUP):
            j = hh * GROUP + i
            o_ref[:, j * HD : (j + 1) * HD] = out[i * rows : (i + 1) * rows]


def attend_back_kernel(
    q_ref, k_ref, v_ref, st_ref, wq_ref, wk_ref, row_ref, col_ref, do_ref, cos_ref, sin_ref,
    dq_ref, dk_ref, dv_ref, dst_ref, dwq_ref, dwk_ref, scr_ref,
):
    rows = q_ref.shape[0]
    window, far = attention_masks(row_ref, col_ref)
    use, live = tile(row_ref[:, 1:2]), tile(row_ref[:, 2:3])
    for hh in range(2):
        at = slice(hh * HD, (hh + 1) * HD)
        k = k_ref[:, at]
        qs, q4, p, e, eu, phi, phi_b, phik, phik_b, a_b, va, stp, nd = head_forward(
            q_ref, k, v_ref[:, at], st_ref[hh], wq_ref, wk_ref[hh], hh, window, far, use
        )
        do4 = jnp.concatenate(
            [do_ref[:, (hh * GROUP + i) * HD : (hh * GROUP + i + 1) * HD] for i in range(GROUP)],
            axis=0,
        )
        inv = 1.0 / nd[:, HD : HD + 1]
        dnum = do4 * (live * inv)
        dden = -jnp.sum(dnum * nd[:, :HD], axis=1, keepdims=True) * inv
        dn = jnp.concatenate([dnum, jnp.zeros_like(dnum)], axis=1)
        lane = lax.broadcasted_iota(jnp.int32, dn.shape, 1)
        dn = jnp.where(lane == HD, dden, dn)
        dn_b = dn.astype(bf16)
        en_b = (eu * dn).astype(bf16)
        da = mm_t(dn_b, va)
        ds_b = (da * p * 0.125).astype(bf16)
        dl_b = jnp.where(far, e * da, 0.0).astype(bf16)
        dv_ref[:, at] = t_mm(a_b, dn_b)[:, :HD]
        dst_ref[hh] = t_mm(en_b, phi_b)[:SROWS].astype(bf16)
        dz = feature_grad(phi, mm(dl_b, phik_b) + mm(en_b, stp)).astype(bf16)
        dzk = feature_grad(phik, t_mm(dl_b, phi_b)).astype(bf16)
        dq4 = mm(ds_b, k)
        dk_ref[:, at] = t_mm(ds_b, q4) + mm_t(dzk, wk_ref[hh])
        dwk_ref[hh] = t_mm(k, dzk)
        for i in range(GROUP):
            j = hh * GROUP + i
            dzi = dz[i * rows : (i + 1) * rows]
            scr_ref[:, j * HD : (j + 1) * HD] = dq4[i * rows : (i + 1) * rows] + mm_t(
                dzi, wq_ref[j]
            )
            dwq_ref[j] = t_mm(qs[i], dzi)
    for s in range(4):
        at = slice(s * 128, (s + 1) * 128)
        dq_ref[:, at] = turn(scr_ref[:, at], cos_ref[...], -sin_ref[...]).astype(bf16)


def state_kernel(k_ref, v_ref, wk_ref, row_ref, add_ref):
    rows = row_ref.shape[0]
    chosen = row_ref[:, 3:4]
    for hh in range(2):
        at = slice(hh * HD, (hh + 1) * HD)
        phik = (feature(mm(k_ref[:rows, at], wk_ref[hh])) * chosen).astype(bf16)
        add_ref[hh] = t_mm(with_one(v_ref[:rows, at]), phik)[:SROWS].astype(bf16)


def state_back_kernel(
    k_ref, v_ref, wk_ref, row_ref, dadd_ref, dk_in, dv_in, dk_ref, dv_ref, dwk_ref
):
    rows = row_ref.shape[0]
    chosen = row_ref[:, 3:4]
    dk_ref[rows:] = dk_in[rows:]
    dv_ref[rows:] = dv_in[rows:]
    for hh in range(2):
        at = slice(hh * HD, (hh + 1) * HD)
        k = k_ref[:rows, at]
        phik = feature(mm(k, wk_ref[hh]))
        dadd = jnp.concatenate([dadd_ref[hh], jnp.zeros((128 - SROWS, 128), bf16)], axis=0)
        dphi = mm(with_one(v_ref[:rows, at]), dadd) * chosen
        dz = feature_grad(phik, dphi).astype(bf16)
        dk_ref[:rows, at] = dk_in[:rows, at] + mm_t(dz, wk_ref[hh])
        dv_ref[:rows, at] = dv_in[:rows, at] + mm_t((phik * chosen).astype(bf16), dadd)[:, :HD]
        dwk_ref[hh] = t_mm(k, dz)


def params():
    return pltpu.CompilerParams(vmem_limit_bytes=48 << 20)


def specs(rows, extent):
    return dict(
        q=pl.BlockSpec((rows, 512), lambda j: (0, j)),
        k=pl.BlockSpec((extent, 128), lambda j: (0, j)),
        v=pl.BlockSpec((extent, 128), lambda j: (0, 4 + j)),
        st=pl.BlockSpec((2, SROWS, 128), lambda j: (j, 0, 0)),
        wq=pl.BlockSpec((8, HD, 128), lambda j: (j, 0, 0)),
        wk=pl.BlockSpec((2, HD, 128), lambda j: (j, 0, 0)),
        row=pl.BlockSpec((rows, 128), lambda j: (0, 0)),
        col=pl.BlockSpec((8, extent), lambda j: (0, 0)),
    )


def attend(qkv, kv_ext, st, wq2, wk2, rowinfo, colinfo):
    rows, extent = qkv.shape[0], kv_ext.shape[0]
    s = specs(rows, extent)
    return pl.pallas_call(
        attend_kernel,
        out_shape=jax.ShapeDtypeStruct((rows, D), bf16),
        grid=(4,),
        in_specs=[s[n] for n in ("q", "k", "v", "st", "wq", "wk", "row", "col")],
        out_specs=s["q"],
        compiler_params=params(),
        cost_estimate=pl.CostEstimate(
            flops=HEADS * rows * extent * 1200, bytes_accessed=4 << 20, transcendentals=1 << 20
        ),
        name="attend",
    )(qkv, kv_ext, kv_ext, st, wq2, wk2, rowinfo, colinfo)


def attend_back(qkv, kv_ext, st, wq2, wk2, rowinfo, colinfo, d_attn, cosine, sine):
    rows, extent = qkv.shape[0], kv_ext.shape[0]
    s = specs(rows, extent)
    return pl.pallas_call(
        attend_back_kernel,
        out_shape=(
            jax.ShapeDtypeStruct((rows, D), bf16),
            jax.ShapeDtypeStruct((extent, KVW), f32),
            jax.ShapeDtypeStruct((extent, KVW), f32),
            jax.ShapeDtypeStruct((KV, SROWS, 128), bf16),
            jax.ShapeDtypeStruct((HEADS, HD, 128), f32),
            jax.ShapeDtypeStruct((KV, HD, 128), f32),
        ),
        grid=(4,),
        in_specs=[
            s[n] for n in ("q", "k", "v", "st", "wq", "wk", "row", "col", "q", "row", "row")
        ],
        out_specs=(s["q"], s["k"], s["k"], s["st"], s["wq"], s["wk"]),
        scratch_shapes=[pltpu.VMEM((rows, 512), f32)],
        compiler_params=params(),
        cost_estimate=pl.CostEstimate(
            flops=HEADS * rows * extent * 3200, bytes_accessed=8 << 20, transcendentals=1 << 20
        ),
        name="attend_back",
    )(qkv, kv_ext, kv_ext, st, wq2, wk2, rowinfo, colinfo, d_attn, cosine, sine)


def state_add(kv_ext, wk2, rowinfo):
    rows, extent = rowinfo.shape[0], kv_ext.shape[0]
    s = specs(rows, extent)
    return pl.pallas_call(
        state_kernel,
        out_shape=jax.ShapeDtypeStruct((KV, SROWS, 128), bf16),
        grid=(4,),
        in_specs=[s[n] for n in ("k", "v", "wk", "row")],
        out_specs=s["st"],
        cost_estimate=pl.CostEstimate(
            flops=KV * rows * 128 * 400, bytes_accessed=1 << 20, transcendentals=1 << 17
        ),
        name="state_add",
    )(kv_ext, kv_ext, wk2, rowinfo)


def state_back(kv_ext, wk2, rowinfo, dadd, dk, dv):
    rows, extent = rowinfo.shape[0], kv_ext.shape[0]
    s = specs(rows, extent)
    return pl.pallas_call(
        state_back_kernel,
        out_shape=(
            jax.ShapeDtypeStruct((extent, KVW), f32),
            jax.ShapeDtypeStruct((extent, KVW), f32),
            jax.ShapeDtypeStruct((KV, HD, 128), f32),
        ),
        grid=(4,),
        in_specs=[s[n] for n in ("k", "v", "wk", "row", "st", "k", "k")],
        out_specs=(s["k"], s["k"], s["wk"]),
        cost_estimate=pl.CostEstimate(
            flops=KV * rows * 128 * 800, bytes_accessed=3 << 20, transcendentals=1 << 17
        ),
        name="state_back",
    )(kv_ext, kv_ext, wk2, rowinfo, dadd, dk, dv)


def weigh(flag, a):
    return jnp.where(flag, a.astype(f32), 0.0)


def entering(add, tags, reach):
    nz = lax.axis_size("z")
    z, x, c = lax.axis_index("z"), lax.axis_index("x"), lax.axis_index("c")
    p = (z * 2 + x) * 2 + c
    tag = lambda i: lax.dynamic_index_in_dim(tags, jnp.clip(i, 0, 4 * nz - 1), 0, False)
    prev = tag(p - 1)
    chip = (z * 2 + x) * 2
    other = swap(add, "c")
    one = tag(chip) == tag(chip + 1)
    chip_sum = (weigh((c == 1) | one, add) + weigh((c == 0) | one, other)).astype(bf16)
    side = swap(chip_sum, "x")
    one = tag(z * 4 + 1) == tag(z * 4 + 3)
    layer = (weigh((x == 1) | one, chip_sum) + weigh((x == 0) | one, side)).astype(bf16)
    state = weigh(c == 1, other) + weigh((x == 1) & (tag(z * 4 + 1) == prev), side)
    for hop in range(1, min(reach, nz - 1) + 1):
        got = lax.ppermute(layer, "z", [(i, i + hop) for i in range(nz - hop)])
        state += weigh((z >= hop) & (tag((z - hop) * 4 + 3) == prev), got)
    return state.astype(bf16)


def leaving(dstate, tags, reach):
    nz = lax.axis_size("z")
    z, x, c = lax.axis_index("z"), lax.axis_index("x"), lax.axis_index("c")
    p = (z * 2 + x) * 2 + c
    tag = lambda i: lax.dynamic_index_in_dim(tags, jnp.clip(i, 0, 4 * nz - 1), 0, False)
    from_tag = lambda i: jnp.where(i > 0, tag(i - 1), -1)
    own = tag(p)
    chip = (z * 2 + x) * 2
    other = swap(dstate, "c")
    one = from_tag(chip) == from_tag(chip + 1)
    chip_sum = (weigh((c == 0) | one, dstate) + weigh((c == 1) | one, other)).astype(bf16)
    side = swap(chip_sum, "x")
    one = from_tag(z * 4) == from_tag(z * 4 + 2)
    layer = (weigh((x == 0) | one, chip_sum) + weigh((x == 1) | one, side)).astype(bf16)
    total = weigh(c == 0, other) + weigh((x == 0) & (from_tag(z * 4 + 2) == own), side)
    for hop in range(1, min(reach, nz - 1) + 1):
        got = lax.ppermute(layer, "z", [(i, i - hop) for i in range(hop, nz)])
        total += weigh((z + hop < nz) & (from_tag((z + hop) * 4) == own), got)
    return total.astype(bf16)


def per_device(
    inputs, cotangent, lengths, padding, gain_attn_own, wqkv_own, adown_own, aup_own, wout_own,
    odown_own, oup_own, featq_own, featk_own, gain_ffn_own, wgu_own, wd_own,
):
    nz = lax.axis_size("z")
    n = 4 * nz
    z, x, c = lax.axis_index("z"), lax.axis_index("x"), lax.axis_index("c")
    place_own = (z * 2 + x) * 2 + c
    micros, rows = inputs.shape[1], inputs.shape[2]
    reach = -(-MAXLEN // (4 * rows))
    chain = (("z", "x", "c"), [(i, i + 1) for i in range(n - 1)])
    unchain = (("z", "x", "c"), [(i, i - 1) for i in range(1, n)])
    r = D // n

    pack = jnp.concatenate(
        [
            gain_attn_own[:, None], adown_own, odown_own, oup_own.T, featq_own,
            gain_ffn_own[:, None], aup_own.reshape(r, 12), featk_own.reshape(r, 16),
        ],
        axis=1,
    )
    small = gather_rows(jnp.pad(pack, ((0, 0), (0, PACK - pack.shape[1]))))
    wqkv = gather_rows(wqkv_own)
    wout = gather_rows(wout_own)
    wgu = gather_gate_up(wgu_own)
    wd_other = swap(wd_own, "x")
    wd = jnp.concatenate(
        [jnp.where(x == 0, wd_own, wd_other), jnp.where(x == 0, wd_other, wd_own)], axis=0
    )
    gain_one = small[:, 0].astype(f32)[None]
    adown = small[:, 1:25]
    odown = small[:, 25:33]
    oup_t = small[:, 33:41]
    featq = small[:, 41:105].reshape(HEADS, HD, HD)
    gain_two = small[:, 105].astype(f32)[None]
    aup = small[:, 106:118].reshape(n, RANK, COLS // n).transpose(1, 0, 2).reshape(RANK, COLS)
    featk = small[:, 118:134].reshape(KV, HD, HD)
    wq2 = jnp.concatenate([featq, -featq], axis=2)
    wk2 = jnp.concatenate([featk, -featk], axis=2)
    column = jnp.arange(COLS)[None]
    owner = jnp.where(column < D, 0, jnp.where(column < D + KVW, 1, 2))
    aup_wide = jnp.concatenate(
        [jnp.where(owner == t, aup, jnp.zeros_like(aup)) for t in range(3)], axis=0
    )

    live_all = padding[0].astype(bf16)
    halo_live = lax.ppermute(live_all[:, rows - WINDOW :], *chain)

    saved = []
    for m in range(micros):
        act = inputs[0, m].astype(f32)
        doc_lengths = lengths[0, m]
        ends = jnp.cumsum(doc_lengths)
        seg_of = lambda t: jnp.sum((ends[None, :] <= t[:, None]).astype(jnp.int32), axis=1)
        places = place_own * rows - WINDOW + jnp.arange(rows + WINDOW, dtype=jnp.int32)
        done = ends[None, :] <= places[:, None]
        seg_ext = jnp.sum(done.astype(jnp.int32), axis=1)
        pos = (places - jnp.sum(jnp.where(done, doc_lengths[None, :], 0), axis=1))[WINDOW:]
        tags = seg_of(jnp.arange(n, dtype=jnp.int32) * rows + (rows - WINDOW - 1))
        live_ext = jnp.concatenate([halo_live[m], live_all[m]]).astype(f32)
        prev_tag = jnp.where(
            place_own > 0,
            lax.dynamic_index_in_dim(tags, jnp.maximum(place_own - 1, 0), 0, False),
            -1,
        )
        own_tag = lax.dynamic_index_in_dim(tags, place_own, 0, False)
        seg_own = seg_ext[WINDOW:]
        info = jnp.stack(
            [
                seg_own.astype(f32),
                (seg_own == prev_tag).astype(f32),
                live_ext[WINDOW:],
                ((seg_ext[:rows] == own_tag) & (live_ext[:rows] > 0)).astype(f32),
            ],
            axis=1,
        )
        rowinfo = jnp.pad(info, ((0, 0), (0, 124)))
        colinfo = jnp.pad(jnp.stack([seg_ext.astype(f32), live_ext]), ((0, 6), (0, 0)))
        lane = jnp.arange(128)
        frequency = ROPE_BASE ** (-((lane % 32).astype(f32) * 2.0) / HD)
        angles = pos.astype(f32)[:, None] * frequency[None, :]
        cosine = jnp.cos(angles)
        sine = jnp.where((lane % 64 < 32)[None], -1.0, 1.0) * jnp.sin(angles)

        inv_one = lax.rsqrt(jnp.mean(act * act, axis=-1, keepdims=True) + NORM_EPS)
        n1 = (act * inv_one * gain_one).astype(bf16)
        adapt = mm(n1, adown).astype(bf16)
        projected = mm(n1, wqkv) + SCALE * mm(adapt, aup_wide)
        qkv = rope(projected, cosine, sine, 5)
        halo = lax.ppermute(qkv[rows - WINDOW :, D:], *chain)
        kv_ext = jnp.concatenate([halo, qkv[:, D:]], axis=0)
        state = entering(state_add(kv_ext, wk2, rowinfo), tags, reach)
        attn = attend(qkv, kv_ext, state, wq2, wk2, rowinfo, colinfo)
        adapt_out = mm(attn, odown).astype(bf16)
        hidden = act + (mm(attn, wout) + SCALE * mm_t(adapt_out, oup_t))
        inv_two = lax.rsqrt(jnp.mean(hidden * hidden, axis=-1, keepdims=True) + NORM_EPS)
        n2 = (hidden * inv_two * gain_two).astype(bf16)
        saved.append(
            dict(
                act=act, tags=tags, rowinfo=rowinfo, colinfo=colinfo, cosine=cosine, sine=sine,
                inv_one=inv_one, n1=n1, adapt=adapt, qkv=qkv, kv_ext=kv_ext, state=state,
                attn=attn, adapt_out=adapt_out, hidden=hidden, inv_two=inv_two, n2=n2,
            )
        )

    half = 2 * FF // (4 * nz)
    ffn = []
    for m in range(micros):
        n2_all = gather_tokens(saved[m]["n2"])
        df_all = gather_tokens(cotangent[0, m])
        gate_up = mm(n2_all, wgu)
        gate, up = gate_up[:, :half], gate_up[:, half:]
        sig = jax.nn.sigmoid(gate)
        swish = gate * sig
        acted = (swish * up).astype(bf16)
        d_act = mm_t(df_all, wd)
        d_gu = jnp.concatenate(
            [d_act * up * (sig * (1.0 + gate * (1.0 - sig))), d_act * swish], axis=1
        ).astype(bf16)
        ffn.append(
            dict(
                n2=n2_all, df=df_all, acted=acted, d_gu=d_gu,
                d_n2=scatter_tokens(mm_t(d_gu, wgu).astype(bf16)),
                out=scatter_tokens(mm(acted, wd).astype(bf16)),
            )
        )
    cat = lambda items, key: jnp.concatenate([i[key] for i in items], axis=0)
    outputs = [(saved[m]["hidden"] + ffn[m]["out"]).astype(bf16) for m in range(micros)]
    g_wd = t_mm(cat(ffn, "acted"), cat(ffn, "df")).astype(bf16)
    loc = g_wd.shape[0] // 2
    g_wd_own = (
        lax.dynamic_slice(g_wd, (x * loc, 0), (loc, D)).astype(f32)
        + swap(lax.dynamic_slice(g_wd, ((1 - x) * loc, 0), (loc, D)), "x").astype(f32)
    )
    g_wd_own = both_replicas(g_wd_own)
    g_wgu = t_mm(cat(ffn, "n2"), cat(ffn, "d_gu")).astype(bf16)
    g_wgu_own = both_replicas(scatter_gate_up(g_wgu))

    back = []
    for m in range(micros):
        s, d_n2 = saved[m], ffn[m]["d_n2"]
        dout = cotangent[0, m].astype(f32)
        hidden, inv_two = s["hidden"], s["inv_two"]
        d_hidden = (
            dout
            + gain_two * inv_two * d_n2
            - hidden * inv_two**3 * jnp.mean(hidden * gain_two * d_n2, axis=-1, keepdims=True)
        )
        d_branch = d_hidden.astype(bf16)
        d_adapt_out = (SCALE * mm(d_branch, oup_t)).astype(bf16)
        d_attn = mm_t(d_branch, wout) + mm_t(d_adapt_out, odown)
        dq, dk, dv, dst, dwq, dwk = attend_back(
            s["qkv"], s["kv_ext"], s["state"], wq2, wk2, s["rowinfo"], s["colinfo"], d_attn,
            s["cosine"], s["sine"],
        )
        dadd = leaving(dst, s["tags"], reach)
        dk, dv, dwk_more = state_back(s["kv_ext"], wk2, s["rowinfo"], dadd, dk, dv)
        d_kv = jnp.concatenate([dk, dv], axis=1)
        sent = lax.ppermute(d_kv[:WINDOW].astype(bf16), *unchain).astype(f32)
        d_kv = jnp.concatenate([d_kv[WINDOW:rows], d_kv[rows:] + sent], axis=0)
        d_kv = rope(d_kv, s["cosine"], -s["sine"], 1)
        back.append(
            dict(
                d_hidden=d_hidden, d_branch=d_branch, d_adapt_out=d_adapt_out,
                d_proj=jnp.concatenate([dq, d_kv], axis=1), dwq=dwq, dwk=dwk + dwk_more,
                gain_two=jnp.sum(d_n2 * hidden * inv_two, axis=0),
            )
        )

    attn_all, d_branch = cat(saved, "attn"), cat(back, "d_branch")
    g_wout_own = both_replicas(scatter_rows(t_mm(attn_all, d_branch).astype(bf16)))
    n1_all, d_proj, adapt_all = cat(saved, "n1"), cat(back, "d_proj"), cat(saved, "adapt")
    g_wqkv_own = both_replicas(scatter_rows(t_mm(n1_all, d_proj).astype(bf16)))
    d_adapt = (SCALE * mm_t(d_proj, aup_wide)).astype(bf16)
    d_n1 = mm_t(d_proj, wqkv) + mm_t(d_adapt, adown)
    acts, inv_one = cat(saved, "act"), cat(saved, "inv_one")
    g_gain_one = jnp.sum(d_n1 * acts * inv_one, axis=0)
    grad_inputs = (
        cat(back, "d_hidden")
        + gain_one * inv_one * d_n1
        - acts * inv_one**3 * jnp.mean(acts * gain_one * d_n1, axis=-1, keepdims=True)
    ).astype(bf16)
    g_adown = t_mm(n1_all, d_adapt)
    wide = SCALE * t_mm(adapt_all, d_proj)
    g_aup = jnp.where(owner == 0, wide[:8], jnp.where(owner == 1, wide[8:16], wide[16:24]))
    g_odown = t_mm(attn_all, cat(back, "d_adapt_out"))
    g_oup_t = SCALE * t_mm(d_branch, cat(saved, "adapt_out"))
    fold = lambda a: a[:, :, :HD] - a[:, :, HD:]
    g_featq = fold(sum(b["dwq"] for b in back)).reshape(D, HD)
    g_featk = fold(sum(b["dwk"] for b in back))
    g_gain_two = sum(b["gain_two"] for b in back)
    g_pack = jnp.concatenate(
        [
            g_gain_one[:, None], g_adown, g_odown, g_oup_t, g_featq, g_gain_two[:, None],
            g_aup.reshape(RANK, n, COLS // n).transpose(1, 0, 2).reshape(D, 12),
            g_featk.reshape(D, 16),
        ],
        axis=1,
    )
    g_pack = jnp.pad(g_pack, ((0, 0), (0, PACK - g_pack.shape[1]))).astype(bf16)
    g_small = both_replicas(scatter_rows(g_pack))
    return (
        jnp.stack(outputs)[None],
        grad_inputs.reshape(1, micros, rows, D),
        g_small[:, 0],
        g_wqkv_own,
        g_small[:, 1:25],
        g_small[:, 106:118].reshape(RANK, COLS // n),
        g_wout_own,
        g_small[:, 25:33],
        g_small[:, 33:41].T,
        g_small[:, 41:105],
        g_small[:, 118:134].reshape(KVW // n, HD),
        g_small[:, 105],
        g_wgu_own,
        g_wd_own,
    )


def solution(mesh):
    n = mesh.shape["shard"]
    fine = Mesh(mesh.devices.reshape(mesh.shape["replica"], n // 4, 2, 2), ("r", "z", "x", "c"))
    shard = ("z", "x", "c")
    tokens, row, col = P("r", None, shard, None), P(shard, None), P(None, shard)
    return jax.shard_map(
        per_device,
        mesh=fine,
        in_specs=(
            tokens, tokens, P("r", None, None), P("r", None, shard), P(shard), row, row, col, row,
            row, col, row, row, P(shard), row, row,
        ),
        out_specs=(
            tokens, tokens, P(shard), row, row, col, row, row, col, row, row, P(shard), row, row,
        ),
        check_vma=False,
    )
```

time: 3960 us -> 1560 us (0.39)
  waiting for transfers between devices: 2530 us -> 569 us
  blocking collectives: 366 us -> 0 us
  matrix products: 512 us -> 191 us
  starting transfers between devices: 24.2 us -> 319 us
  Pallas kernels: 0 us -> 112 us
  loops' own time: 83.2 us -> 0 us
  other arithmetic: 238 us -> 155 us
    reduce_scatter x9 -> x0, waiting for transfers between devices: 2180 us -> none  [the longest x1 1240 us: ffn_sums_joined(): lax.psum_scatter(contract_row_pairs(normed_two, gate_up_grad), 'shard', s...]
    ppermute x10 -> x169, waiting for transfers between devices: 2.49 us -> 569 us  [the longest x66 239 us: swap(): return lax.ppermute(a, axis, [(0, 1), (1, 0)])]
    dot_general x104 -> x37, matrix products: 493 us -> 191 us  [the longest x13 75.3 us: mm_t(): lax.dot_general(a, b, (((1,), (1,)), ((), ())), preferred_element_type=f32)]
    ppermute x10 -> x169, starting transfers between devices: 23.2 us -> 319 us  [the longest x21 107 us: line_scatter(): lax.ppermute(up.astype(bf16), 'z', [(i, i + 1) for i in range(min(s, nz -...]
    all_gather x12 -> x0, blocking collectives: 235 us -> none  [the longest x2 39.2 us: entering(): lax.all_gather(part.astype(kind), axis)]
    psum x1 -> x0, waiting for transfers between devices: 171 us -> none  [per_device(): lax.psum(shortened(totals), 'replica')]
    all_gather x8 -> x0, waiting for transfers between devices: 130 us -> none  [the longest x1 119 us: gather_feedforward(): lax.all_gather(shards[2], 'shard', axis=0, tiled=True)]
    unnamed x3 -> x0, blocking collectives: 122 us -> none
  transfers between devices with their start and end apart: 29 -> 169, of which waited for: 13 -> 58; matrix products, arithmetic and copies ran while one was open for 19% -> 29% of each run, Pallas kernels for 0% -> 7%
where the time goes in v1:
time: 1560 us; the launch traced here: 1550 us
  waiting for transfers between devices  569 us (36%)
  starting transfers between devices  319 us (20%)
  matrix products  191 us (12%)
  local copies, waits for them, and re-layouts  170 us (11%)
  other arithmetic  155 us (10%)
  Pallas kernels  112 us (7%)
  between operations  30.7 us (2%)
    ppermute x66, waiting for transfers between devices, swap(): return lax.ppermute(a, axis, [(0, 1), (1, 0)])  239 us
    ppermute x21, waiting for transfers between devices, line_gather(): lax.ppermute(lefts[-1], 'z', [(i, i - 1) for i in range(1, nz - k + 1)])  146 us
    ppermute x21, starting transfers between devices, line_scatter(): lax.ppermute(up.astype(bf16), 'z', [(i, i + 1) for i in range(min(s, nz -...  107 us
    dot_general x13, matrix products, mm_t(): lax.dot_general(a, b, (((1,), (1,)), ((), ())), preferred_element_type=f32)  75.3 us
    ppermute x21, waiting for transfers between devices, line_scatter(): lax.ppermute(up.astype(bf16), 'z', [(i, i + 1) for i in range(min(s, nz -...  71.1 us
    ppermute x66, starting transfers between devices, swap(): return lax.ppermute(a, axis, [(0, 1), (1, 0)])  68.1 us
    dot_general x8, matrix products, t_mm(): lax.dot_general(a, b, (((0,), (0,)), ((), ())), preferred_element_type=f32)  57.9 us
    dot_general x16, matrix products, mm(): return jnp.dot(a, b, preferred_element_type=f32)  57.6 us
  transfers between devices with their start and end apart: 169, of which 58 were waited for; matrix products, arithmetic and copies ran while one was open for 29% of the time, Pallas kernels for 7%

profile of v1, /device:TPU:0, one launch (start us, length us, event | category | flops | bytes accessed | tf_op | source)
XLA Modules:
  0.0 1546.3 jit_solution(4836658126910210818)
XLA Ops:
  130.1 12.6 collective-permute-done.28
  177.8 35.9 %collective-permute-done.57 = bf16[128,4096]{1,0:T(8,128)(2,1)} collective-permute-done((bf16[128,4096]{1,0:T(8,128)(2,1)}, bf16[128,4096]{1,0:T(8,128)(2,1)}, u32[]{:S(2)}, u32[]{:S(2)}) %collective-permute-start.57) | collective-permute-done | bytes 1048608 | tf_op jit(solution)/shard_map/ppermute | solution.py:135
  279.9 23.4 %collective-permute-done.32 = bf16[128,2048]{1,0:T(8,128)(2,1)S(1)} collective-permute-done((bf16[128,2048]{1,0:T(8,128)(2,1)S(1)}, bf16[128,2048]{1,0:T(8,128)(2,1)S(1)}, u32[]{:S(2)}, u32[]{:S(2)}) %collective-permute-start.32) | collective-permute-done | bytes 524320 | tf_op jit(solution)/shard_map/ppermute | solution.py:51
  361.0 14.3 collective-permute-done.18
  379.4 21.9 %collective-permute-done.53 = bf16[2,128,2048]{2,1,0:T(8,128)(2,1)S(1)} collective-permute-done((bf16[2,128,2048]{2,1,0:T(8,128)(2,1)S(1)}, bf16[2,128,2048]{2,1,0:T(8,128)(2,1)S(1)}, u32[]{:S(2)}, u32[]{:S(2)}) %collective-permute-start.53) | collective-permute-done | bytes 1048608 | tf_op jit(solution)/shard_map/ppermute | solution.py:41
  401.8 21.9 %collective-permute-done.56 = bf16[2,128,2048]{2,1,0:T(8,128)(2,1)S(1)} collective-permute-done((bf16[2,128,2048]{2,1,0:T(8,128)(2,1)S(1)}, bf16[2,128,2048]{2,1,0:T(8,128)(2,1)S(1)}, u32[]{:S(2)}, u32[]{:S(2)}) %collective-permute-start.56) | collective-permute-done | bytes 1048608 | tf_op jit(solution)/shard_map/ppermute | solution.py:41
  424.2 16.4 %collective-permute-done.20 = bf16[128,3072]{1,0:T(8,128)(2,1)S(1)} collective-permute-done((bf16[128,3072]{1,0:T(8,128)(2,1)S(1)}, bf16[128,3072]{1,0:T(8,128)(2,1)S(1)}, u32[]{:S(2)}, u32[]{:S(2)}) %collective-permute-start.20) | collective-permute-done | bytes 786464 | tf_op jit(solution)/shard_map/ppermute | solution.py:41
  441.9 31.1 %collective-permute-done.35 = bf16[128,2048]{1,0:T(8,128)(2,1)S(1)} collective-permute-done((bf16[128,2048]{1,0:T(8,128)(2,1)S(1)}, bf16[128,2048]{1,0:T(8,128)(2,1)S(1)}, u32[]{:S(2)}, u32[]{:S(2)}) %collective-permute-start.35) | collective-permute-done | bytes 524320 | tf_op jit(solution)/shard_map/ppermute | solution.py:41
  487.0 22.5 %collective-permute-done.111 = bf16[128,2048]{1,0:T(8,128)(2,1)S(1)} collective-permute-done((bf16[128,2048]{1,0:T(8,128)(2,1)S(1)}, bf16[128,2048]{1,0:T(8,128)(2,1)S(1)}, u32[]{:S(2)}, u32[]{:S(2)}) %collective-permute-start.111) | collective-permute-done | bytes 524320 | tf_op jit(solution)/shard_map/ppermute | solution.py:51
  591.5 14.0 attend.2
  663.8 14.0 attend.3
  743.7 14.2 collective-permute-done.76
  839.8 12.4 multiply_convert_fusion.1
  926.0 26.1 %fusion.11 = bf16[2048,2048]{1,0:T(8,128)(2,1)} fusion(bf16[2048,2048]{1,0:T(8,128)(2,1)} %get-tuple-element.297, bf16[1024,1024]{1,0:T(8,128)(2,1)} %get-tuple-element.187, bf16[1024,1024]{1,0:T(8,128)(2,1)} %get-tuple-element.186, bf16[1024,1024]{1,0:T(8,128)(2,1)} %get-tuple-element.185, bf16[1024,1024]{1,0:T(8,128)(2,1)} %get-tuple-element.184), kind=kOutput, calls=%fused_computation.18 | convolution fusion | flops 17217617920 | bytes 25165824 | tf_op jit(solution)/shard_map/dot_general | solution.py:37
  1027.0 25.4 %attend_back.2 = (bf16[128,2048]{1,0:T(8,128)(2,1)S(1)}, f32[192,512]{1,0:T(8,128)S(1)}, f32[192,512]{1,0:T(8,128)S(1)}, bf16[8,80,128]{2,1,0:T(8,128)(2,1)S(1)}...) custom-call(bf16[128,3072]{1,0:T(8,128)(2,1)S(1)} %copy-done.10, bf16[192,1024]{1,0:T(8,128)(2,1)S(1)} %copy-done, ...), custom_call_target="tpu_custom_call" | custom-call | flops 2516582400 | bytes 8388608 | tf_op jit(solution)/shard_map/attend_back/pallas_call | solution.py:417
  1060.7 25.2 %attend_back.3 = (bf16[128,2048]{1,0:T(8,128)(2,1)S(1)}, f32[192,512]{1,0:T(8,128)S(1)}, f32[192,512]{1,0:T(8,128)S(1)}, bf16[8,80,128]{2,1,0:T(8,128)(2,1)S(1)}...) custom-call(bf16[128,3072]{1,0:T(8,128)(2,1)S(1)} %copy-done.12, bf16[192,1024]{1,0:T(8,128)(2,1)S(1)} %copy-done.2, ...), custom_call_target="tpu_custom_call" | custom-call | flops 2516582400 | bytes 8388608 | tf_op jit(solution)/shard_map/attend_back/pallas_call | solution.py:417
  1283.9 32.4 %collective-permute-done.164 = bf16[128,4096]{1,0:T(8,128)(2,1)} collective-permute-done((bf16[128,4096]{1,0:T(8,128)(2,1)}, bf16[128,4096]{1,0:T(8,128)(2,1)}, u32[]{:S(2)}, u32[]{:S(2)}) %collective-permute-start.164) | collective-permute-done | bytes 1048608 | tf_op jit(solution)/shard_map/ppermute | solution.py:176
  1320.7 23.4 %collective-permute-start.154 = (bf16[128,2048]{1,0:T(8,128)(2,1)S(1)}, bf16[128,2048]{1,0:T(8,128)(2,1)S(1)}, u32[]{:S(2)}, u32[]{:S(2)}) collective-permute-start(bf16[128,2048]{1,0:T(8,128)(2,1)S(1)} %dynamic-slice_bitcast_fusion.10), channel_id=1, source_target_pairs={{0,4},{1,5},{2,6},{3,7},{16,20},{17,21},{18,22},{19,23}} | collective-permute-start | bytes 1572872 | tf_op jit(solution)/shard_map/ppermute | solution.py:62
  1344.1 27.9 %collective-permute-done.144 = bf16[4,128,3072]{2,1,0:T(8,128)(2,1)S(1)} collective-permute-done((bf16[4,128,3072]{2,1,0:T(8,128)(2,1)S(1)}, bf16[4,128,3072]{2,1,0:T(8,128)(2,1)S(1)}, u32[]{:S(2)}, u32[]{:S(2)}) %collective-permute-start.144) | collective-permute-done | bytes 3145760 | tf_op jit(solution)/shard_map/ppermute | solution.py:41
  1379.8 14.5 collective-permute-done.145
  1435.5 12.5 collective-permute-start.147
  1459.3 17.0 %collective-permute-start.160 = (bf16[128,2048]{1,0:T(8,128)(2,1)S(1)}, bf16[128,2048]{1,0:T(8,128)(2,1)S(1)}, u32[]{:S(2)}, u32[]{:S(2)}) collective-permute-start(bf16[128,2048]{1,0:T(8,128)(2,1)S(1)} %fusion.71), channel_id=1, source_target_pairs={{0,16},{16,0},{1,17},{17,1},{2,18},{18,2},{3,19},{19,3},{4,20},{20... | collective-permute-start | bytes 1572872 | tf_op jit(solution)/shard_map/ppermute | solution.py:41
  1482.2 35.1 %collective-permute-done.166 = bf16[128,16384]{1,0:T(8,128)(2,1)} collective-permute-done((bf16[128,16384]{1,0:T(8,128)(2,1)}, bf16[128,16384]{1,0:T(8,128)(2,1)}, u32[]{:S(2)}, u32[]{:S(2)}) %collective-permute-start.166) | collective-permute-done | bytes 4194336 | tf_op jit(solution)/shard_map/ppermute | solution.py:41
  1529.5 15.3 collective-permute-done.151
  (1045 shorter events, 1005.9 us)
Async XLA Ops:
  3.1 163.3 %collective-permute-start.92 = (bf16[128,2048]{1,0:T(8,128)(2,1)}, bf16[128,2048]{1,0:T(8,128)(2,1)}, u32[]{:S(2)}, u32[]{:S(2)}) collective-permute-start(bf16[128,2048]{1,0:T(8,128)(2,1)} %get-tuple-element.247), channel_id=1, source_target_pairs={{4,0},{8,4},{12,8},{5,1},{9,5},{13,9},{6,2},{10,6},{14,10},{7,3},{... | collective-permute-start | bytes 1572872 | tf_op jit(solution)/shard_map/ppermute | solution.py:51
  4.3 115.2 %collective-permute-start.90 = (bf16[128,2048]{1,0:T(8,128)(2,1)}, bf16[128,2048]{1,0:T(8,128)(2,1)S(1)}, u32[]{:S(2)}, u32[]{:S(2)}) collective-permute-start(bf16[128,2048]{1,0:T(8,128)(2,1)} %get-tuple-element.247), channel_id=1, source_target_pairs={{0,1},{1,0},{2,3},{3,2},{4,5},{5,4},{6,7},{7,6},{8,9},{9,8},{10,11... | collective-permute-start | bytes 1572872 | tf_op jit(solution)/shard_map/ppermute | solution.py:41
  4.9 234.2 %collective-permute-start.91 = (bf16[128,2048]{1,0:T(8,128)(2,1)}, bf16[128,2048]{1,0:T(8,128)(2,1)}, u32[]{:S(2)}, u32[]{:S(2)}) collective-permute-start(bf16[128,2048]{1,0:T(8,128)(2,1)} %get-tuple-element.247), channel_id=1, source_target_pairs={{0,4},{4,8},{8,12},{1,5},{5,9},{9,13},{2,6},{6,10},{10,14},{3,7},{... | collective-permute-start | bytes 1572872 | tf_op jit(solution)/shard_map/ppermute | solution.py:49
  18.0 70.8 %collective-permute-start = (bf16[128,256]{1,0:T(8,128)(2,1)}, bf16[128,256]{1,0:T(8,128)(2,1)}, u32[]{:S(2)}, u32[]{:S(2)}) collective-permute-start(bf16[128,256]{1,0:T(8,128)(2,1)} %pad.23), channel_id=1, source_target_pairs={{0,2},{2,0},{1,3},{3,1},{4,6},{6,4},{5,7},{7,5},{8,10},{10,8},{9,1... | collective-permute-start | bytes 196616 | tf_op jit(solution)/shard_map/ppermute | solution.py:41
  142.6 71.1 %collective-permute-start.57 = (bf16[128,4096]{1,0:T(8,128)(2,1)}, bf16[128,4096]{1,0:T(8,128)(2,1)}, u32[]{:S(2)}, u32[]{:S(2)}) collective-permute-start(bf16[128,4096]{1,0:T(8,128)(2,1)} %pad_maximum_fusion.10), channel_id=1, source_target_pairs={{0,12},{4,0},{8,4},{12,8},{1,13},{5,1},{9,5},{13,9},{2,14},{6,2},{... | collective-permute-start | bytes 3145736 | tf_op jit(solution)/shard_map/ppermute | solution.py:135
  154.9 60.8 %collective-permute-start.51 = (bf16[128,4096]{1,0:T(8,128)(2,1)}, bf16[128,4096]{1,0:T(8,128)(2,1)}, u32[]{:S(2)}, u32[]{:S(2)}) collective-permute-start(bf16[128,4096]{1,0:T(8,128)(2,1)} %pad_maximum_fusion.6), channel_id=1, source_target_pairs={{0,4},{4,8},{8,12},{12,0},{1,5},{5,9},{9,13},{13,1},{2,6},{6,10},{... | collective-permute-start | bytes 3145736 | tf_op jit(solution)/shard_map/ppermute | solution.py:135
  166.3 58.5 %collective-permute-start.30 = (bf16[128,2048]{1,0:T(8,128)(2,1)S(1)}, bf16[128,2048]{1,0:T(8,128)(2,1)S(1)}, u32[]{:S(2)}, u32[]{:S(2)}) collective-permute-start(bf16[128,2048]{1,0:T(8,128)(2,1)S(1)} %copy-done.103), channel_id=1, source_target_pairs={{4,0},{8,4},{12,8},{5,1},{9,5},{13,9},{6,2},{10,6},{14,10},{7,3},{... | collective-permute-start | bytes 1572872 | tf_op jit(solution)/shard_map/ppermute | solution.py:51
  176.5 59.4 %collective-permute-start.93 = (bf16[128,2048]{1,0:T(8,128)(2,1)}, bf16[128,2048]{1,0:T(8,128)(2,1)S(1)}, u32[]{:S(2)}, u32[]{:S(2)}) collective-permute-start(bf16[128,2048]{1,0:T(8,128)(2,1)} %collective-permute-done.92), channel_id=1, source_target_pairs={{4,0},{8,4},{5,1},{9,5},{6,2},{10,6},{7,3},{11,7},{20,16},{24,20},... | collective-permute-start | bytes 1572872 | tf_op jit(solution)/shard_map/ppermute | solution.py:51
  315.3 160.2 %collective-permute-start.110 = (bf16[128,2048]{1,0:T(8,128)(2,1)S(1)}, bf16[128,2048]{1,0:T(8,128)(2,1)S(1)}, u32[]{:S(2)}, u32[]{:S(2)}) collective-permute-start(bf16[128,2048]{1,0:T(8,128)(2,1)S(1)} %collective-permute-done.109), channel_id=1, source_target_pairs={{4,0},{8,4},{5,1},{9,5},{6,2},{10,6},{7,3},{11,7},{20,16},{24,20},... | collective-permute-start | bytes 1572872 | tf_op jit(solution)/shard_map/ppermute | solution.py:51
  323.5 152.0 %collective-permute-start.113 = (bf16[128,2048]{1,0:T(8,128)(2,1)S(1)}, bf16[128,2048]{1,0:T(8,128)(2,1)}, u32[]{:S(2)}, u32[]{:S(2)}) collective-permute-start(bf16[128,2048]{1,0:T(8,128)(2,1)S(1)} %collective-permute-done.108), channel_id=1, source_target_pairs={{4,8},{8,12},{5,9},{9,13},{6,10},{10,14},{7,11},{11,15},{20,24},{2... | collective-permute-start | bytes 1572872 | tf_op jit(solution)/shard_map/ppermute | solution.py:49
  356.5 117.4 %collective-permute-start.36 = (bf16[128,2048]{1,0:T(8,128)(2,1)S(1)}, bf16[128,2048]{1,0:T(8,128)(2,1)S(1)}, u32[]{:S(2)}, u32[]{:S(2)}) collective-permute-start(bf16[128,2048]{1,0:T(8,128)(2,1)S(1)} %collective-permute-done.34), channel_id=1, source_target_pairs={{8,12},{9,13},{10,14},{11,15},{24,28},{25,29},{26,30},{27,31}} | collective-permute-start | bytes 1572872 | tf_op jit(solution)/shard_map/ppermute | solution.py:49
  476.9 138.0 %collective-permute-start.115 = (bf16[128,2048]{1,0:T(8,128)(2,1)}, bf16[128,2048]{1,0:T(8,128)(2,1)}, u32[]{:S(2)}, u32[]{:S(2)}) collective-permute-start(bf16[128,2048]{1,0:T(8,128)(2,1)} %collective-permute-done.113), channel_id=1, source_target_pairs={{8,12},{9,13},{10,14},{11,15},{24,28},{25,29},{26,30},{27,31}} | collective-permute-start | bytes 1572872 | tf_op jit(solution)/shard_map/ppermute | solution.py:49
  690.7 70.5 %collective-permute-start.73 = (bf16[128,2048]{1,0:T(8,128)(2,1)S(1)}, bf16[128,2048]{1,0:T(8,128)(2,1)}, u32[]{:S(2)}, u32[]{:S(2)}) collective-permute-start(bf16[128,2048]{1,0:T(8,128)(2,1)S(1)} %get-tuple-element.145), channel_id=1, source_target_pairs={{0,1},{1,0},{2,3},{3,2},{4,5},{5,4},{6,7},{7,6},{8,9},{9,8},{10,11... | collective-permute-start | bytes 1572872 | tf_op jit(solution)/shard_map/ppermute | solution.py:41
  901.0 87.4 %collective-permute-start.167 = (bf16[512,2048]{1,0:T(8,128)(2,1)}, bf16[512,2048]{1,0:T(8,128)(2,1)}, u32[]{:S(2)}, u32[]{:S(2)}) collective-permute-start(bf16[512,2048]{1,0:T(8,128)(2,1)} %constant_dynamic-slice_fusion), channel_id=1, source_target_pairs={{0,2},{2,0},{1,3},{3,1},{4,6},{6,4},{5,7},{7,5},{8,10},{10,8},{9,1... | collective-permute-start | bytes 6291464 | tf_op jit(solution)/shard_map/ppermute | solution.py:41
  993.7 183.1 %collective-permute-start.161 = (bf16[4,2,128,2048]{3,2,1,0:T(8,128)(2,1)}, bf16[4,2,128,2048]{3,2,1,0:T(8,128)(2,1)}, u32[]{:S(2)}, u32[]{:S(2)}) collective-permute-start(bf16[4,2,128,2048]{3,2,1,0:T(8,128)(2,1)} %dynamic-slice_bitcast_fusion), channel_id=1, source_target_pairs={{0,2},{2,0},{1,3},{3,1},{4,6},{6,4},{5,7},{7,5},{8,10},{10,8},{9,1... | collective-permute-start | bytes 12582920 | tf_op jit(solution)/shard_map/ppermute | solution.py:41
  999.4 226.2 %collective-permute-start.168 = (bf16[512,2048]{1,0:T(8,128)(2,1)}, bf16[512,2048]{1,0:T(8,128)(2,1)}, u32[]{:S(2)}, u32[]{:S(2)}) collective-permute-start(bf16[512,2048]{1,0:T(8,128)(2,1)} %add_convert_fusion), channel_id=1, source_target_pairs={{0,16},{16,0},{1,17},{17,1},{2,18},{18,2},{3,19},{19,3},{4,20},{20... | collective-permute-start | bytes 6291464 | tf_op jit(solution)/shard_map/ppermute | solution.py:41
  1242.1 185.1 %collective-permute-start.142 = (bf16[128,256]{1,0:T(8,128)(2,1)S(1)}, bf16[128,256]{1,0:T(8,128)(2,1)S(1)}, u32[]{:S(2)}, u32[]{:S(2)}) collective-permute-start(bf16[128,256]{1,0:T(8,128)(2,1)S(1)} %fusion.152), channel_id=1, source_target_pairs={{0,16},{16,0},{1,17},{17,1},{2,18},{18,2},{3,19},{19,3},{4,20},{20... | collective-permute-start | bytes 196616 | tf_op jit(solution)/shard_map/ppermute | solution.py:41
  1248.8 67.5 %collective-permute-start.164 = (bf16[128,4096]{1,0:T(8,128)(2,1)}, bf16[128,4096]{1,0:T(8,128)(2,1)}, u32[]{:S(2)}, u32[]{:S(2)}) collective-permute-start(bf16[128,4096]{1,0:T(8,128)(2,1)} %get-tuple-element.199), channel_id=1, source_target_pairs={{0,8},{4,12},{8,0},{12,4},{1,9},{5,13},{9,1},{13,5},{2,10},{6,14},... | collective-permute-start | bytes 3145736 | tf_op jit(solution)/shard_map/ppermute | solution.py:176
  1260.1 58.2 %collective-permute-start.153 = (bf16[4,128,2048]{2,1,0:T(8,128)(2,1)}, bf16[4,128,2048]{2,1,0:T(8,128)(2,1)}, u32[]{:S(2)}, u32[]{:S(2)}) collective-permute-start(bf16[4,128,2048]{2,1,0:T(8,128)(2,1)} %dynamic-slice_bitcast_fusion.3), channel_id=1, source_target_pairs={{0,2},{2,0},{1,3},{3,1},{4,6},{6,4},{5,7},{7,5},{8,10},{10,8},{9,1... | collective-permute-start | bytes 6291464 | tf_op jit(solution)/shard_map/ppermute | solution.py:41
  1272.6 99.4 %collective-permute-start.144 = (bf16[4,128,3072]{2,1,0:T(8,128)(2,1)S(1)}, bf16[4,128,3072]{2,1,0:T(8,128)(2,1)S(1)}, u32[]{:S(2)}, u32[]{:S(2)}) collective-permute-start(bf16[4,128,3072]{2,1,0:T(8,128)(2,1)S(1)} %dynamic-slice_bitcast_fusion.1), channel_id=1, source_target_pairs={{0,2},{2,0},{1,3},{3,1},{4,6},{6,4},{5,7},{7,5},{8,10},{10,8},{9,1... | collective-permute-start | bytes 9437192 | tf_op jit(solution)/shard_map/ppermute | solution.py:41
  1277.0 121.9 %collective-permute-start.165 = (bf16[128,4096]{1,0:T(8,128)(2,1)S(1)}, bf16[128,4096]{1,0:T(8,128)(2,1)S(1)}, u32[]{:S(2)}, u32[]{:S(2)}) collective-permute-start(bf16[128,4096]{1,0:T(8,128)(2,1)S(1)} %copy-done.93), channel_id=1, source_target_pairs={{0,12},{4,0},{8,4},{12,8},{1,13},{5,1},{9,5},{13,9},{2,14},{6,2},{... | collective-permute-start | bytes 3145736 | tf_op jit(solution)/shard_map/ppermute | solution.py:176
  1420.2 97.1 %collective-permute-start.166 = (bf16[128,16384]{1,0:T(8,128)(2,1)}, bf16[128,16384]{1,0:T(8,128)(2,1)}, u32[]{:S(2)}, u32[]{:S(2)}) collective-permute-start(bf16[128,16384]{1,0:T(8,128)(2,1)} %slice_dynamic-update-slice_fusion), channel_id=1, source_target_pairs={{0,16},{16,0},{1,17},{17,1},{2,18},{18,2},{3,19},{19,3},{4,20},{20... | collective-permute-start | bytes 12582920 | tf_op jit(solution)/shard_map/ppermute | solution.py:41
  1459.3 69.1 %collective-permute-start.160 = (bf16[128,2048]{1,0:T(8,128)(2,1)S(1)}, bf16[128,2048]{1,0:T(8,128)(2,1)S(1)}, u32[]{:S(2)}, u32[]{:S(2)}) collective-permute-start(bf16[128,2048]{1,0:T(8,128)(2,1)S(1)} %fusion.71), channel_id=1, source_target_pairs={{0,16},{16,0},{1,17},{17,1},{2,18},{18,2},{3,19},{19,3},{4,20},{20... | collective-permute-start | bytes 1572872 | tf_op jit(solution)/shard_map/ppermute | solution.py:41
  1480.6 64.2 %collective-permute-start.151 = (bf16[128,3072]{1,0:T(8,128)(2,1)S(1)}, bf16[128,3072]{1,0:T(8,128)(2,1)S(1)}, u32[]{:S(2)}, u32[]{:S(2)}) collective-permute-start(bf16[128,3072]{1,0:T(8,128)(2,1)S(1)} %fusion.51), channel_id=1, source_target_pairs={{0,16},{16,0},{1,17},{17,1},{2,18},{18,2},{3,19},{19,3},{4,20},{20... | collective-permute-start | bytes 2359304 | tf_op jit(solution)/shard_map/ppermute | solution.py:41
  (318 other events, 8006.3 us)

commit v2 on v1

v2 whole, which is shorter than its diff:
```python
import jax
import jax.numpy as jnp
from jax import lax
from jax.experimental import pallas as pl
from jax.experimental.pallas import tpu as pltpu
from jax.sharding import Mesh, PartitionSpec as P

D = 2048
HEADS = 32
KV = 8
HD = 64
FF = 8192
RANK = 8
WINDOW = 64
MAXLEN = 1024
KVW = KV * HD
COLS = D + 2 * KVW
GROUP = HEADS // KV
NORM_EPS = 1e-05
SCALE = 2.0
ROPE_BASE = 500000.0
SROWS = 80
PACK = 256
bf16 = jnp.bfloat16
f32 = jnp.float32


def mm(a, b):
    return jnp.dot(a, b, preferred_element_type=f32)


def mm_t(a, b):
    return lax.dot_general(a, b, (((1,), (1,)), ((), ())), preferred_element_type=f32)


def t_mm(a, b):
    return lax.dot_general(a, b, (((0,), (0,)), ((), ())), preferred_element_type=f32)


class Links:
    def __init__(self):
        self.last = {}

    def move(self, a, axis, pairs, on=None):
        on = on or {"z": ("outer", "middle")}.get(axis, (axis,))
        before = [self.last[link] for link in on if link in self.last]
        if before:
            a = lax.optimization_barrier((a, *before))[0]
        out = lax.ppermute(a, axis, pairs)
        self.last.update({link: out for link in on})
        return out

    def swap(self, a, axis):
        return self.move(a, axis, [(0, 1), (1, 0)])

    def shift(self, a, k):
        nz = lax.axis_size("z")
        return self.move(a, "z", [(i, (i + k) % nz) for i in range(nz)])

    def slots(self):
        nz, z = lax.axis_size("z"), lax.axis_index("z")
        if nz == 4:
            low = z < 2
            return [z, z ^ 1, jnp.where(low, 2, 1), jnp.where(low, 3, 0)]
        return [lax.rem(z - k + nz, nz) for k in [0] + self.line_order()]

    def line_gather(self, block):
        z = lax.axis_index("z")
        if lax.axis_size("z") != 4:
            return [block] + [self.shift(block, k) for k in self.line_order()]
        ends, ends_out, middle = [(0, 1), (1, 0), (2, 3), (3, 2)], [(1, 0), (2, 3)], [(1, 2), (2, 1)]
        inner = (z == 1) | (z == 2)
        first = self.move(block, "z", ends, ("outer",))
        second = self.move(block, "z", middle, ("middle",))
        second_end = self.move(second, "z", ends_out, ("outer",))
        third = self.move(first, "z", middle, ("middle",))
        third_end = self.move(third, "z", ends_out, ("outer",))
        return [
            block,
            first,
            lambda: jnp.where(inner, second, second_end),
            lambda: jnp.where(inner, third, third_end),
        ]

    def line_scatter(self, parts, hold=()):
        if lax.axis_size("z") != 4:
            moved = [self.shift(parts[i + 1], -k) for i, k in enumerate(self.line_order())]
            return sum([m.astype(f32) for m in moved], parts[0].astype(f32))
        ends, ends_in, middle = [(0, 1), (1, 0), (2, 3), (3, 2)], [(0, 1), (3, 2)], [(1, 2), (2, 1)]
        add = lambda a, b: (a.astype(f32) + b.astype(f32)).astype(bf16)
        own, first, second, third = parts
        third_in = self.move(third, "z", ends_in, ("outer",))
        second_in = self.move(second, "z", ends_in, ("outer",))
        third_in = self.move(add(third, third_in), "z", middle, ("middle",))
        second_in = self.move(add(second, second_in), "z", middle, ("middle",))
        first_in = self.move(add(first, third_in), "z", ends, ("outer",))
        return own.astype(f32) + first_in.astype(f32) + second_in.astype(f32)

    def line_order(self):
        nz = lax.axis_size("z")
        return sorted(range(1, nz), key=lambda k: (min(k, nz - k), k))


def pick(a, i, dim):
    return lax.dynamic_index_in_dim(a, i, dim, False)


def after(a, *others):
    return lax.optimization_barrier((a,) + others)[0]


def by_owner(a):
    nz = lax.axis_size("z")
    z, x, c = lax.axis_index("z"), lax.axis_index("x"), lax.axis_index("c")
    width = a.shape[1] // (4 * nz)
    pieces = []
    for dc in range(2):
        for dx in range(2):
            for k in range(nz):
                at = (lax.rem(z - k + nz, nz) * 2 + (x ^ dx)) * 2 + (c ^ dc)
                pieces.append(lax.dynamic_slice_in_dim(a, at * width, width, 1))
    half = 2 * nz
    return jnp.concatenate(pieces[:half], axis=1), jnp.concatenate(pieces[half:], axis=1)


def core_product(links, mine, theirs, right):
    other = links.swap(t_mm(theirs, right).astype(bf16), "c")
    return lambda *late: (t_mm(mine, right) + after(other, *late).astype(f32)).astype(bf16)


def scatter_x(links, t):
    half = t.shape[0] // 2
    other = links.swap(t[half:], "x")
    return lambda *late: (t[:half].astype(f32) + after(other, *late).astype(f32)).astype(bf16)


def scatter_line(links, t):
    nz = lax.axis_size("z")
    mine, theirs = split_replica(t.reshape(nz, -1, t.shape[1]))
    other = links.swap(theirs, "r")

    def second(*late):
        half = (mine.astype(f32) + after(other, *late).astype(f32)).astype(bf16)
        moved = [links.shift(half[k], -k) for k in links.line_order()]

        def third(*late):
            own = sum([after(m, *late).astype(f32) for m in moved], half[0].astype(f32))
            own = own.astype(bf16)
            far = links.swap(own, "r")
            return lambda: join_replica(own, far)

        return third

    return second


def line_columns(links, weight):
    nz, z = lax.axis_size("z"), lax.axis_index("z")
    rows = weight.shape[0]
    wide = FF // nz
    parts = [None] * nz
    for k in [0] + links.line_order():
        to = lax.rem(z + k, nz)
        part = jnp.concatenate(
            [lax.dynamic_slice(weight, (0, g * FF + to * wide), (rows, wide)) for g in range(2)],
            axis=1,
        )
        parts[k] = links.shift(part, k) if k else part
    return parts


def core_columns(links, parts):
    c = lax.axis_index("c")
    loc = parts[0].shape[1] // 8

    def columns(core):
        return jnp.stack(
            [
                jnp.concatenate(
                    [
                        lax.dynamic_slice_in_dim(p, (4 * g + 2 * x + core) * loc, loc, 1)
                        for x in range(2)
                        for g in range(2)
                    ],
                    axis=1,
                )
                for p in parts
            ]
        )

    mine, theirs = columns(c), links.swap(columns(1 - c), "c")
    return jnp.stack([jnp.where(c == 0, mine, theirs), jnp.where(c == 0, theirs, mine)], axis=1)


def join_gate_up(near, far, near_other, far_other):
    nz = lax.axis_size("z")
    z, x, y = lax.axis_index("z"), lax.axis_index("x"), lax.axis_index("r")
    rows, wide = near.shape[2:]

    def body(at_ref, near_ref, far_ref, near_o_ref, far_o_ref, out_ref):
        h, d = at_ref[2], pl.program_id(1)
        for where, mine, other in ((0, near_ref, near_o_ref), (1, far_ref, far_o_ref)):

            @pl.when(d == where)
            def _():
                for c in range(2):
                    out_ref[0, 0, c, pl.ds(h, 1)] = mine[0, c][None]
                    out_ref[0, 0, c, pl.ds(1 - h, 1)] = other[0, c][None]

    block = pl.BlockSpec((1, 2, rows, wide), lambda k, d, at: (k, 0, 0, 0))
    place = lambda k, d, at: (lax.rem(at[0] - k + nz, nz), at[1] ^ d, 0, 0, 0, 0)
    out = pl.pallas_call(
        body,
        out_shape=jax.ShapeDtypeStruct((nz, 2, 2, 2, rows, wide), bf16),
        grid_spec=pltpu.PrefetchScalarGridSpec(
            num_scalar_prefetch=1,
            grid=(nz, 2),
            in_specs=[block] * 4,
            out_specs=pl.BlockSpec((1, 1, 2, 2, rows, wide), place),
        ),
        cost_estimate=pl.CostEstimate(
            flops=0, bytes_accessed=16 * near.size, transcendentals=0
        ),
        name="join_gate_up",
    )(jnp.stack([z, x, y]).astype(jnp.int32), near, far, near_other, far_other)
    return out.reshape(-1, wide)


def split_replica(t):
    y = lax.axis_index("r")
    t = t.reshape(t.shape[0], 2, -1, t.shape[2])
    return pick(t, y, 1), pick(t, 1 - y, 1)


def join_replica(mine, other):
    y = lax.axis_index("r")
    return jnp.concatenate(
        [jnp.where(y == 0, mine, other), jnp.where(y == 0, other, mine)], axis=0
    ).astype(f32)


def whole_rows(halves):
    rows, cols = halves[0][0].shape
    wide = min(cols, 2048)
    tiles = cols // wide

    def body(at_ref, *refs):
        out_ref, g, h = refs[-1], pl.program_id(0), at_ref[0]
        for i in range(len(halves)):

            @pl.when(g == i)
            def _():
                out_ref[pl.ds(h, 1)] = refs[2 * i][...].astype(f32)[None]
                out_ref[pl.ds(1 - h, 1)] = refs[2 * i + 1][...].astype(f32)[None]

    def block(i):
        return pl.BlockSpec(
            (rows, wide), lambda g, j, at: (0, jnp.where(g == i, j, jnp.where(g < i, 0, tiles - 1)))
        )

    out = pl.pallas_call(
        body,
        out_shape=jax.ShapeDtypeStruct((2, rows, len(halves) * cols), f32),
        grid_spec=pltpu.PrefetchScalarGridSpec(
            num_scalar_prefetch=1,
            grid=(len(halves), tiles),
            in_specs=[block(i) for i in range(len(halves)) for _ in range(2)],
            out_specs=pl.BlockSpec((2, rows, wide), lambda g, j, at: (0, 0, g * tiles + j)),
        ),
        cost_estimate=pl.CostEstimate(
            flops=0, bytes_accessed=12 * len(halves) * rows * cols, transcendentals=0
        ),
        name="whole_rows",
    )(lax.axis_index("r").astype(jnp.int32)[None], *[a for pair in halves for a in pair])
    return out.reshape(2 * rows, -1)


def split_core(links, t, *late):
    c = lax.axis_index("c")
    t = t.reshape(t.shape[0], 2, -1, t.shape[2])
    loc = t.shape[3] // 2
    mine, theirs = pick(t, c, 1), after(links.swap(pick(t, 1 - c, 1), "c"), *late)
    first, second = jnp.where(c == 0, mine, theirs), jnp.where(c == 0, theirs, mine)
    pieces = []
    for j in range(2):
        pieces += [first[:, :, j * loc : (j + 1) * loc], second[:, :, j * loc : (j + 1) * loc]]
    return jnp.concatenate(pieces, axis=2)


def split_line(links, t):
    nz, z = lax.axis_size("z"), lax.axis_index("z")
    parts = [pick(t, lax.rem(z + k, nz), 0) for k in range(nz)]
    for k in links.line_order():
        parts[k] = links.shift(parts[k], k)
    return parts


def join_line(parts):
    nz, z = lax.axis_size("z"), lax.axis_index("z")
    rows, wide = parts[0].shape
    out = jnp.zeros((rows, nz * wide), bf16)
    for k in range(nz):
        at = lax.rem(z - k + nz, nz)
        out = lax.dynamic_update_slice(out, parts[k], (0, at * wide))
    return out


def turn(v, cosine, sine):
    lane = lax.broadcasted_iota(jnp.int32, v.shape, 1)
    low_half = (lane & 63) < 32
    other = jnp.where(low_half, pltpu.roll(v, 96, 1), pltpu.roll(v, 32, 1))
    return v * cosine + other * sine


def rope_kernel(v_ref, cos_ref, sin_ref, o_ref, *, turned):
    j = pl.program_id(0)

    @pl.when(j < turned)
    def _():
        for s in range(4):
            at = slice(s * 128, (s + 1) * 128)
            o_ref[:, at] = turn(v_ref[:, at], cos_ref[...], sin_ref[...]).astype(bf16)

    @pl.when(j >= turned)
    def _():
        o_ref[...] = v_ref[...].astype(bf16)


def rope(values, cosine, sine, turned):
    rows, cols = values.shape
    full = pl.BlockSpec((rows, 128), lambda j: (0, 0))
    return pl.pallas_call(
        lambda *refs: rope_kernel(*refs, turned=turned),
        out_shape=jax.ShapeDtypeStruct((rows, cols), bf16),
        grid=(cols // 512,),
        in_specs=[pl.BlockSpec((rows, 512), lambda j: (0, j)), full, full],
        out_specs=pl.BlockSpec((rows, 512), lambda j: (0, j)),
        cost_estimate=pl.CostEstimate(
            flops=6 * rows * cols, bytes_accessed=6 * rows * cols, transcendentals=0
        ),
        name="rope",
    )(values, cosine, sine)


def halves(shape):
    return lax.broadcasted_iota(jnp.int32, shape, 1) < 64


def feature(z2):
    first = halves(z2.shape)
    top = jnp.max(jnp.where(first, z2, -jnp.inf), axis=1, keepdims=True)
    low = jnp.max(jnp.where(first, -jnp.inf, z2), axis=1, keepdims=True)
    e = jnp.exp(z2 - jnp.where(first, top, low))
    s1 = jnp.sum(jnp.where(first, e, 0.0), axis=1, keepdims=True)
    s2 = jnp.sum(jnp.where(first, 0.0, e), axis=1, keepdims=True)
    return e * jnp.where(first, 1.0 / s1, 1.0 / s2)


def feature_grad(phi, dphi):
    first = halves(phi.shape)
    t = phi * dphi
    s1 = jnp.sum(jnp.where(first, t, 0.0), axis=1, keepdims=True)
    s2 = jnp.sum(jnp.where(first, 0.0, t), axis=1, keepdims=True)
    return t - phi * jnp.where(first, s1, s2)


def with_one(v):
    wide = jnp.concatenate([v, jnp.zeros_like(v)], axis=1)
    lane = lax.broadcasted_iota(jnp.int32, wide.shape, 1)
    return jnp.where(lane == 64, jnp.ones_like(wide), wide)


def tile(a):
    return jnp.concatenate([a] * GROUP, axis=0)


def attention_masks(row_ref, col_ref):
    rows, extent = row_ref.shape[0], col_ref.shape[1]
    offset = (
        lax.broadcasted_iota(jnp.int32, (rows, extent), 0)
        + WINDOW
        - lax.broadcasted_iota(jnp.int32, (rows, extent), 1)
    )
    same = row_ref[:, 0:1] == col_ref[0:1, :]
    live = col_ref[1:2, :] > 0
    window = (offset >= 0) & (offset < WINDOW) & same & (live | (offset == 0))
    far = (offset >= WINDOW) & same & live
    return tile(window.astype(f32)) > 0, tile(far.astype(f32)) > 0


def query_heads(ref, hh):
    return [ref[:, (hh * GROUP + i) * HD : (hh * GROUP + i + 1) * HD] for i in range(GROUP)]


def head_forward(q_ref, k, wq_ref, wk, hh, window, far):
    qs = query_heads(q_ref, hh)
    q4 = jnp.concatenate(qs, axis=0)
    s = jnp.where(window, mm_t(q4, k) * 0.125, -1e30)
    top = jnp.max(s, axis=1, keepdims=True)
    p = jnp.exp(s - top)
    e = jnp.exp(-top)
    phi = feature(
        jnp.concatenate([mm(qs[i], wq_ref[hh * GROUP + i]) for i in range(GROUP)], axis=0)
    )
    phik = feature(mm(k, wk))
    phi_b, phik_b = phi.astype(bf16), phik.astype(bf16)
    a_b = (p + e * jnp.where(far, mm_t(phi_b, phik_b), 0.0)).astype(bf16)
    return qs, q4, p, e, phi, phi_b, phik, phik_b, a_b


def full_state(st):
    return jnp.concatenate([st, jnp.zeros((128 - SROWS, 128), bf16)], axis=0)


def attend_kernel(q_ref, k_ref, v_ref, wq_ref, wk_ref, row_ref, col_ref, nd_ref, phi_ref):
    window, far = attention_masks(row_ref, col_ref)
    use = tile(row_ref[:, 1:2])
    for hh in range(2):
        at = slice(hh * HD, (hh + 1) * HD)
        _, _, _, e, phi, _, _, _, a_b = head_forward(
            q_ref, k_ref[:, at], wq_ref, wk_ref[hh], hh, window, far
        )
        nd_ref[0, hh] = mm(a_b, with_one(v_ref[:, at]))
        phi_ref[0, hh] = ((e * use) * phi).astype(bf16)


def finish_kernel(nd_ref, phi_ref, st_ref, row_ref, nd_out, o_ref):
    rows = row_ref.shape[0]
    live = tile(row_ref[:, 2:3])
    for hh in range(2):
        nd = nd_ref[0, hh] + mm_t(phi_ref[0, hh], full_state(st_ref[0, hh]))
        nd_out[0, hh] = nd
        out = (nd[:, :HD] * (live / nd[:, HD : HD + 1])).astype(bf16)
        for i in range(GROUP):
            j = hh * GROUP + i
            o_ref[:, j * HD : (j + 1) * HD] = out[i * rows : (i + 1) * rows]


def numerator_grad(do_ref, nd, live, hh):
    do4 = jnp.concatenate(query_heads(do_ref, hh), axis=0)
    inv = 1.0 / nd[:, HD : HD + 1]
    dnum = do4 * (live * inv)
    dden = -jnp.sum(dnum * nd[:, :HD], axis=1, keepdims=True) * inv
    dn = jnp.concatenate([dnum, jnp.zeros_like(dnum)], axis=1)
    lane = lax.broadcasted_iota(jnp.int32, dn.shape, 1)
    return jnp.where(lane == HD, dden, dn)


def state_grad_kernel(do_ref, nd_ref, phi_ref, row_ref, dst_ref):
    live = tile(row_ref[:, 2:3])
    for hh in range(2):
        dn = numerator_grad(do_ref, nd_ref[0, hh], live, hh)
        dst_ref[0, hh] = t_mm(dn.astype(bf16), phi_ref[0, hh])[:SROWS].astype(bf16)


def attend_back_kernel(
    q_ref, k_ref, v_ref, st_ref, wq_ref, wk_ref, row_ref, col_ref, do_ref, nd_ref, cos_ref,
    sin_ref, dq_ref, dk_ref, dv_ref, dwq_ref, dwk_ref, scr_ref,
):
    rows = q_ref.shape[0]
    window, far = attention_masks(row_ref, col_ref)
    use, live = tile(row_ref[:, 1:2]), tile(row_ref[:, 2:3])
    for hh in range(2):
        at = slice(hh * HD, (hh + 1) * HD)
        k = k_ref[:, at]
        qs, q4, p, e, phi, phi_b, phik, phik_b, a_b = head_forward(
            q_ref, k, wq_ref, wk_ref[hh], hh, window, far
        )
        dn = numerator_grad(do_ref, nd_ref[0, hh], live, hh)
        dn_b = dn.astype(bf16)
        en_b = ((e * use) * dn).astype(bf16)
        da = mm_t(dn_b, with_one(v_ref[:, at]))
        ds_b = (da * p * 0.125).astype(bf16)
        dl_b = jnp.where(far, e * da, 0.0).astype(bf16)
        dv_ref[:, at] = t_mm(a_b, dn_b)[:, :HD]
        dphi = mm(dl_b, phik_b) + mm(en_b, full_state(st_ref[0, hh]))
        dz = feature_grad(phi, dphi).astype(bf16)
        dzk = feature_grad(phik, t_mm(dl_b, phi_b)).astype(bf16)
        dq4 = mm(ds_b, k)
        dk_ref[:, at] = t_mm(ds_b, q4) + mm_t(dzk, wk_ref[hh])
        dwk_ref[0, hh] = t_mm(k, dzk)
        for i in range(GROUP):
            j = hh * GROUP + i
            dzi = dz[i * rows : (i + 1) * rows]
            scr_ref[:, j * HD : (j + 1) * HD] = dq4[i * rows : (i + 1) * rows] + mm_t(
                dzi, wq_ref[j]
            )
            dwq_ref[0, j] = t_mm(qs[i], dzi)
    for s in range(4):
        at = slice(s * 128, (s + 1) * 128)
        dq_ref[:, at] = turn(scr_ref[:, at], cos_ref[...], -sin_ref[...]).astype(bf16)


def state_kernel(k_ref, v_ref, wk_ref, row_ref, add_ref):
    rows = row_ref.shape[0]
    chosen = row_ref[:, 3:4]
    for hh in range(2):
        at = slice(hh * HD, (hh + 1) * HD)
        phik = (feature(mm(k_ref[:rows, at], wk_ref[hh])) * chosen).astype(bf16)
        add_ref[0, hh] = t_mm(with_one(v_ref[:rows, at]), phik)[:SROWS].astype(bf16)


def state_back_kernel(
    k_ref, v_ref, wk_ref, row_ref, dadd_ref, dk_in, dv_in, dk_ref, dv_ref, dwk_ref
):
    rows = row_ref.shape[0]
    chosen = row_ref[:, 3:4]
    dk_ref[rows:] = dk_in[rows:]
    dv_ref[rows:] = dv_in[rows:]
    for hh in range(2):
        at = slice(hh * HD, (hh + 1) * HD)
        k = k_ref[:rows, at]
        phik = feature(mm(k, wk_ref[hh]))
        dadd = full_state(dadd_ref[0, hh])
        dphi = mm(with_one(v_ref[:rows, at]), dadd) * chosen
        dz = feature_grad(phik, dphi).astype(bf16)
        dk_ref[:rows, at] = dk_in[:rows, at] + mm_t(dz, wk_ref[hh])
        dv_ref[:rows, at] = dv_in[:rows, at] + mm_t((phik * chosen).astype(bf16), dadd)[:, :HD]
        dwk_ref[0, hh] = t_mm(k, dz)


def call(kernel, micros, rows, extent, ins, outs, args, flops, scratch=(), only=None, into=()):
    base, count, skip, pairs = (0, micros, 0, 4) if only is None else (only[0], 1, only[1], only[2])
    block = dict(
        q=((rows, 512), lambda m, j: (m + base, j + skip)),
        k=((extent, 128), lambda m, j: (m + base, j + skip)),
        v=((extent, 128), lambda m, j: (m + base, 4 + j + skip)),
        st=((1, 2, SROWS, 128), lambda m, j: (m + base, j + skip, 0, 0)),
        nd=((1, 2, GROUP * rows, 128), lambda m, j: (m + base, j + skip, 0, 0)),
        wq=((8, HD, 128), lambda m, j: (j + skip, 0, 0)),
        wk=((2, HD, 128), lambda m, j: (j + skip, 0, 0)),
        dwq=((1, 8, HD, 128), lambda m, j: (m + base, j + skip, 0, 0)),
        dwk=((1, 2, HD, 128), lambda m, j: (m + base, j + skip, 0, 0)),
        row=((rows, 128), lambda m, j: (m + base, 0)),
        col=((8, extent), lambda m, j: (m + base, 0)),
    )
    shapes = dict(
        q=(micros * rows, D),
        k=(micros * extent, KVW),
        st=(micros, KV, SROWS, 128),
        nd=(micros, KV, GROUP * rows, 128),
        dwq=(micros, HEADS, HD, 128),
        dwk=(micros, KV, HD, 128),
    )
    spec = lambda name: pl.BlockSpec(*block[name])
    size = lambda a: a.size * a.dtype.itemsize
    out_shape = tuple(jax.ShapeDtypeStruct(shapes[name], kind) for name, kind in outs)

    def body(*refs):
        kernel(*refs[: len(ins)], *refs[len(ins) + len(into) :])

    return pl.pallas_call(
        body,
        out_shape=out_shape,
        grid=(count, pairs),
        in_specs=[spec(name) for name in ins] + [pl.BlockSpec(memory_space=pl.ANY)] * len(into),
        out_specs=tuple(spec(name) for name, _ in outs),
        scratch_shapes=scratch,
        input_output_aliases={len(ins) + i: i for i in range(len(into))},
        compiler_params=pltpu.CompilerParams(vmem_limit_bytes=48 << 20),
        cost_estimate=pl.CostEstimate(
            flops=flops * count * pairs // (4 * micros),
            bytes_accessed=(sum(size(a) for a in args) + sum(size(a) for a in out_shape))
            * (count * pairs)
            // (4 * micros),
            transcendentals=count * pairs * HEADS * rows * extent // 4,
        ),
        name=kernel.__name__,
    )(*args, *into)


def ffn_kernel(at_ref, own_ref, other_ref, pair_ref, w_ref, wd_ref, *refs):
    act_ref, dg_ref, du_ref, n2_ref, df_ref, mine_ref, theirs_ref, out_ref, dn_acc, out_acc = refs[-10:]
    f, rows, width = pl.program_id(0), own_ref.shape[0], wd_ref.shape[0]
    here = pl.ds(pl.multiple_of(at_ref[1] * rows, rows), rows)
    there = pl.ds(pl.multiple_of((1 - at_ref[1]) * rows, rows), rows)

    @pl.when(f == 0)
    def _():
        n2_ref[here] = own_ref[...]
        n2_ref[there] = other_ref[...]
        df_ref[:rows] = pair_ref[0, 0]
        df_ref[rows:] = pair_ref[0, 1]

    gate_up = mm(n2_ref[...], w_ref[...])
    gate, up = gate_up[:, :width], gate_up[:, width:]
    d_act = mm_t(df_ref[...], wd_ref[...])
    sig = 1.0 / (1.0 + jnp.exp(-gate))
    swish = gate * sig
    acted = (swish * up).astype(bf16)
    d_gate = (d_act * up * (sig * (1.0 + gate * (1.0 - sig)))).astype(bf16)
    d_up = (d_act * swish).astype(bf16)
    act_ref[...] = acted
    dg_ref[...] = d_gate
    du_ref[...] = d_up
    d_n2 = mm_t(jnp.concatenate([d_gate, d_up], axis=1), w_ref[...])
    out = mm(acted, wd_ref[...])

    @pl.when(f == 0)
    def _():
        dn_acc[...] = d_n2
        out_acc[...] = out

    @pl.when(f > 0)
    def _():
        dn_acc[...] += d_n2
        out_acc[...] += out

    @pl.when(f == pl.num_programs(0) - 1)
    def _():
        mine_ref[...] = dn_acc[here]
        theirs_ref[...] = dn_acc[there].astype(bf16)
        out_ref[0, 0] = out_acc[:rows].astype(bf16)
        out_ref[0, 1] = out_acc[rows:].astype(bf16)


def ffn_chunk(k, at, own, other, df_all, wgu, wd, held):
    rows = own.shape[0]
    total, half = df_all.shape[0] * df_all.shape[1] * rows, wd.shape[0]
    width = half // 2
    tiles = half // width
    tokens = pl.BlockSpec((rows, D), lambda f, a: (0, 0))
    chunk = pl.BlockSpec((2 * rows, D), lambda f, a: (k, 0))
    hidden = pl.BlockSpec((2 * rows, width), lambda f, a: (k, f))
    pair = pl.BlockSpec((1, 2, rows, D), lambda f, a: (a[0], 0, 0, 0))
    whole = (total, D)
    outs = [((total, half), bf16)] * 3 + [(whole, bf16)] * 2
    outs += [((rows, D), f32), ((rows, D), bf16), (df_all.shape, bf16)]
    return pl.pallas_call(
        ffn_kernel,
        out_shape=tuple(jax.ShapeDtypeStruct(a, b) for a, b in outs),
        grid_spec=pltpu.PrefetchScalarGridSpec(
            num_scalar_prefetch=1,
            grid=(tiles,),
            in_specs=[
                tokens,
                tokens,
                pair,
                pl.BlockSpec((D, 2 * width), lambda f, a: (0, f)),
                pl.BlockSpec((width, D), lambda f, a: (f, 0)),
            ]
            + [pl.BlockSpec(memory_space=pl.ANY)] * len(held),
            out_specs=(
                hidden, hidden, hidden, chunk, chunk, tokens, tokens,
                pair,
            ),
            scratch_shapes=[pltpu.VMEM((2 * rows, D), f32)] * 2,
        ),
        input_output_aliases={6 + i: (i if i < 5 else 7) for i in range(len(held))},
        compiler_params=pltpu.CompilerParams(vmem_limit_bytes=56 << 20),
        cost_estimate=pl.CostEstimate(
            flops=24 * rows * D * half,
            bytes_accessed=6 * D * half + 40 * rows * D,
            transcendentals=2 * rows * half,
        ),
        name="ffn_chunk",
    )(at, own, other, df_all, wgu, wd, *held)


def weigh(flag, a):
    return jnp.where(flag[:, None, None, None], a.astype(f32), 0.0)


def entering(links, add, tags, reach):
    nz = lax.axis_size("z")
    z, x, c = lax.axis_index("z"), lax.axis_index("x"), lax.axis_index("c")
    p = (z * 2 + x) * 2 + c
    tag = lambda i: pick(tags, jnp.clip(i, 0, 4 * nz - 1), 1)
    prev = tag(p - 1)
    chip = (z * 2 + x) * 2
    other = links.swap(add, "c")
    other = after(other, (yield))
    one = tag(chip) == tag(chip + 1)
    chip_sum = (weigh((c == 1) | one, add) + weigh((c == 0) | one, other)).astype(bf16)
    side = links.swap(chip_sum, "x")
    side = after(side, (yield))
    one = tag(z * 4 + 1) == tag(z * 4 + 3)
    layer = (weigh((x == 1) | one, chip_sum) + weigh((x == 0) | one, side)).astype(bf16)
    state = weigh((c == 1) & (prev >= 0), other) + weigh((x == 1) & (tag(z * 4 + 1) == prev), side)
    got = [
        links.move(layer, "z", [(i, i + hop) for i in range(nz - hop)])
        for hop in range(1, min(reach, nz - 1) + 1)
    ]
    late = yield
    for hop, far in enumerate(got, 1):
        state += weigh((z >= hop) & (tag((z - hop) * 4 + 3) == prev), after(far, late))
    yield state.astype(bf16)


def leaving(links, dstate, tags, reach):
    nz = lax.axis_size("z")
    z, x, c = lax.axis_index("z"), lax.axis_index("x"), lax.axis_index("c")
    p = (z * 2 + x) * 2 + c
    tag = lambda i: pick(tags, jnp.clip(i, 0, 4 * nz - 1), 1)
    from_tag = lambda i: jnp.where(i > 0, tag(i - 1), -1)
    own = tag(p)
    chip = (z * 2 + x) * 2
    other = links.swap(dstate, "c")
    other = after(other, (yield))
    one = from_tag(chip) == from_tag(chip + 1)
    chip_sum = (weigh((c == 0) | one, dstate) + weigh((c == 1) | one, other)).astype(bf16)
    side = links.swap(chip_sum, "x")
    side = after(side, (yield))
    one = from_tag(z * 4) == from_tag(z * 4 + 2)
    layer = (weigh((x == 0) | one, chip_sum) + weigh((x == 1) | one, side)).astype(bf16)
    total = weigh((c == 0) & (own >= 0), other) + weigh(
        (x == 0) & (from_tag(z * 4 + 2) == own), side
    )
    got = [
        links.move(layer, "z", [(i, i - hop) for i in range(hop, nz)])
        for hop in range(1, min(reach, nz - 1) + 1)
    ]
    late = yield
    for hop, far in enumerate(got, 1):
        total += weigh((z + hop < nz) & (from_tag((z + hop) * 4) == own), after(far, late))
    yield total.astype(bf16)


def per_device(
    inputs, cotangent, lengths, padding, gain_attn_own, wqkv_own, adown_own, aup_own, wout_own,
    odown_own, oup_own, featq_own, featk_own, gain_ffn_own, wgu_own, wd_own,
):
    nz = lax.axis_size("z")
    n = 4 * nz
    z, x, c = lax.axis_index("z"), lax.axis_index("x"), lax.axis_index("c")
    place_own = (z * 2 + x) * 2 + c
    micros, rows = inputs.shape[1], inputs.shape[2]
    both = micros * rows
    extent = rows + WINDOW
    reach = -(-MAXLEN // (4 * rows))
    everyone = ("z", "x", "c")
    chain = (everyone, [(i, i + 1) for i in range(n - 1)])
    unchain = (everyone, [(i, i - 1) for i in range(1, n)])
    r = D // n

    pack = jnp.concatenate(
        [
            gain_attn_own[:, None], adown_own, odown_own, oup_own.T, featq_own,
            gain_ffn_own[:, None], aup_own.reshape(r, 12), featk_own.reshape(r, 16),
        ],
        axis=1,
    )
    pack = jnp.pad(pack, ((0, 0), (0, PACK - pack.shape[1])))
    links = Links()
    live_all = padding[0].astype(bf16)
    halo_live = lax.ppermute(live_all[:, rows - WINDOW :], *chain)
    first = lax.all_gather(
        jnp.concatenate([wqkv_own, wout_own, pack], axis=1), everyone, axis=0, tiled=True
    )
    wqkv, wout, small = first[:, :COLS], first[:, COLS : COLS + D], first[:, COLS + D :]
    cot = cotangent[0].reshape(both, D)
    y = lax.axis_index("r")
    wgu_half = lax.dynamic_slice_in_dim(wgu_own, y * (r // 2), r // 2, 0)
    wgu_near = core_columns(links, line_columns(links, wgu_half))
    wgu_near_other = links.swap(wgu_near, "r")
    small, wgu_send = lax.optimization_barrier((small, wgu_near, wgu_near_other))[:2]
    wgu_far = links.swap(wgu_send, "x")
    gain_one = small[:, 0].astype(f32)[None]
    adown = small[:, 1:25]
    odown = small[:, 25:33]
    oup_t = small[:, 33:41]
    featq = small[:, 41:105].reshape(HEADS, HD, HD)
    gain_two = small[:, 105].astype(f32)[None]
    aup = small[:, 106:118].reshape(n, RANK, COLS // n).transpose(1, 0, 2).reshape(RANK, COLS)
    featk = small[:, 118:134].reshape(KV, HD, HD)
    wq2 = jnp.concatenate([featq, -featq], axis=2)
    wk2 = jnp.concatenate([featk, -featk], axis=2)
    column = jnp.arange(COLS)[None]
    owner = jnp.where(column < D, 0, jnp.where(column < D + KVW, 1, 2))
    aup_wide = jnp.concatenate(
        [jnp.where(owner == t, aup, jnp.zeros_like(aup)) for t in range(3)], axis=0
    )

    doc_lengths = lengths[0]
    ends = jnp.cumsum(doc_lengths, axis=1)
    places = place_own * rows - WINDOW + jnp.arange(extent, dtype=jnp.int32)
    done = ends[:, None, :] <= places[None, :, None]
    seg_ext = jnp.sum(done.astype(jnp.int32), axis=2)
    pos = places[None] - jnp.sum(jnp.where(done, doc_lengths[:, None, :], 0), axis=2)
    pos = pos[:, WINDOW:].reshape(both)
    edges = jnp.arange(n, dtype=jnp.int32) * rows + (rows - WINDOW - 1)
    tags = jnp.sum((ends[:, None, :] <= edges[None, :, None]).astype(jnp.int32), axis=2)
    live_ext = jnp.concatenate([halo_live, live_all], axis=1).astype(f32)
    prev_tag = jnp.where(place_own > 0, pick(tags, jnp.maximum(place_own - 1, 0), 1), -1)
    own_tag = pick(tags, place_own, 1)
    seg_own = seg_ext[:, WINDOW:]
    info = jnp.stack(
        [
            seg_own.astype(f32),
            (seg_own == prev_tag[:, None]).astype(f32),
            live_ext[:, WINDOW:],
            ((seg_ext[:, :rows] == own_tag[:, None]) & (live_ext[:, :rows] > 0)).astype(f32),
        ],
        axis=2,
    ).reshape(both, 4)
    rowinfo = jnp.pad(info, ((0, 0), (0, 124)))
    colinfo = jnp.pad(
        jnp.stack([seg_ext.astype(f32), live_ext], axis=1), ((0, 0), (0, 6), (0, 0))
    ).reshape(micros * 8, extent)
    lane = jnp.arange(128)
    frequency = ROPE_BASE ** (-((lane % 32).astype(f32) * 2.0) / HD)
    angles = pos.astype(f32)[:, None] * frequency[None, :]
    cosine = jnp.cos(angles)
    sine = jnp.where((lane % 64 < 32)[None], -1.0, 1.0) * jnp.sin(angles)

    act = inputs[0].reshape(both, D).astype(f32)
    inv_one = lax.rsqrt(jnp.mean(act * act, axis=-1, keepdims=True) + NORM_EPS)
    n1 = (act * inv_one * gain_one).astype(bf16)
    adapt = mm(n1, adown).astype(bf16)
    projected = mm(n1, wqkv) + SCALE * mm(adapt, aup_wide)
    qkv = rope(projected, cosine, sine, 5)
    kv = qkv[:, D:].reshape(micros, rows, 2 * KVW)
    halo = lax.ppermute(kv[:, rows - WINDOW :], *chain)
    kv_ext = jnp.concatenate([halo, kv], axis=1).reshape(micros * extent, 2 * KVW)
    launch = lambda kernel, ins, outs, args, work, **k: call(
        kernel, micros, rows, extent, ins, outs, args, micros * HEADS * rows * work, **k
    )
    (add,) = launch(
        state_kernel, ("k", "v", "wk", "row"), [("st", bf16)], (kv_ext, kv_ext, wk2, rowinfo), 8192
    )
    df_all = lax.all_gather(after(cot, small), ("z", "c"), axis=0, tiled=True)
    df_all = df_all.reshape(nz, 2, both, D)
    wd = lax.all_gather(after(wd_own, df_all), "x", axis=0, tiled=True)
    parts = [(m, j, 2) for m in range(micros) for j in (0, 2)]
    travel = entering(links, add, tags, reach)
    next(travel)
    wgu_far, wk2_late = lax.optimization_barrier((wgu_far, wk2, add))[:2]
    wgu_far_other = links.swap(wgu_far, "r")
    local = ()
    for i, part in enumerate(parts):
        local = launch(
            attend_kernel,
            ("q", "k", "v", "wq", "wk", "row", "col"),
            [("nd", f32), ("nd", bf16)],
            (qkv, kv_ext, kv_ext, wq2, wk2_late, rowinfo, colinfo),
            1000 * extent,
            only=part,
            into=local,
        )
        if i < 2:
            travel.send(local[1])
    nd, phi = local
    state = travel.send(phi)
    nd, attn = launch(
        finish_kernel,
        ("nd", "nd", "st", "row"),
        [("nd", f32), ("q", bf16)],
        (nd, phi, state, rowinfo),
        32768,
    )
    adapt_out = mm(attn, odown).astype(bf16)
    hidden = act + (mm(attn, wout) + SCALE * mm_t(adapt_out, oup_t))
    inv_two = lax.rsqrt(jnp.mean(hidden * hidden, axis=-1, keepdims=True) + NORM_EPS)
    n2 = (hidden * inv_two * gain_two).astype(bf16)

    half = 2 * FF // n
    loc = half // 2
    n2_parts = links.line_gather(n2)
    late = lambda a: after(a, attn)
    wgu = join_gate_up(late(wgu_near), wgu_far, late(wgu_near_other), late(wgu_far_other))
    returned, held = [], ()
    for i, (place, part) in enumerate(zip(links.slots(), n2_parts)):
        at = jnp.stack([place, c]).astype(jnp.int32)
        part = part() if callable(part) else part
        if i:
            part = after(part, held[0])
        result = ffn_chunk(i, at, part, links.swap(part, "c"), df_all, wgu, wd, held)
        held = result[:5] + result[7:]
        d_n2_i = result[5] + links.swap(result[6], "c").astype(f32)
        returned.append(d_n2_i.astype(bf16) if i else d_n2_i)
    acted, d_gate, d_up, n2_all, df_held, out_parts = held
    d_n2 = links.line_scatter(returned)
    g_gate = t_mm(n2_all, d_gate).astype(bf16)
    g_up = t_mm(n2_all, d_up).astype(bf16)
    g_wd = t_mm(acted, df_held).astype(bf16)
    d_n2 = after(d_n2, g_gate, g_up, g_wd)
    plus = lambda a, b: (a.astype(f32) + b.astype(f32)).astype(bf16)
    out_sum = lax.psum_scatter(
        after(out_parts, d_n2).reshape(-1, D), ("z", "c"), scatter_dimension=0, tiled=True
    )
    g_gate, g_up = g_gate.reshape(n, r, half), g_up.reshape(n, r, half)
    g_wd = g_wd.reshape(2, loc, D)
    gu_mine, gu_other = [], []
    for g in (g_gate, g_up, g_wd):
        mine, theirs = split_replica(g)
        gu_mine.append(mine)
        gu_other.append(links.swap(theirs, "r"))

    def replica_sum(i, *late):
        return (gu_mine[i].astype(f32) + after(gu_other[i], *late).astype(f32)).astype(bf16)

    def x_parts(t):
        t = t.reshape(-1, 2, t.shape[-2] * (2 if t.shape[0] == n else 1), t.shape[-1])
        return pick(t, x, 1), pick(t, 1 - x, 1)

    d_hidden = (
        cot.astype(f32)
        + gain_two * inv_two * d_n2
        - hidden * inv_two**3 * jnp.mean(hidden * gain_two * d_n2, axis=-1, keepdims=True)
    )
    d_branch = d_hidden.astype(bf16)
    d_adapt_out = (SCALE * mm(d_branch, oup_t)).astype(bf16)
    d_attn = mm_t(d_branch, wout) + mm_t(d_adapt_out, odown)
    (dst,) = launch(
        state_grad_kernel,
        ("q", "nd", "nd", "row"),
        [("st", bf16)],
        (d_attn, nd, phi, rowinfo),
        32768,
    )
    attn_owner, n1_owner = by_owner(attn), by_owner(n1)
    gate_mine, gate_theirs = x_parts(replica_sum(0, d_attn))
    gate_side = links.swap(gate_theirs, "x")
    travel = leaving(links, dst, tags, reach)
    next(travel)
    wout_core = core_product(links, *attn_owner, d_branch)
    grads = ()
    d_attn_late = d_attn
    for i, part in enumerate(parts):
        grads = launch(
            attend_back_kernel,
            ("q", "k", "v", "st", "wq", "wk", "row", "col", "q", "nd", "row", "row"),
            [("q", bf16), ("k", f32), ("k", f32), ("dwq", f32), ("dwk", f32)],
            (qkv, kv_ext, kv_ext, state, wq2, wk2, rowinfo, colinfo, d_attn_late, nd, cosine, sine),
            2000 * extent,
            scratch=[pltpu.VMEM((rows, 512), f32)],
            only=part,
            into=grads,
        )
        done = grads[0]
        if i == 0:
            travel.send(done)
            wout_x = scatter_x(links, wout_core(done))
            gate_rows = split_core(links, plus(gate_mine, after(gate_side, done)))
        elif i == 1:
            travel.send(done)
            gate_line = split_line(links, gate_rows)
            up_mine, up_theirs = x_parts(replica_sum(1, done))
            up_side = links.swap(up_theirs, "x")
        elif i == 2:
            d_attn_late = after(d_attn_late, out_sum)
    dq, dk, dv, dwq, dwk = grads
    dadd = travel.send(dq)
    wout_line = scatter_line(links, wout_x(dq))
    q_core = core_product(links, *n1_owner, dq)
    dk, dv, dwk_more = launch(
        state_back_kernel,
        ("k", "v", "wk", "row", "st", "k", "k"),
        [("k", f32), ("k", f32), ("dwk", f32)],
        (kv_ext, kv_ext, wk2, rowinfo, dadd, dk, dv),
        16384,
    )
    d_kv = jnp.concatenate([dk, dv], axis=1).reshape(micros, extent, 2 * KVW)
    sent = lax.ppermute(d_kv[:, :WINDOW].astype(bf16), *unchain)
    gate_half = join_line([after(p, dk) for p in gate_line])
    gate_far = links.swap(gate_half, "r")
    q_sum, up_rows = lax.optimization_barrier(
        (q_core(dadd), plus(up_mine, after(up_side, dadd)), sent)
    )[:2]
    q_x = scatter_x(links, q_sum)
    wout_line = wout_line(dadd, sent)
    up_line = split_line(links, split_core(links, up_rows))
    sent = sent.astype(f32)
    d_kv = jnp.concatenate([d_kv[:, WINDOW:rows], d_kv[:, rows:] + sent], axis=1)
    d_kv = rope(d_kv.reshape(both, 2 * KVW), cosine, -sine, 1)
    kv_sum = core_product(links, *n1_owner, d_kv)()
    kv_x = scatter_x(links, kv_sum)
    wd_mine, wd_theirs = x_parts(replica_sum(2, kv_sum))
    wd_side = links.swap(wd_theirs, "x")
    d_proj = jnp.concatenate([dq, d_kv], axis=1)
    d_adapt = (SCALE * mm_t(d_proj, aup_wide)).astype(bf16)
    d_n1 = mm_t(d_proj, wqkv) + mm_t(d_adapt, adown)
    g_gain_one = jnp.sum(d_n1 * act * inv_one, axis=0)
    grad_inputs = (
        d_hidden
        + gain_one * inv_one * d_n1
        - act * inv_one**3 * jnp.mean(act * gain_one * d_n1, axis=-1, keepdims=True)
    ).astype(bf16)
    g_adown = t_mm(n1, d_adapt)
    wide = SCALE * t_mm(adapt, d_proj)
    g_aup = jnp.where(owner == 0, wide[:8], jnp.where(owner == 1, wide[8:16], wide[16:24]))
    g_odown = t_mm(attn, d_adapt_out)
    g_oup_t = SCALE * t_mm(d_branch, adapt_out)
    fold = lambda a: a[:, :, :HD] - a[:, :, HD:]
    g_featq = fold(jnp.sum(dwq, axis=0)).reshape(D, HD)
    g_featk = fold(jnp.sum(dwk + dwk_more, axis=0))
    g_gain_two = jnp.sum(d_n2 * hidden * inv_two, axis=0)
    g_pack = jnp.concatenate(
        [
            g_gain_one[:, None], g_adown, g_odown, g_oup_t, g_featq, g_gain_two[:, None],
            g_aup.reshape(RANK, n, COLS // n).transpose(1, 0, 2).reshape(D, 12),
            g_featk.reshape(D, 16),
        ],
        axis=1,
    )
    g_pack = jnp.pad(g_pack, ((0, 0), (0, PACK - g_pack.shape[1]))).astype(bf16)
    nat = g_pack.reshape(nz, 2, 2, r, PACK)
    mine, theirs = pick(nat, c, 2), pick(nat, 1 - c, 2)
    nat = plus(mine, links.swap(theirs, "c"))
    mine, theirs = pick(nat, x, 1), pick(nat, 1 - x, 1)
    pack_side = links.swap(theirs, "x")
    wout_line = wout_line(theirs)
    q_line = scatter_line(links, q_x(theirs))
    kv_line = scatter_line(links, kv_x(theirs))
    wd_half = plus(wd_mine, after(wd_side, theirs)).reshape(-1, D)
    nat = plus(mine, pack_side)
    nat = jnp.concatenate([pick(nat, lax.rem(z - k + nz, nz), 0) for k in range(nz)], axis=0)
    q_line = q_line()
    up_half = join_line([after(p, theirs) for p in up_line])
    up_far = links.swap(up_half, "r")
    kv_line = kv_line()
    pack_line = scatter_line(links, nat)
    wd_far = links.swap(wd_half, "r")
    pack_line = pack_line()
    output = (hidden + after(out_sum, nat).astype(f32)).astype(bf16)
    q_line, kv_line, pack_line = q_line(), kv_line(), pack_line()
    g_small = pack_line()
    g_wout_own = wout_line()
    g_wd_own = join_replica(wd_half, wd_far)
    g_wgu_own = whole_rows([(gate_half, gate_far), (up_half, up_far)])
    g_wqkv_own = jnp.concatenate([q_line(), kv_line()], axis=1)
    return (
        output.reshape(1, micros, rows, D),
        grad_inputs.reshape(1, micros, rows, D),
        g_small[:, 0],
        g_wqkv_own,
        g_small[:, 1:25],
        g_small[:, 106:118].reshape(RANK, COLS // n),
        g_wout_own,
        g_small[:, 25:33],
        g_small[:, 33:41].T,
        g_small[:, 41:105],
        g_small[:, 118:134].reshape(KVW // n, HD),
        g_small[:, 105],
        g_wgu_own,
        g_wd_own,
    )


def solution(mesh):
    n = mesh.shape["shard"]
    fine = Mesh(mesh.devices.reshape(mesh.shape["replica"], n // 4, 2, 2), ("r", "z", "x", "c"))
    shard = ("z", "x", "c")
    tokens, row, col = P("r", None, shard, None), P(shard, None), P(None, shard)
    return jax.shard_map(
        per_device,
        mesh=fine,
        in_specs=(
            tokens, tokens, P("r", None, None), P("r", None, shard), P(shard), row, row, col, row,
            row, col, row, row, P(shard), row, row,
        ),
        out_specs=(
            tokens, tokens, P(shard), row, row, col, row, row, col, row, row, P(shard), row, row,
        ),
        check_vma=False,
    )
```

time: 1560 us -> 1070 us (0.69)
  starting transfers between devices: 319 us -> 125 us
  waiting for transfers between devices: 569 us -> 438 us
  Pallas kernels: 112 us -> 224 us
  matrix products: 191 us -> 86.5 us
  local copies, waits for them, and re-layouts: 170 us -> 83.6 us
  other arithmetic: 155 us -> 82.5 us
    ppermute x168 -> x80, waiting for transfers between devices: 569 us -> 375 us  [the longest x78 375 us: move(): out = lax.ppermute(a, axis, pairs)]
    ppermute x168 -> x80, starting transfers between devices: 317 us -> 123 us  [the longest x78 109 us: move(): out = lax.ppermute(a, axis, pairs)]
    pallas_call x8 -> x18, Pallas kernels: 98.5 us -> 217 us  [the longest x4 100 us: ffn_chunk(): pl.pallas_call(ffn_kernel, out_shape=tuple((jax.ShapeDtypeStruct(a, b) fo...]
    all_gather x0 -> x3, waiting for transfers between devices: none -> 62.8 us  [the longest x1 53.8 us: per_device(): lax.all_gather(jnp.concatenate([wqkv_own, wout_own, pack], axis=1), every...]
    dot_general x13 -> x6, matrix products: 75.3 us -> 16 us  [mm_t(): lax.dot_general(a, b, (((1,), (1,)), ((), ())), preferred_element_type=f32)]
    dot_general x16 -> x6, matrix products: 57.6 us -> 16.4 us  [mm(): return jnp.dot(a, b, preferred_element_type=f32)]
    dynamic_slice x10 -> x3, local copies, waits for them, and re-layouts: 31.9 us -> 3.84 us  [the longest x1 3.02 us: line_columns(): lax.dynamic_slice(weight, (0, g * FF + to * wide), (rows, wide))]
    unnamed x393 -> x302, local copies, waits for them, and re-layouts: 51.1 us -> 28.7 us
  transfers between devices with their start and end apart: 169 -> 85, of which waited for: 58 -> 46; matrix products, arithmetic and copies ran while one was open for 29% -> 20% of each run, Pallas kernels for 7% -> 19%
where the time goes in v2:
time: 1070 us; the launch traced here: 1060 us
  waiting for transfers between devices  438 us (41%)
  Pallas kernels  224 us (21%)
  starting transfers between devices  125 us (12%)
  matrix products  86.5 us (8%)
  local copies, waits for them, and re-layouts  83.6 us (8%)
  other arithmetic  82.5 us (8%)
  between operations  17 us (2%)
    ppermute x78, waiting for transfers between devices, move(): out = lax.ppermute(a, axis, pairs)  375 us
    ppermute x78, starting transfers between devices, move(): out = lax.ppermute(a, axis, pairs)  109 us
    pallas_call x4, Pallas kernels, ffn_chunk(): pl.pallas_call(ffn_kernel, out_shape=tuple((jax.ShapeDtypeStruct(a, b) fo...  100 us
    pallas_call x12, Pallas kernels, call(): pl.pallas_call(body, out_shape=out_shape, grid=(count, pairs), in_specs=[...  98.2 us
    dot_general x13, matrix products, t_mm(): lax.dot_general(a, b, (((0,), (0,)), ((), ())), preferred_element_type=f32)  54.1 us
    all_gather x1, waiting for transfers between devices, per_device(): lax.all_gather(jnp.concatenate([wqkv_own, wout_own, pack], axis=1), every...  53.8 us
    unnamed x302, local copies, waits for them, and re-layouts  28.7 us
  transfers between devices with their start and end apart: 85, of which 46 were waited for; matrix products, arithmetic and copies ran while one was open for 20% of the time, Pallas kernels for 19%

profile of v2, /device:TPU:0, one launch (start us, length us, event | category | flops | bytes accessed | tf_op | source)
XLA Modules:
  0.0 1056.6 jit_solution(15307963314307243864)
XLA Ops:
  22.6 21.6 %collective-permute-done = bf16[64,4096]{1,0:T(8,128)(2,1)S(1)} collective-permute-done((bf16[64,4096]{1,0:T(8,128)(2,1)S(1)}, bf16[64,4096]{1,0:T(8,128)(2,1)S(1)}, u32[]{:S(2)}, u32[]{:S(2)}) %collective-permute-start) | collective-permute-done | bytes 524320 | tf_op jit(solution)/shard_map/ppermute | solution.py:49
  47.5 22.9 %collective-permute-done.1 = bf16[64,4096]{1,0:T(8,128)(2,1)S(1)} collective-permute-done((bf16[64,4096]{1,0:T(8,128)(2,1)S(1)}, bf16[64,4096]{1,0:T(8,128)(2,1)S(1)}, u32[]{:S(2)}, u32[]{:S(2)}) %collective-permute-start.1) | collective-permute-done | bytes 524320 | tf_op jit(solution)/shard_map/ppermute | solution.py:49
  71.5 34.3 %collective-permute-done.2 = bf16[64,4096]{1,0:T(8,128)(2,1)S(1)} collective-permute-done((bf16[64,4096]{1,0:T(8,128)(2,1)S(1)}, bf16[64,4096]{1,0:T(8,128)(2,1)S(1)}, u32[]{:S(2)}, u32[]{:S(2)}) %collective-permute-start.2) | collective-permute-done | bytes 524320 | tf_op jit(solution)/shard_map/ppermute | solution.py:49
  112.6 53.8 %all-gather.4.cloned.1.call-done = bf16[2048,5376]{1,0:T(8,128)(2,1)} async-done(((bf16[128,5376]{1,0:T(8,128)(2,1)}), bf16[2048,5376]{1,0:T(8,128)(2,1)}) %all-gather.4.cloned.1.call-update) | async-done | bytes 22020112 | tf_op jit(solution)/shard_map/all_gather | solution.py:747
  192.9 11.7 %collective-permute-start.5 = (bf16[2,64,1024]{2,1,0:T(8,128)(2,1)S(1)}, bf16[2,64,1024]{2,1,0:T(8,128)(2,1)S(1)}, u32[]{:S(2)}, u32[]{:S(2)}) collective-permute-start(bf16[2,64,1024]{2,1,0:T(8,128)(2,1)S(1)} %slice.274), channel_id=1, source_target_pairs={{0,1},{1,2},{2,3},{3,4},{4,5},{5,6},{6,7},{7,8},{8,9},{9,10},{10,1... | collective-permute-start | bytes 786440 | tf_op jit(solution)/shard_map/ppermute | solution.py:813
  210.5 19.5 %collective-permute-start.8 = (bf16[2,8,80,128]{3,2,1,0:T(8,128)(2,1)S(1)}, bf16[2,8,80,128]{3,2,1,0:T(8,128)(2,1)S(1)}, u32[]{:S(2)}, u32[]{:S(2)}) collective-permute-start(bf16[2,8,80,128]{3,2,1,0:T(8,128)(2,1)S(1)} %state_kernel.1), channel_id=1, source_target_pairs={{0,1},{1,0},{2,3},{3,2},{4,5},{5,4},{6,7},{7,6},{8,9},{9,8},{10,11... | collective-permute-start | bytes 983048 | tf_op jit(solution)/shard_map/ppermute | solution.py:49
  310.4 12.7 %collective-permute-done.18.far_o_ref = bf16[4,2,64,2048]{3,2,1,0:T(8,128)(2,1)} collective-permute-done((bf16[4,2,64,2048]{3,2,1,0:T(8,128)(2,1)}, bf16[4,2,64,2048]{3,2,1,0:T(8,128)(2,1)}, u32[]{:S(2)}, u32[]{:S(2)}) %collective-permute-start.18) | collective-permute-done | bytes 2097184 | tf_op jit(solution)/shard_map/ppermute | solution.py:49
  333.9 25.2 %ffn_chunk.4 = (bf16[2048,1024]{1,0:T(8,128)(2,1)}, bf16[2048,1024]{1,0:T(8,128)(2,1)}, bf16[2048,1024]{1,0:T(8,128)(2,1)}, bf16[2048,2048]{1,0:T(8,128)(2,1)}, ...) custom-call(s32[2]{0:T(128)} %pad_add_fusion.3.at_ref, ...), custom_call_target="tpu_custom_call" | custom-call | flops 12884901888 | bytes 33554432 | tf_op jit(solution)/shard_map/ffn_chunk/pallas_call | solution.py:629
  364.9 25.0 %ffn_chunk.5 = (bf16[2048,1024]{1,0:T(8,128)(2,1)}, bf16[2048,1024]{1,0:T(8,128)(2,1)}, bf16[2048,1024]{1,0:T(8,128)(2,1)}, bf16[2048,2048]{1,0:T(8,128)(2,1)}, ...) custom-call(s32[2]{0:T(128)} %pad_add_fusion.2.at_ref, ...), custom_call_target="tpu_custom_call", output_to_operand_aliasing={{0}: (6, {}), {1}: (7, {}), {2}: (8, {}), {3}: (9, {}), {4}... | custom-call | flops 12884901888 | bytes 33554432 | tf_op jit(solution)/shard_map/ffn_chunk/pallas_call | solution.py:629
  391.7 20.3 %collective-permute-done.15 = bf16[256,2048]{1,0:T(8,128)(2,1)} collective-permute-done((bf16[256,2048]{1,0:T(8,128)(2,1)}, bf16[256,2048]{1,0:T(8,128)(2,1)}, u32[]{:S(2)}, u32[]{:S(2)}) %collective-permute-start.15) | collective-permute-done | bytes 1048608 | tf_op jit(solution)/shard_map/ppermute | solution.py:49
  416.2 24.9 %ffn_chunk.6 = (bf16[2048,1024]{1,0:T(8,128)(2,1)}, bf16[2048,1024]{1,0:T(8,128)(2,1)}, bf16[2048,1024]{1,0:T(8,128)(2,1)}, bf16[2048,2048]{1,0:T(8,128)(2,1)}, ...) custom-call(s32[2]{0:T(128)} %pad_add_fusion.1.at_ref, ...), custom_call_target="tpu_custom_call", output_to_operand_aliasing={{0}: (6, {}), {1}: (7, {}), {2}: (8, {}), {3}: (9, {}), {4}... | custom-call | flops 12884901888 | bytes 33554432 | tf_op jit(solution)/shard_map/ffn_chunk/pallas_call | solution.py:629
  441.3 25.5 %collective-permute-done.16 = bf16[256,2048]{1,0:T(8,128)(2,1)S(1)} collective-permute-done((bf16[256,2048]{1,0:T(8,128)(2,1)}, bf16[256,2048]{1,0:T(8,128)(2,1)S(1)}, u32[]{:S(2)}, u32[]{:S(2)}) %collective-permute-start.16) | collective-permute-done | bytes 1048608 | tf_op jit(solution)/shard_map/ppermute | solution.py:49
  469.9 25.1 %ffn_chunk.7 = (bf16[2048,1024]{1,0:T(8,128)(2,1)}, bf16[2048,1024]{1,0:T(8,128)(2,1)}, bf16[2048,1024]{1,0:T(8,128)(2,1)}, bf16[2048,2048]{1,0:T(8,128)(2,1)}, ...) custom-call(s32[2]{0:T(128)} %pad_add_fusion.at_ref, ...), custom_call_target="tpu_custom_call", output_to_operand_aliasing={{0}: (6, {}), {1}: (7, {}), {2}: (8, {}), {3}: (9, {}), {4}... | custom-call | flops 12884901888 | bytes 33554432 | tf_op jit(solution)/shard_map/ffn_chunk/pallas_call | solution.py:629
  506.5 13.2 %convolution_convert_fusion.2 = bf16[1024,2048]{1,0:T(8,128)(2,1)} fusion(bf16[2048,1024]{1,0:T(8,128)(2,1)} %get-tuple-element.280, bf16[2048,2048]{1,0:T(8,128)(2,1)S(1)} %copy-done.34), kind=kOutput, calls=%fused_computation.23 | convolution fusion | flops 8592031744 | bytes 16777216 | tf_op jit(solution)/shard_map/dot_general | solution.py:37
  535.0 10.9 %convolution_convert_fusion.4 = bf16[2048,1024]{1,0:T(8,128)(2,1)} fusion(bf16[2048,2048]{1,0:T(8,128)(2,1)S(1)} %bitcast.321, bf16[2048,1024]{1,0:T(8,128)(2,1)S(1)} %copy-done.43), kind=kOutput, calls=%fused_computation.25 | convolution fusion | flops 8592031744 | bytes 16777216 | tf_op jit(solution)/shard_map/dot_general | solution.py:37
  564.3 11.0 %convolution_convert_fusion.3 = bf16[2048,1024]{1,0:T(8,128)(2,1)} fusion(bf16[2048,2048]{1,0:T(8,128)(2,1)S(1)} %bitcast.321, bf16[2048,1024]{1,0:T(8,128)(2,1)S(1)} %copy-done.44), kind=kOutput, calls=%fused_computation.24 | convolution fusion | flops 8592031744 | bytes 16777216 | tf_op jit(solution)/shard_map/dot_general | solution.py:37
  628.2 39.9 %collective-permute-done.32 = bf16[16,64,1024]{2,1,0:T(8,128)(2,1)} collective-permute-done((bf16[16,64,1024]{2,1,0:T(8,128)(2,1)}, bf16[16,64,1024]{2,1,0:T(8,128)(2,1)}, u32[]{:S(2)}, u32[]{:S(2)}) %collective-permute-start.32) | collective-permute-done | bytes 2097184 | tf_op jit(solution)/shard_map/ppermute | solution.py:49
  678.7 11.6 %attend_back_kernel.4 = (bf16[256,2048]{1,0:T(8,128)(2,1)S(1)}, f32[384,512]{1,0:T(8,128)S(1)}, f32[384,512]{1,0:T(8,128)S(1)}, f32[2,32,64,128]{3,2,1,0:T(8,128)}, f32[2,8,64,128]{3,2,1,0:T(8,128)S(1)}) custom-call(bf16[256,3072]{1,0:T(8,128)(2,1)} %rope.2.refs_0_, bf16[384,1024]{1,0:T(8,128)(2,1)S(1)} %bitcast.301, bf16[384,1024]{1,0:T(8,128)(2,1)S(1)} %bitcast.302, ...), custom_call_target="tpu_custom_call" | custom-call | flops 786432000 | bytes 4017152 | tf_op jit(solution)/shard_map/attend_back_kernel/pallas_call | solution.py:552
  702.0 12.0 %attend_back_kernel.5 = (bf16[256,2048]{1,0:T(8,128)(2,1)S(1)}, f32[384,512]{1,0:T(8,128)S(1)}, f32[384,512]{1,0:T(8,128)S(1)}, f32[2,32,64,128]{3,2,1,0:T(8,128)}, f32[2,8,64,128]{3,2,1,0:T(8,128)S(1)}) custom-call(bf16[256,3072]{1,0:T(8,128)(2,1)} %rope.2.refs_0_, ...), custom_call_target="tpu_custom_call", output_to_operand_aliasing={{0}: (12, {}), {1}: (13, {}), {2}: (14, {}), {3}: (15, {}),... | custom-call | flops 786432000 | bytes 4017152 | tf_op jit(solution)/shard_map/attend_back_kernel/pallas_call | solution.py:552
  730.8 17.9 %collective-permute-done.36 = bf16[2,8,80,128]{3,2,1,0:T(8,128)(2,1)} collective-permute-done((bf16[2,8,80,128]{3,2,1,0:T(8,128)(2,1)}, bf16[2,8,80,128]{3,2,1,0:T(8,128)(2,1)}, u32[]{:S(2)}, u32[]{:S(2)}) %collective-permute-start.36) | collective-permute-done | bytes 327712 | tf_op jit(solution)/shard_map/ppermute | solution.py:49
  765.7 12.3 %attend_back_kernel.6 = (bf16[256,2048]{1,0:T(8,128)(2,1)S(1)}, f32[384,512]{1,0:T(8,128)S(1)}, f32[384,512]{1,0:T(8,128)S(1)}, f32[2,32,64,128]{3,2,1,0:T(8,128)}, f32[2,8,64,128]{3,2,1,0:T(8,128)S(1)}) custom-call(bf16[256,3072]{1,0:T(8,128)(2,1)} %rope.2.refs_0_, ...), custom_call_target="tpu_custom_call", output_to_operand_aliasing={{0}: (12, {}), {1}: (13, {}), {2}: (14, {}), {3}: (15, {}),... | custom-call | flops 786432000 | bytes 4017152 | tf_op jit(solution)/shard_map/attend_back_kernel/pallas_call | solution.py:552
  786.7 11.6 %attend_back_kernel.7 = (bf16[256,2048]{1,0:T(8,128)(2,1)S(1)}, f32[384,512]{1,0:T(8,128)S(1)}, f32[384,512]{1,0:T(8,128)S(1)}, f32[2,32,64,128]{3,2,1,0:T(8,128)}, f32[2,8,64,128]{3,2,1,0:T(8,128)S(1)}) custom-call(bf16[256,3072]{1,0:T(8,128)(2,1)} %rope.2.refs_0_, ...), custom_call_target="tpu_custom_call", output_to_operand_aliasing={{0}: (12, {}), {1}: (13, {}), {2}: (14, {}), {3}: (15, {}),... | custom-call | flops 786432000 | bytes 4017152 | tf_op jit(solution)/shard_map/attend_back_kernel/pallas_call | solution.py:552
  912.9 12.5 %collective-permute-done.48 = bf16[512,2048]{1,0:T(8,128)(2,1)} collective-permute-done((bf16[512,2048]{1,0:T(8,128)(2,1)}, bf16[512,2048]{1,0:T(8,128)(2,1)}, u32[]{:S(2)}, u32[]{:S(2)}) %collective-permute-start.48) | collective-permute-done | bytes 2097184 | tf_op jit(solution)/shard_map/ppermute | solution.py:49
  935.9 13.4 %collective-permute-done.49 = bf16[512,1024]{1,0:T(8,128)(2,1)S(1)} collective-permute-done((bf16[512,1024]{1,0:T(8,128)(2,1)S(1)}, bf16[512,1024]{1,0:T(8,128)(2,1)S(1)}, u32[]{:S(2)}, u32[]{:S(2)}) %collective-permute-start.49) | collective-permute-done | bytes 1048608 | tf_op jit(solution)/shard_map/ppermute | solution.py:49
  (703 shorter events, 550.8 us)
Async XLA Ops:
  7.2 159.2 %all-gather.4.cloned.1.call-start = ((), (), s32[]{:S(2)}) async-start(), calls=%async_computation.1 | async-start | bytes 23396352 | tf_op jit(solution)/shard_map/all_gather | solution.py:747
  16.3 241.1 %all-gather.6.cloned.1.call-start = ((), (), s32[]{:S(2)}) async-start(), calls=%async_computation.2 | async-start | bytes 9437184 | tf_op jit(solution)/shard_map/all_gather | solution.py:821
  70.4 35.4 %collective-permute-start.2 = (bf16[64,4096]{1,0:T(8,128)(2,1)S(1)}, bf16[64,4096]{1,0:T(8,128)(2,1)S(1)}, u32[]{:S(2)}, u32[]{:S(2)}) collective-permute-start(bf16[64,4096]{1,0:T(8,128)(2,1)S(1)} %pad_maximum_fusion.10), channel_id=1, source_target_pairs={{0,8},{4,12},{8,0},{12,4},{1,9},{5,13},{9,1},{13,5},{2,10},{6,14},... | collective-permute-start | bytes 1572872 | tf_op jit(solution)/shard_map/ppermute | solution.py:49
  111.3 56.3 %collective-permute-start.4 = (bf16[4,2,64,2048]{3,2,1,0:T(8,128)(2,1)}, bf16[4,2,64,2048]{3,2,1,0:T(8,128)(2,1)}, u32[]{:S(2)}, u32[]{:S(2)}) collective-permute-start(bf16[4,2,64,2048]{3,2,1,0:T(8,128)(2,1)} %pad_maximum_fusion.near_ref), channel_id=1, source_target_pairs={{0,16},{16,0},{1,17},{17,1},{2,18},{18,2},{3,19},{19,3},{4,20},{20... | collective-permute-start | bytes 6291464 | tf_op jit(solution)/shard_map/ppermute | solution.py:49
  167.7 166.2 %all-gather.8.cloned.1.call-start = ((), (), s32[]{:S(2)}) async-start(), calls=%async_computation.3 | async-start | bytes 6291456 | tf_op jit(solution)/shard_map/all_gather | solution.py:823
  174.5 56.3 %collective-permute-start.6 = (bf16[4,2,64,2048]{3,2,1,0:T(8,128)(2,1)}, bf16[4,2,64,2048]{3,2,1,0:T(8,128)(2,1)}, u32[]{:S(2)}, u32[]{:S(2)}) collective-permute-start(bf16[4,2,64,2048]{3,2,1,0:T(8,128)(2,1)} %pad_maximum_fusion.near_ref), channel_id=1, source_target_pairs={{0,2},{2,0},{1,3},{3,1},{4,6},{6,4},{5,7},{7,5},{8,10},{10,8},{9,1... | collective-permute-start | bytes 6291464 | tf_op jit(solution)/shard_map/ppermute | solution.py:49
  257.5 525.9 %reduce-scatter.2.cloned.1.call-start = ((), (), s32[]{:S(2)}) async-start(), calls=%async_computation.4 | async-start | bytes 9437184 | tf_op jit(solution)/shard_map/reduce_scatter | solution.py:878
  276.1 47.0 %collective-permute-start.18 = (bf16[4,2,64,2048]{3,2,1,0:T(8,128)(2,1)}, bf16[4,2,64,2048]{3,2,1,0:T(8,128)(2,1)}, u32[]{:S(2)}, u32[]{:S(2)}) collective-permute-start(bf16[4,2,64,2048]{3,2,1,0:T(8,128)(2,1)} %collective-permute-done.6.far_ref), channel_id=1, source_target_pairs={{0,16},{16,0},{1,17},{17,1},{2,18},{18,2},{3,19},{19,3},{4,20},{20... | collective-permute-start | bytes 6291464 | tf_op jit(solution)/shard_map/ppermute | solution.py:49
  309.9 50.8 %collective-permute-start.12 = (bf16[256,2048]{1,0:T(8,128)(2,1)}, bf16[256,2048]{1,0:T(8,128)(2,1)S(1)}, u32[]{:S(2)}, u32[]{:S(2)}) collective-permute-start(bf16[256,2048]{1,0:T(8,128)(2,1)} %multiply_convert_fusion.own_ref), channel_id=1, source_target_pairs={{0,4},{4,0},{8,12},{12,8},{1,5},{5,1},{9,13},{13,9},{2,6},{6,2},{1... | collective-permute-start | bytes 3145736 | tf_op jit(solution)/shard_map/ppermute | solution.py:49
  362.8 49.1 %collective-permute-start.15 = (bf16[256,2048]{1,0:T(8,128)(2,1)}, bf16[256,2048]{1,0:T(8,128)(2,1)}, u32[]{:S(2)}, u32[]{:S(2)}) collective-permute-start(bf16[256,2048]{1,0:T(8,128)(2,1)} %collective-permute-done.13), channel_id=1, source_target_pairs={{4,0},{8,12},{5,1},{9,13},{6,2},{10,14},{7,3},{11,15},{20,16},{24,... | collective-permute-start | bytes 3145736 | tf_op jit(solution)/shard_map/ppermute | solution.py:49
  414.2 52.7 %collective-permute-start.16 = (bf16[256,2048]{1,0:T(8,128)(2,1)}, bf16[256,2048]{1,0:T(8,128)(2,1)S(1)}, u32[]{:S(2)}, u32[]{:S(2)}) collective-permute-start(bf16[256,2048]{1,0:T(8,128)(2,1)} %collective-permute-done.14), channel_id=1, source_target_pairs={{4,0},{8,12},{5,1},{9,13},{6,2},{10,14},{7,3},{11,15},{20,16},{24,... | collective-permute-start | bytes 3145736 | tf_op jit(solution)/shard_map/ppermute | solution.py:49
  499.8 29.5 %collective-permute-start.26 = (bf16[256,2048]{1,0:T(8,128)(2,1)S(1)}, bf16[256,2048]{1,0:T(8,128)(2,1)S(1)}, u32[]{:S(2)}, u32[]{:S(2)}) collective-permute-start(bf16[256,2048]{1,0:T(8,128)(2,1)S(1)} %add_convert_fusion.12), channel_id=1, source_target_pairs={{0,4},{12,8},{1,5},{13,9},{2,6},{14,10},{3,7},{15,11},{16,20},{28,... | collective-permute-start | bytes 3145736 | tf_op jit(solution)/shard_map/ppermute | solution.py:49
  558.9 27.1 %collective-permute-start.29 = (bf16[256,2048]{1,0:T(8,128)(2,1)S(1)}, bf16[256,2048]{1,0:T(8,128)(2,1)S(1)}, u32[]{:S(2)}, u32[]{:S(2)}) collective-permute-start(bf16[256,2048]{1,0:T(8,128)(2,1)S(1)} %add_convert_fusion.10), channel_id=1, source_target_pairs={{0,4},{4,0},{8,12},{12,8},{1,5},{5,1},{9,13},{13,9},{2,6},{6,2},{1... | collective-permute-start | bytes 3145736 | tf_op jit(solution)/shard_map/ppermute | solution.py:49
  618.2 83.8 %collective-permute-start.38 = (bf16[1024,2048]{1,0:T(8,128)(2,1)}, bf16[1024,2048]{1,0:T(8,128)(2,1)}, u32[]{:S(2)}, u32[]{:S(2)}) collective-permute-start(bf16[1024,2048]{1,0:T(8,128)(2,1)} %convolution_convert_fusion), channel_id=1, source_target_pairs={{0,1},{1,0},{2,3},{3,2},{4,5},{5,4},{6,7},{7,6},{8,9},{9,8},{10,11... | collective-permute-start | bytes 12582920 | tf_op jit(solution)/shard_map/ppermute | solution.py:49
  620.3 47.9 %collective-permute-start.32 = (bf16[16,64,1024]{2,1,0:T(8,128)(2,1)}, bf16[16,64,1024]{2,1,0:T(8,128)(2,1)}, u32[]{:S(2)}, u32[]{:S(2)}) collective-permute-start(bf16[16,64,1024]{2,1,0:T(8,128)(2,1)} %dynamic-slice_bitcast_fusion.2), channel_id=1, source_target_pairs={{0,16},{16,0},{1,17},{17,1},{2,18},{18,2},{3,19},{19,3},{4,20},{20... | collective-permute-start | bytes 6291464 | tf_op jit(solution)/shard_map/ppermute | solution.py:49
  677.2 79.9 %collective-permute-start.41 = (bf16[16,64,1024]{2,1,0:T(8,128)(2,1)}, bf16[16,64,1024]{2,1,0:T(8,128)(2,1)}, u32[]{:S(2)}, u32[]{:S(2)}) collective-permute-start(bf16[16,64,1024]{2,1,0:T(8,128)(2,1)} %dynamic-slice_bitcast_fusion.1), channel_id=1, source_target_pairs={{0,16},{16,0},{1,17},{17,1},{2,18},{18,2},{3,19},{19,3},{4,20},{20... | collective-permute-start | bytes 6291464 | tf_op jit(solution)/shard_map/ppermute | solution.py:49
  727.9 53.7 %collective-permute-start.42 = (bf16[512,2048]{1,0:T(8,128)(2,1)}, bf16[512,2048]{1,0:T(8,128)(2,1)}, u32[]{:S(2)}, u32[]{:S(2)}) collective-permute-start(bf16[512,2048]{1,0:T(8,128)(2,1)} %slice.290), channel_id=1, source_target_pairs={{0,2},{2,0},{1,3},{3,1},{4,6},{6,4},{5,7},{7,5},{8,10},{10,8},{9,1... | collective-permute-start | bytes 6291464 | tf_op jit(solution)/shard_map/ppermute | solution.py:49
  757.1 73.4 %collective-permute-start.47 = (bf16[2,256,2048]{2,1,0:T(8,128)(2,1)}, bf16[2,256,2048]{2,1,0:T(8,128)(2,1)}, u32[]{:S(2)}, u32[]{:S(2)}) collective-permute-start(bf16[2,256,2048]{2,1,0:T(8,128)(2,1)} %dynamic-slice_bitcast_fusion), channel_id=1, source_target_pairs={{0,16},{16,0},{1,17},{17,1},{2,18},{18,2},{3,19},{19,3},{4,20},{20... | collective-permute-start | bytes 6291464 | tf_op jit(solution)/shard_map/ppermute | solution.py:49
  781.6 34.5 %collective-permute-start.55 = (bf16[64,2048]{1,0:T(8,128)(2,1)}, bf16[64,2048]{1,0:T(8,128)(2,1)}, u32[]{:S(2)}, u32[]{:S(2)}) collective-permute-start(bf16[64,2048]{1,0:T(8,128)(2,1)} %get-tuple-element.349), channel_id=1, source_target_pairs={{0,8},{4,12},{8,0},{12,4},{1,9},{5,13},{9,1},{13,5},{2,10},{6,14},... | collective-permute-start | bytes 786440 | tf_op jit(solution)/shard_map/ppermute | solution.py:49
  781.6 34.5 %collective-permute-start.43 = (bf16[4,128,1024]{2,1,0:T(8,128)(2,1)}, bf16[4,128,1024]{2,1,0:T(8,128)(2,1)}, u32[]{:S(2)}, u32[]{:S(2)}) collective-permute-start(bf16[4,128,1024]{2,1,0:T(8,128)(2,1)} %dynamic-slice_bitcast_fusion.5), channel_id=1, source_target_pairs={{0,2},{2,0},{1,3},{3,1},{4,6},{6,4},{5,7},{7,5},{8,10},{10,8},{9,1... | collective-permute-start | bytes 3145736 | tf_op jit(solution)/shard_map/ppermute | solution.py:49
  814.8 44.8 %collective-permute-start.40 = (bf16[1024,2048]{1,0:T(8,128)(2,1)}, bf16[1024,2048]{1,0:T(8,128)(2,1)}, u32[]{:S(2)}, u32[]{:S(2)}) collective-permute-start(bf16[1024,2048]{1,0:T(8,128)(2,1)} %convolution_convert_fusion.1), channel_id=1, source_target_pairs={{0,1},{1,0},{2,3},{3,2},{4,5},{5,4},{6,7},{7,6},{8,9},{9,8},{10,11... | collective-permute-start | bytes 12582920 | tf_op jit(solution)/shard_map/ppermute | solution.py:49
  866.9 40.9 %collective-permute-start.45 = (bf16[1024,1024]{1,0:T(8,128)(2,1)}, bf16[1024,1024]{1,0:T(8,128)(2,1)}, u32[]{:S(2)}, u32[]{:S(2)}) collective-permute-start(bf16[1024,1024]{1,0:T(8,128)(2,1)} %convolution_convert_fusion.7), channel_id=1, source_target_pairs={{0,1},{1,0},{2,3},{3,2},{4,5},{5,4},{6,7},{7,6},{8,9},{9,8},{10,11... | collective-permute-start | bytes 6291464 | tf_op jit(solution)/shard_map/ppermute | solution.py:49
  877.9 47.6 %collective-permute-start.48 = (bf16[512,2048]{1,0:T(8,128)(2,1)}, bf16[512,2048]{1,0:T(8,128)(2,1)}, u32[]{:S(2)}, u32[]{:S(2)}) collective-permute-start(bf16[512,2048]{1,0:T(8,128)(2,1)} %slice.233), channel_id=1, source_target_pairs={{0,2},{2,0},{1,3},{3,1},{4,6},{6,4},{5,7},{7,5},{8,10},{10,8},{9,1... | collective-permute-start | bytes 6291464 | tf_op jit(solution)/shard_map/ppermute | solution.py:49
  906.6 28.1 %collective-permute-start.61 = (bf16[64,2048]{1,0:T(8,128)(2,1)S(1)}, bf16[64,2048]{1,0:T(8,128)(2,1)S(1)}, u32[]{:S(2)}, u32[]{:S(2)}) collective-permute-start(bf16[64,2048]{1,0:T(8,128)(2,1)S(1)} %copy-done.105), channel_id=1, source_target_pairs={{0,8},{4,12},{8,0},{12,4},{1,9},{5,13},{9,1},{13,5},{2,10},{6,14},... | collective-permute-start | bytes 786440 | tf_op jit(solution)/shard_map/ppermute | solution.py:49
  (202 other events, 2483.1 us)
Sparse Core Ops, SparseCore 0:
  16.5 149.8 all-gather.3
  167.9 89.4 all-gather.5
  259.0 57.8 all-gather.7
  589.2 92.7 reduce-scatter.1

commit v3 on v2

--- a/solution.py
+++ b/solution.py
@@ -77,9 +77,9 @@
         third_end = self.move(third, "z", ends_out, ("outer",))
         return [
             block,
-            first,
-            lambda: jnp.where(inner, second, second_end),
-            lambda: jnp.where(inner, third, third_end),
+            lambda *late: after(first, second),
+            lambda *late: after(jnp.where(inner, second, second_end), third),
+            lambda *late: jnp.where(inner, third, third_end),
         ]
 
     def line_scatter(self, parts, hold=()):
@@ -192,22 +192,31 @@
     return jnp.stack([jnp.where(c == 0, mine, theirs), jnp.where(c == 0, theirs, mine)], axis=1)
 
 
-def join_gate_up(near, far, near_other, far_other):
+def join_gate_up(near, near_other, far, far_other):
     nz = lax.axis_size("z")
     z, x, y = lax.axis_index("z"), lax.axis_index("x"), lax.axis_index("r")
     rows, wide = near.shape[2:]
-
-    def body(at_ref, near_ref, far_ref, near_o_ref, far_o_ref, out_ref):
-        h, d = at_ref[2], pl.program_id(1)
-        for where, mine, other in ((0, near_ref, near_o_ref), (1, far_ref, far_o_ref)):
-
-            @pl.when(d == where)
+    half = nz // 2
+
+    def body(at_ref, *refs):
+        out_ref, h = refs[-1], at_ref[2]
+        k, d = pl.program_id(0), pl.program_id(1)
+        cases = [(d == 0, refs[0], refs[1])]
+        cases += [((d == 1) & (k // half == i), refs[2 + i], refs[4 + i]) for i in range(2)]
+        for case, mine, other in cases:
+
+            @pl.when(case)
             def _():
                 for c in range(2):
                     out_ref[0, 0, c, pl.ds(h, 1)] = mine[0, c][None]
                     out_ref[0, 0, c, pl.ds(1 - h, 1)] = other[0, c][None]
 
-    block = pl.BlockSpec((1, 2, rows, wide), lambda k, d, at: (k, 0, 0, 0))
+    shape = (1, 2, rows, wide)
+    block = pl.BlockSpec(shape, lambda k, d, at: (k, 0, 0, 0))
+    pieces = [
+        pl.BlockSpec(shape, lambda k, d, at, i=i: (jnp.clip(k - i * half, 0, half - 1), 0, 0, 0))
+        for i in range(2)
+    ]
     place = lambda k, d, at: (lax.rem(at[0] - k + nz, nz), at[1] ^ d, 0, 0, 0, 0)
     out = pl.pallas_call(
         body,
@@ -215,14 +224,14 @@
         grid_spec=pltpu.PrefetchScalarGridSpec(
             num_scalar_prefetch=1,
             grid=(nz, 2),
-            in_specs=[block] * 4,
+            in_specs=[block, block] + pieces + pieces,
             out_specs=pl.BlockSpec((1, 1, 2, 2, rows, wide), place),
         ),
         cost_estimate=pl.CostEstimate(
             flops=0, bytes_accessed=16 * near.size, transcendentals=0
         ),
         name="join_gate_up",
-    )(jnp.stack([z, x, y]).astype(jnp.int32), near, far, near_other, far_other)
+    )(jnp.stack([z, x, y]).astype(jnp.int32), near, near_other, *far, *far_other)
     return out.reshape(-1, wide)
 
 
@@ -240,49 +249,35 @@
 
 
 def whole_rows(halves):
-    rows, cols = halves[0][0].shape
-    wide = min(cols, 2048)
-    tiles = cols // wide
-
-    def body(at_ref, *refs):
-        out_ref, g, h = refs[-1], pl.program_id(0), at_ref[0]
-        for i in range(len(halves)):
-
-            @pl.when(g == i)
-            def _():
-                out_ref[pl.ds(h, 1)] = refs[2 * i][...].astype(f32)[None]
-                out_ref[pl.ds(1 - h, 1)] = refs[2 * i + 1][...].astype(f32)[None]
-
-    def block(i):
-        return pl.BlockSpec(
-            (rows, wide), lambda g, j, at: (0, jnp.where(g == i, j, jnp.where(g < i, 0, tiles - 1)))
-        )
+    nz = lax.axis_size("z")
+    rows, cols = halves.shape[1:]
+    wide = cols // (4 * nz)
+
+    def body(in_ref, out_ref):
+        out_ref[...] = in_ref[...].astype(f32)
 
     out = pl.pallas_call(
         body,
-        out_shape=jax.ShapeDtypeStruct((2, rows, len(halves) * cols), f32),
-        grid_spec=pltpu.PrefetchScalarGridSpec(
-            num_scalar_prefetch=1,
-            grid=(len(halves), tiles),
-            in_specs=[block(i) for i in range(len(halves)) for _ in range(2)],
-            out_specs=pl.BlockSpec((2, rows, wide), lambda g, j, at: (0, 0, g * tiles + j)),
-        ),
+        out_shape=jax.ShapeDtypeStruct(halves.shape, f32),
+        grid=(2, 2 * nz),
+        in_specs=[pl.BlockSpec((2, rows, wide), lambda g, j: (0, 0, 2 * j + g))],
+        out_specs=pl.BlockSpec((2, rows, wide), lambda g, j: (0, 0, g * 2 * nz + j)),
         cost_estimate=pl.CostEstimate(
-            flops=0, bytes_accessed=12 * len(halves) * rows * cols, transcendentals=0
+            flops=0, bytes_accessed=12 * rows * cols, transcendentals=0
         ),
         name="whole_rows",
-    )(lax.axis_index("r").astype(jnp.int32)[None], *[a for pair in halves for a in pair])
-    return out.reshape(2 * rows, -1)
+    )(halves)
+    return out.reshape(2 * rows, cols)
 
 
 def split_core(links, t, *late):
     c = lax.axis_index("c")
     t = t.reshape(t.shape[0], 2, -1, t.shape[2])
-    loc = t.shape[3] // 2
+    loc = FF // (4 * lax.axis_size("z"))
     mine, theirs = pick(t, c, 1), after(links.swap(pick(t, 1 - c, 1), "c"), *late)
     first, second = jnp.where(c == 0, mine, theirs), jnp.where(c == 0, theirs, mine)
     pieces = []
-    for j in range(2):
+    for j in range(t.shape[3] // loc):
         pieces += [first[:, :, j * loc : (j + 1) * loc], second[:, :, j * loc : (j + 1) * loc]]
     return jnp.concatenate(pieces, axis=2)
 
@@ -570,7 +565,7 @@
 
 
 def ffn_kernel(at_ref, own_ref, other_ref, pair_ref, w_ref, wd_ref, *refs):
-    act_ref, dg_ref, du_ref, n2_ref, df_ref, mine_ref, theirs_ref, out_ref, dn_acc, out_acc = refs[-10:]
+    act_ref, dgu_ref, n2_ref, df_ref, mine_ref, theirs_ref, out_ref, dn_acc, out_acc = refs[-9:]
     f, rows, width = pl.program_id(0), own_ref.shape[0], wd_ref.shape[0]
     here = pl.ds(pl.multiple_of(at_ref[1] * rows, rows), rows)
     there = pl.ds(pl.multiple_of((1 - at_ref[1]) * rows, rows), rows)
@@ -591,9 +586,9 @@
     d_gate = (d_act * up * (sig * (1.0 + gate * (1.0 - sig)))).astype(bf16)
     d_up = (d_act * swish).astype(bf16)
     act_ref[...] = acted
-    dg_ref[...] = d_gate
-    du_ref[...] = d_up
-    d_n2 = mm_t(jnp.concatenate([d_gate, d_up], axis=1), w_ref[...])
+    d_gu = jnp.concatenate([d_gate, d_up], axis=1)
+    dgu_ref[...] = d_gu
+    d_n2 = mm_t(d_gu, w_ref[...])
     out = mm(acted, wd_ref[...])
 
     @pl.when(f == 0)
@@ -624,7 +619,7 @@
     hidden = pl.BlockSpec((2 * rows, width), lambda f, a: (k, f))
     pair = pl.BlockSpec((1, 2, rows, D), lambda f, a: (a[0], 0, 0, 0))
     whole = (total, D)
-    outs = [((total, half), bf16)] * 3 + [(whole, bf16)] * 2
+    outs = [((total, half), bf16), ((total, 2 * half), bf16)] + [(whole, bf16)] * 2
     outs += [((rows, D), f32), ((rows, D), bf16), (df_all.shape, bf16)]
     return pl.pallas_call(
         ffn_kernel,
@@ -641,12 +636,13 @@
             ]
             + [pl.BlockSpec(memory_space=pl.ANY)] * len(held),
             out_specs=(
-                hidden, hidden, hidden, chunk, chunk, tokens, tokens,
+                hidden, pl.BlockSpec((2 * rows, 2 * width), lambda f, a: (k, f)), chunk, chunk,
+                tokens, tokens,
                 pair,
             ),
             scratch_shapes=[pltpu.VMEM((2 * rows, D), f32)] * 2,
         ),
-        input_output_aliases={6 + i: (i if i < 5 else 7) for i in range(len(held))},
+        input_output_aliases={6 + i: (i if i < 4 else 6) for i in range(len(held))},
         compiler_params=pltpu.CompilerParams(vmem_limit_bytes=56 << 20),
         cost_estimate=pl.CostEstimate(
             flops=24 * rows * D * half,
@@ -754,7 +750,7 @@
     wgu_near = core_columns(links, line_columns(links, wgu_half))
     wgu_near_other = links.swap(wgu_near, "r")
     small, wgu_send = lax.optimization_barrier((small, wgu_near, wgu_near_other))[:2]
-    wgu_far = links.swap(wgu_send, "x")
+    wgu_far = [links.swap(wgu_send[: nz // 2], "x")]
     gain_one = small[:, 0].astype(f32)[None]
     adown = small[:, 1:25]
     odown = small[:, 25:33]
@@ -810,7 +806,8 @@
     projected = mm(n1, wqkv) + SCALE * mm(adapt, aup_wide)
     qkv = rope(projected, cosine, sine, 5)
     kv = qkv[:, D:].reshape(micros, rows, 2 * KVW)
-    halo = lax.ppermute(kv[:, rows - WINDOW :], *chain)
+    crossing = ("x", "outer", "middle", "c")
+    halo = links.move(kv[:, rows - WINDOW :], *chain, crossing)
     kv_ext = jnp.concatenate([halo, kv], axis=1).reshape(micros * extent, 2 * KVW)
     launch = lambda kernel, ins, outs, args, work, **k: call(
         kernel, micros, rows, extent, ins, outs, args, micros * HEADS * rows * work, **k
@@ -820,12 +817,11 @@
     )
     df_all = lax.all_gather(after(cot, small), ("z", "c"), axis=0, tiled=True)
     df_all = df_all.reshape(nz, 2, both, D)
-    wd = lax.all_gather(after(wd_own, df_all), "x", axis=0, tiled=True)
     parts = [(m, j, 2) for m in range(micros) for j in (0, 2)]
     travel = entering(links, add, tags, reach)
     next(travel)
-    wgu_far, wk2_late = lax.optimization_barrier((wgu_far, wk2, add))[:2]
-    wgu_far_other = links.swap(wgu_far, "r")
+    wgu_far[0], wk2_late = lax.optimization_barrier((wgu_far[0], wk2, add))[:2]
+    wgu_far_other = [links.swap(wgu_far[0], "r")]
     local = ()
     for i, part in enumerate(parts):
         local = launch(
@@ -837,10 +833,18 @@
             only=part,
             into=local,
         )
-        if i < 2:
+        if i == 0:
             travel.send(local[1])
+            wgu_far.append(links.swap(wgu_near[nz // 2 :], "x"))
+            wd_other = links.swap(wd_own, "x")
+        elif i == 1:
+            travel.send(local[1])
+        elif i == 2:
+            state = travel.send(local[1])
+            wk2_late = after(wk2_late, state)
     nd, phi = local
-    state = travel.send(phi)
+    wgu_far[1], nd = lax.optimization_barrier((wgu_far[1], nd, wgu_far_other[0]))[:2]
+    wgu_far_other.append(links.swap(wgu_far[1], "r"))
     nd, attn = launch(
         finish_kernel,
         ("nd", "nd", "st", "row"),
@@ -857,7 +861,10 @@
     loc = half // 2
     n2_parts = links.line_gather(n2)
     late = lambda a: after(a, attn)
-    wgu = join_gate_up(late(wgu_near), wgu_far, late(wgu_near_other), late(wgu_far_other))
+    wgu = join_gate_up(*[late(a) for a in (wgu_near, wgu_near_other)], wgu_far, [late(a) for a in wgu_far_other])
+    wd = jnp.concatenate(
+        [jnp.where(x == 0, wd_own, wd_other), jnp.where(x == 0, wd_other, wd_own)], axis=0
+    )
     returned, held = [], ()
     for i, (place, part) in enumerate(zip(links.slots(), n2_parts)):
         at = jnp.stack([place, c]).astype(jnp.int32)
@@ -865,33 +872,28 @@
         if i:
             part = after(part, held[0])
         result = ffn_chunk(i, at, part, links.swap(part, "c"), df_all, wgu, wd, held)
-        held = result[:5] + result[7:]
-        d_n2_i = result[5] + links.swap(result[6], "c").astype(f32)
+        held = result[:4] + result[6:]
+        d_n2_i = result[4] + links.swap(result[5], "c").astype(f32)
         returned.append(d_n2_i.astype(bf16) if i else d_n2_i)
-    acted, d_gate, d_up, n2_all, df_held, out_parts = held
+    acted, d_gu, n2_all, df_held, out_parts = held
     d_n2 = links.line_scatter(returned)
-    g_gate = t_mm(n2_all, d_gate).astype(bf16)
-    g_up = t_mm(n2_all, d_up).astype(bf16)
+    g_wgu = t_mm(n2_all, d_gu).astype(bf16)
     g_wd = t_mm(acted, df_held).astype(bf16)
-    d_n2 = after(d_n2, g_gate, g_up, g_wd)
+    d_n2 = after(d_n2, g_wgu, g_wd)
     plus = lambda a, b: (a.astype(f32) + b.astype(f32)).astype(bf16)
+
+    def replica_sum(g):
+        halves = g.reshape(g.shape[0], 2, -1, g.shape[2]).transpose(1, 0, 2, 3)
+        return lax.psum_scatter(halves, "r", scatter_dimension=0, tiled=False)
+
+    def x_parts(t):
+        return pick(t, x, 1), pick(t, 1 - x, 1)
+
+    g_wgu = replica_sum(g_wgu.reshape(n, r, 2 * half))
     out_sum = lax.psum_scatter(
         after(out_parts, d_n2).reshape(-1, D), ("z", "c"), scatter_dimension=0, tiled=True
     )
-    g_gate, g_up = g_gate.reshape(n, r, half), g_up.reshape(n, r, half)
-    g_wd = g_wd.reshape(2, loc, D)
-    gu_mine, gu_other = [], []
-    for g in (g_gate, g_up, g_wd):
-        mine, theirs = split_replica(g)
-        gu_mine.append(mine)
-        gu_other.append(links.swap(theirs, "r"))
-
-    def replica_sum(i, *late):
-        return (gu_mine[i].astype(f32) + after(gu_other[i], *late).astype(f32)).astype(bf16)
-
-    def x_parts(t):
-        t = t.reshape(-1, 2, t.shape[-2] * (2 if t.shape[0] == n else 1), t.shape[-1])
-        return pick(t, x, 1), pick(t, 1 - x, 1)
+    g_wd = replica_sum(after(g_wd, out_sum).reshape(2, loc, D))
 
     d_hidden = (
         cot.astype(f32)
@@ -909,8 +911,6 @@
         32768,
     )
     attn_owner, n1_owner = by_owner(attn), by_owner(n1)
-    gate_mine, gate_theirs = x_parts(replica_sum(0, d_attn))
-    gate_side = links.swap(gate_theirs, "x")
     travel = leaving(links, dst, tags, reach)
     next(travel)
     wout_core = core_product(links, *attn_owner, d_branch)
@@ -930,17 +930,16 @@
         done = grads[0]
         if i == 0:
             travel.send(done)
+            gu_mine, gu_theirs = x_parts(after(g_wgu, done).reshape(nz, 2, r, 2 * half))
+            gu_side = links.swap(gu_theirs, "x")
             wout_x = scatter_x(links, wout_core(done))
-            gate_rows = split_core(links, plus(gate_mine, after(gate_side, done)))
         elif i == 1:
             travel.send(done)
-            gate_line = split_line(links, gate_rows)
-            up_mine, up_theirs = x_parts(replica_sum(1, done))
-            up_side = links.swap(up_theirs, "x")
         elif i == 2:
-            d_attn_late = after(d_attn_late, out_sum)
+            dadd = travel.send(done)
+            d_attn_late = after(d_attn_late, dadd, out_sum)
     dq, dk, dv, dwq, dwk = grads
-    dadd = travel.send(dq)
+    gu_rows = split_core(links, plus(gu_mine, after(gu_side, dq)))
     wout_line = scatter_line(links, wout_x(dq))
     q_core = core_product(links, *n1_owner, dq)
     dk, dv, dwk_more = launch(
@@ -951,22 +950,15 @@
         16384,
     )
     d_kv = jnp.concatenate([dk, dv], axis=1).reshape(micros, extent, 2 * KVW)
-    sent = lax.ppermute(d_kv[:, :WINDOW].astype(bf16), *unchain)
-    gate_half = join_line([after(p, dk) for p in gate_line])
-    gate_far = links.swap(gate_half, "r")
-    q_sum, up_rows = lax.optimization_barrier(
-        (q_core(dadd), plus(up_mine, after(up_side, dadd)), sent)
-    )[:2]
+    sent = links.move(d_kv[:, :WINDOW].astype(bf16), *unchain, crossing)
+    q_sum, gu_rows, sent = lax.optimization_barrier((q_core(dadd), gu_rows, sent))
     q_x = scatter_x(links, q_sum)
+    gu_line = split_line(links, gu_rows)
     wout_line = wout_line(dadd, sent)
-    up_line = split_line(links, split_core(links, up_rows))
     sent = sent.astype(f32)
     d_kv = jnp.concatenate([d_kv[:, WINDOW:rows], d_kv[:, rows:] + sent], axis=1)
     d_kv = rope(d_kv.reshape(both, 2 * KVW), cosine, -sine, 1)
     kv_sum = core_product(links, *n1_owner, d_kv)()
-    kv_x = scatter_x(links, kv_sum)
-    wd_mine, wd_theirs = x_parts(replica_sum(2, kv_sum))
-    wd_side = links.swap(wd_theirs, "x")
     d_proj = jnp.concatenate([dq, d_kv], axis=1)
     d_adapt = (SCALE * mm_t(d_proj, aup_wide)).astype(bf16)
     d_n1 = mm_t(d_proj, wqkv) + mm_t(d_adapt, adown)
@@ -997,28 +989,28 @@
     nat = g_pack.reshape(nz, 2, 2, r, PACK)
     mine, theirs = pick(nat, c, 2), pick(nat, 1 - c, 2)
     nat = plus(mine, links.swap(theirs, "c"))
-    mine, theirs = pick(nat, x, 1), pick(nat, 1 - x, 1)
-    pack_side = links.swap(theirs, "x")
-    wout_line = wout_line(theirs)
-    q_line = scatter_line(links, q_x(theirs))
-    kv_line = scatter_line(links, kv_x(theirs))
-    wd_half = plus(wd_mine, after(wd_side, theirs)).reshape(-1, D)
-    nat = plus(mine, pack_side)
-    nat = jnp.concatenate([pick(nat, lax.rem(z - k + nz, nz), 0) for k in range(nz)], axis=0)
+    nat = jnp.concatenate(
+        [pick(pick(nat, x ^ dx, 1), lax.rem(z - k + nz, nz), 0) for dx in range(2) for k in range(nz)],
+        axis=0,
+    )
+    kv_x = scatter_x(links, jnp.concatenate([kv_sum, nat], axis=1))
+    wd_mine, wd_theirs = x_parts(after(g_wd, nat)[None])
+    wd_side = links.swap(wd_theirs[0], "x")
+    q_line = scatter_line(links, q_x(nat))
+    gu_half = join_line([after(p, nat) for p in gu_line])
+    gu_both = lax.all_gather(gu_half, "r", axis=0)
+    wout_line = wout_line(nat)
+    kv_line = scatter_line(links, kv_x(nat))
     q_line = q_line()
-    up_half = join_line([after(p, theirs) for p in up_line])
-    up_far = links.swap(up_half, "r")
+    wd_both = lax.all_gather(plus(wd_mine[0], wd_side), "r", axis=0, tiled=True)
     kv_line = kv_line()
-    pack_line = scatter_line(links, nat)
-    wd_far = links.swap(wd_half, "r")
-    pack_line = pack_line()
     output = (hidden + after(out_sum, nat).astype(f32)).astype(bf16)
-    q_line, kv_line, pack_line = q_line(), kv_line(), pack_line()
-    g_small = pack_line()
-    g_wout_own = wout_line()
-    g_wd_own = join_replica(wd_half, wd_far)
-    g_wgu_own = whole_rows([(gate_half, gate_far), (up_half, up_far)])
-    g_wqkv_own = jnp.concatenate([q_line(), kv_line()], axis=1)
+    q_line, kv_line = q_line(), kv_line()
+    g_wout_own, g_q_own, g_kv_own = wout_line(), q_line(), kv_line()
+    g_small = g_kv_own[:, 2 * KVW :]
+    g_wd_own = wd_both.astype(f32)
+    g_wgu_own = whole_rows(gu_both)
+    g_wqkv_own = jnp.concatenate([g_q_own, g_kv_own[:, : 2 * KVW]], axis=1)
     return (
         output.reshape(1, micros, rows, D),
         grad_inputs.reshape(1, micros, rows, D),

time: 1070 us -> 1030 us (0.963)
  waiting for transfers between devices: 438 us -> 365 us
  local copies, waits for them, and re-layouts: 83.6 us -> 104 us
    ppermute x78 -> x66, waiting for transfers between devices: 375 us -> 308 us  [move(): out = lax.ppermute(a, axis, pairs)]
    ppermute x78 -> x66, starting transfers between devices: 109 us -> 127 us  [move(): out = lax.ppermute(a, axis, pairs)]
    ppermute x2 -> x0, starting transfers between devices: 13.2 us -> none  [the longest x1 11.7 us: per_device(): halo = lax.ppermute(kv[:, rows - WINDOW:], *chain)]
    another operation x5, local copies, waits for them, and re-layouts: 4.71 us -> 16 us  [the longest x2 13 us: replica_sum(): halves = g.reshape(g.shape[0], 2, -1, g.shape[2]).transpose(1, 0, 2, 3)]
    unnamed x302 -> x328, local copies, waits for them, and re-layouts: 28.7 us -> 38.1 us
    dot_general x13 -> x12, matrix products: 54.1 us -> 55.9 us  [t_mm(): lax.dot_general(a, b, (((0,), (0,)), ((), ())), preferred_element_type=f32)]
  transfers between devices with their start and end apart: 85 -> 74, of which waited for: 46 -> 38; matrix products, arithmetic and copies ran while one was open for 20% -> 21% of each run, Pallas kernels for 19% -> 20%
where the time goes in v3:
time: 1030 us; the launch traced here: 1020 us
  waiting for transfers between devices  365 us (35%)
  Pallas kernels  226 us (22%)
  starting transfers between devices  129 us (13%)
  local copies, waits for them, and re-layouts  104 us (10%)
  other arithmetic  92.9 us (9%)
  matrix products  88.8 us (9%)
  between operations  17.1 us (2%)
    ppermute x66, waiting for transfers between devices, move(): out = lax.ppermute(a, axis, pairs)  308 us
    ppermute x66, starting transfers between devices, move(): out = lax.ppermute(a, axis, pairs)  127 us
    pallas_call x4, Pallas kernels, ffn_chunk(): pl.pallas_call(ffn_kernel, out_shape=tuple((jax.ShapeDtypeStruct(a, b) fo...  99.3 us
    pallas_call x12, Pallas kernels, call(): pl.pallas_call(body, out_shape=out_shape, grid=(count, pairs), in_specs=[...  97.9 us
    dot_general x12, matrix products, t_mm(): lax.dot_general(a, b, (((0,), (0,)), ((), ())), preferred_element_type=f32)  55.9 us
    all_gather x1, waiting for transfers between devices, per_device(): lax.all_gather(jnp.concatenate([wqkv_own, wout_own, pack], axis=1), every...  53.3 us
    unnamed x328, local copies, waits for them, and re-layouts  38.1 us
  transfers between devices with their start and end apart: 74, of which 38 were waited for; matrix products, arithmetic and copies ran while one was open for 21% of the time, Pallas kernels for 20%

profile of v3, /device:TPU:0, one launch (start us, length us, event | category | flops | bytes accessed | tf_op | source)
XLA Modules:
  0.0 1022.9 jit_solution(11331917289611150116)
XLA Ops:
  22.6 21.6 %collective-permute-done = bf16[64,4096]{1,0:T(8,128)(2,1)S(1)} collective-permute-done((bf16[64,4096]{1,0:T(8,128)(2,1)S(1)}, bf16[64,4096]{1,0:T(8,128)(2,1)S(1)}, u32[]{:S(2)}, u32[]{:S(2)}) %collective-permute-start) | collective-permute-done | bytes 524320 | tf_op jit(solution)/shard_map/ppermute | solution.py:49
  47.5 22.9 %collective-permute-done.1 = bf16[64,4096]{1,0:T(8,128)(2,1)S(1)} collective-permute-done((bf16[64,4096]{1,0:T(8,128)(2,1)S(1)}, bf16[64,4096]{1,0:T(8,128)(2,1)S(1)}, u32[]{:S(2)}, u32[]{:S(2)}) %collective-permute-start.1) | collective-permute-done | bytes 524320 | tf_op jit(solution)/shard_map/ppermute | solution.py:49
  71.4 34.3 %collective-permute-done.2 = bf16[64,4096]{1,0:T(8,128)(2,1)S(1)} collective-permute-done((bf16[64,4096]{1,0:T(8,128)(2,1)S(1)}, bf16[64,4096]{1,0:T(8,128)(2,1)S(1)}, u32[]{:S(2)}, u32[]{:S(2)}) %collective-permute-start.2) | collective-permute-done | bytes 524320 | tf_op jit(solution)/shard_map/ppermute | solution.py:49
  113.0 53.3 %all-gather.5.cloned.1.call-done = bf16[2048,5376]{1,0:T(8,128)(2,1)} async-done(((bf16[128,5376]{1,0:T(8,128)(2,1)}), bf16[2048,5376]{1,0:T(8,128)(2,1)}) %all-gather.5.cloned.1.call-update) | async-done | bytes 22020112 | tf_op jit(solution)/shard_map/all_gather | solution.py:743
  196.5 11.2 %collective-permute-start.6 = (bf16[2,64,1024]{2,1,0:T(8,128)(2,1)}, bf16[2,64,1024]{2,1,0:T(8,128)(2,1)S(1)}, u32[]{:S(2)}, u32[]{:S(2)}) collective-permute-start(bf16[2,64,1024]{2,1,0:T(8,128)(2,1)} %slice.281), channel_id=1, source_target_pairs={{0,1},{1,2},{2,3},{3,4},{4,5},{5,6},{6,7},{7,8},{8,9},{9,10},{10,1... | collective-permute-start | bytes 786440 | tf_op jit(solution)/shard_map/ppermute | solution.py:49
  221.9 13.9 %collective-permute-start.9 = (bf16[2,8,80,128]{3,2,1,0:T(8,128)(2,1)S(1)}, bf16[2,8,80,128]{3,2,1,0:T(8,128)(2,1)S(1)}, u32[]{:S(2)}, u32[]{:S(2)}) collective-permute-start(bf16[2,8,80,128]{3,2,1,0:T(8,128)(2,1)S(1)} %fusion.36), channel_id=1, source_target_pairs={{0,2},{2,0},{1,3},{3,1},{4,6},{6,4},{5,7},{7,5},{8,10},{10,8},{9,1... | collective-permute-start | bytes 983048 | tf_op jit(solution)/shard_map/ppermute | solution.py:49
  312.6 10.7 %join_gate_up.1 = bf16[4,2,2,2,64,2048]{5,4,3,2,1,0:T(8,128)(2,1)} custom-call(s32[3]{0:T(128)} %pad_add_fusion.4.at_ref, bf16[4,2,64,2048]{3,2,1,0:T(8,128)(2,1)} %pad_maximum_fusion.1.refs_0_, bf16[4,2,64,2048]{3,2,1,0:T(8,128)(2,1)} %collective-permute-done.4.refs_1_, bf16[2,2,64,2048]{3,2,1,0:T(8,128)(2,1)} %collective-permute-done.5.refs_2_, ...), custom_call_target="tpu_custom_call" | custom-call | bytes 16777216 | tf_op jit(solution)/shard_map/join_gate_up/pallas_call | solution.py:221
  334.1 24.7 %ffn_chunk.4 = (bf16[2048,1024]{1,0:T(8,128)(2,1)}, bf16[2048,2048]{1,0:T(8,128)(2,1)}, bf16[2048,2048]{1,0:T(8,128)(2,1)}, bf16[2048,2048]{1,0:T(8,128)(2,1)}, ...) custom-call(s32[2]{0:T(128)} %pad_add_fusion.3.at_ref, ...), custom_call_target="tpu_custom_call" | custom-call | flops 12884901888 | bytes 33554432 | tf_op jit(solution)/shard_map/ffn_chunk/pallas_call | solution.py:624
  365.8 24.7 %ffn_chunk.5 = (bf16[2048,1024]{1,0:T(8,128)(2,1)}, bf16[2048,2048]{1,0:T(8,128)(2,1)}, bf16[2048,2048]{1,0:T(8,128)(2,1)}, bf16[2048,2048]{1,0:T(8,128)(2,1)}, ...) custom-call(s32[2]{0:T(128)} %pad_add_fusion.2.at_ref, ...), custom_call_target="tpu_custom_call", output_to_operand_aliasing={{0}: (6, {}), {1}: (7, {}), {2}: (8, {}), {3}: (9, {}), {6}... | custom-call | flops 12884901888 | bytes 33554432 | tf_op jit(solution)/shard_map/ffn_chunk/pallas_call | solution.py:624
  402.5 24.7 %ffn_chunk.6 = (bf16[2048,1024]{1,0:T(8,128)(2,1)}, bf16[2048,2048]{1,0:T(8,128)(2,1)}, bf16[2048,2048]{1,0:T(8,128)(2,1)}, bf16[2048,2048]{1,0:T(8,128)(2,1)}, ...) custom-call(s32[2]{0:T(128)} %pad_add_fusion.1.at_ref, ...), custom_call_target="tpu_custom_call", output_to_operand_aliasing={{0}: (6, {}), {1}: (7, {}), {2}: (8, {}), {3}: (9, {}), {6}... | custom-call | flops 12884901888 | bytes 33554432 | tf_op jit(solution)/shard_map/ffn_chunk/pallas_call | solution.py:624
  433.3 25.1 %ffn_chunk.7 = (bf16[2048,1024]{1,0:T(8,128)(2,1)}, bf16[2048,2048]{1,0:T(8,128)(2,1)}, bf16[2048,2048]{1,0:T(8,128)(2,1)}, bf16[2048,2048]{1,0:T(8,128)(2,1)}, ...) custom-call(s32[2]{0:T(128)} %pad_add_fusion.at_ref, ...), custom_call_target="tpu_custom_call", output_to_operand_aliasing={{0}: (6, {}), {1}: (7, {}), {2}: (8, {}), {3}: (9, {}), {6}... | custom-call | flops 12884901888 | bytes 33554432 | tf_op jit(solution)/shard_map/ffn_chunk/pallas_call | solution.py:624
  458.4 23.8 %convolution_convert_fusion = bf16[2048,2048]{1,0:T(8,128)(2,1)} fusion(bf16[2048,2048]{1,0:T(8,128)(2,1)} %get-tuple-element.265, bf16[2048,2048]{1,0:T(8,128)(2,1)} %get-tuple-element.266), kind=kOutput, calls=%fused_computation.7 | convolution fusion | flops 17184063488 | bytes 25165824 | tf_op jit(solution)/shard_map/dot_general | solution.py:37
  500.2 22.9 %collective-permute-done.29 = bf16[256,2048]{1,0:T(8,128)(2,1)S(1)} collective-permute-done((bf16[256,2048]{1,0:T(8,128)(2,1)S(1)}, bf16[256,2048]{1,0:T(8,128)(2,1)S(1)}, u32[]{:S(2)}, u32[]{:S(2)}) %collective-permute-start.29) | collective-permute-done | bytes 1048608 | tf_op jit(solution)/shard_map/ppermute | solution.py:49
  537.8 19.7 %collective-permute-done.31 = bf16[256,2048]{1,0:T(8,128)(2,1)S(1)} collective-permute-done((bf16[256,2048]{1,0:T(8,128)(2,1)S(1)}, bf16[256,2048]{1,0:T(8,128)(2,1)S(1)}, u32[]{:S(2)}, u32[]{:S(2)}) %collective-permute-start.31) | collective-permute-done | bytes 1048608 | tf_op jit(solution)/shard_map/ppermute | solution.py:49
  561.2 11.0 %convolution_convert_fusion.3 = bf16[1024,2048]{1,0:T(8,128)(2,1)} fusion(bf16[2048,1024]{1,0:T(8,128)(2,1)S(1)} %copy-done.40, bf16[2048,2048]{1,0:T(8,128)(2,1)S(1)} %bitcast.282), kind=kOutput, calls=%fused_computation.23 | convolution fusion | flops 8592031744 | bytes 16777216 | tf_op jit(solution)/shard_map/dot_general | solution.py:37
  620.3 11.6 %attend_back_kernel.4 = (bf16[256,2048]{1,0:T(8,128)(2,1)S(1)}, f32[384,512]{1,0:T(8,128)S(1)}, f32[384,512]{1,0:T(8,128)S(1)}, f32[2,32,64,128]{3,2,1,0:T(8,128)}, f32[2,8,64,128]{3,2,1,0:T(8,128)S(1)}) custom-call(bf16[256,3072]{1,0:T(8,128)(2,1)} %rope.2.refs_0_, bf16[384,1024]{1,0:T(8,128)(2,1)S(1)} %bitcast.262, bf16[384,1024]{1,0:T(8,128)(2,1)S(1)} %bitcast.263, ...), custom_call_target="tpu_custom_call" | custom-call | flops 786432000 | bytes 4017152 | tf_op jit(solution)/shard_map/attend_back_kernel/pallas_call | solution.py:547
  647.9 12.0 %attend_back_kernel.5 = (bf16[256,2048]{1,0:T(8,128)(2,1)S(1)}, f32[384,512]{1,0:T(8,128)S(1)}, f32[384,512]{1,0:T(8,128)S(1)}, f32[2,32,64,128]{3,2,1,0:T(8,128)}, f32[2,8,64,128]{3,2,1,0:T(8,128)S(1)}) custom-call(bf16[256,3072]{1,0:T(8,128)(2,1)} %rope.2.refs_0_, ...), custom_call_target="tpu_custom_call", output_to_operand_aliasing={{0}: (12, {}), {1}: (13, {}), {2}: (14, {}), {3}: (15, {}),... | custom-call | flops 786432000 | bytes 4017152 | tf_op jit(solution)/shard_map/attend_back_kernel/pallas_call | solution.py:547
  663.9 18.9 %collective-permute-done.36 = bf16[2,8,80,128]{3,2,1,0:T(8,128)(2,1)S(1)} collective-permute-done((bf16[2,8,80,128]{3,2,1,0:T(8,128)(2,1)S(1)}, bf16[2,8,80,128]{3,2,1,0:T(8,128)(2,1)S(1)}, u32[]{:S(2)}, u32[]{:S(2)}) %collective-permute-start.36) | collective-permute-done | bytes 327712 | tf_op jit(solution)/shard_map/ppermute | solution.py:49
  693.9 11.8 %attend_back_kernel.6 = (bf16[256,2048]{1,0:T(8,128)(2,1)S(1)}, f32[384,512]{1,0:T(8,128)S(1)}, f32[384,512]{1,0:T(8,128)S(1)}, f32[2,32,64,128]{3,2,1,0:T(8,128)}, f32[2,8,64,128]{3,2,1,0:T(8,128)S(1)}) custom-call(bf16[256,3072]{1,0:T(8,128)(2,1)} %rope.2.refs_0_, ...), custom_call_target="tpu_custom_call", output_to_operand_aliasing={{0}: (12, {}), {1}: (13, {}), {2}: (14, {}), {3}: (15, {}),... | custom-call | flops 786432000 | bytes 4017152 | tf_op jit(solution)/shard_map/attend_back_kernel/pallas_call | solution.py:547
  713.8 11.8 %attend_back_kernel.7 = (bf16[256,2048]{1,0:T(8,128)(2,1)S(1)}, f32[384,512]{1,0:T(8,128)S(1)}, f32[384,512]{1,0:T(8,128)S(1)}, f32[2,32,64,128]{3,2,1,0:T(8,128)}, f32[2,8,64,128]{3,2,1,0:T(8,128)S(1)}) custom-call(bf16[256,3072]{1,0:T(8,128)(2,1)} %rope.2.refs_0_, ...), custom_call_target="tpu_custom_call", output_to_operand_aliasing={{0}: (12, {}), {1}: (13, {}), {2}: (14, {}), {3}: (15, {}),... | custom-call | flops 786432000 | bytes 4017152 | tf_op jit(solution)/shard_map/attend_back_kernel/pallas_call | solution.py:547
  828.1 19.3 %collective-permute-done.51 = bf16[64,4096]{1,0:T(8,128)(2,1)} collective-permute-done((bf16[64,4096]{1,0:T(8,128)(2,1)}, bf16[64,4096]{1,0:T(8,128)(2,1)}, u32[]{:S(2)}, u32[]{:S(2)}) %collective-permute-start.51) | collective-permute-done | bytes 524320 | tf_op jit(solution)/shard_map/ppermute | solution.py:49
  889.5 20.3 %collective-permute-done.55 = bf16[4,64,2048]{2,1,0:T(8,128)(2,1)} collective-permute-done((bf16[4,64,2048]{2,1,0:T(8,128)(2,1)}, bf16[4,64,2048]{2,1,0:T(8,128)(2,1)}, u32[]{:S(2)}, u32[]{:S(2)}) %collective-permute-start.55) | collective-permute-done | bytes 1048608 | tf_op jit(solution)/shard_map/ppermute | solution.py:49
  942.5 17.1 %collective-permute-done.57 = bf16[4,64,1280]{2,1,0:T(8,128)(2,1)S(1)} collective-permute-done((bf16[4,64,1280]{2,1,0:T(8,128)(2,1)S(1)}, bf16[4,64,1280]{2,1,0:T(8,128)(2,1)S(1)}, u32[]{:S(2)}, u32[]{:S(2)}) %collective-permute-start.57) | collective-permute-done | bytes 655392 | tf_op jit(solution)/shard_map/ppermute | solution.py:49
  997.3 10.8 %whole_rows.1 = f32[2,64,16384]{2,1,0:T(8,128)} custom-call(bf16[2,64,16384]{2,1,0:T(8,128)(2,1)} %all-gather.9.cloned.1.call-done.in_ref), custom_call_target="tpu_custom_call" | custom-call | bytes 12582912 | tf_op jit(solution)/shard_map/whole_rows/pallas_call | solution.py:259
  (687 shorter events, 527.5 us)
Async XLA Ops:
  7.2 159.1 %all-gather.5.cloned.1.call-start = ((), (), s32[]{:S(2)}) async-start(), calls=%async_computation.3 | async-start | bytes 23396352 | tf_op jit(solution)/shard_map/all_gather | solution.py:743
  16.3 317.7 %all-gather.7.cloned.1.call-start = ((), (), s32[]{:S(2)}) async-start(), calls=%async_computation.4 | async-start | bytes 9437184 | tf_op jit(solution)/shard_map/all_gather | solution.py:818
  70.4 35.4 %collective-permute-start.2 = (bf16[64,4096]{1,0:T(8,128)(2,1)S(1)}, bf16[64,4096]{1,0:T(8,128)(2,1)S(1)}, u32[]{:S(2)}, u32[]{:S(2)}) collective-permute-start(bf16[64,4096]{1,0:T(8,128)(2,1)S(1)} %pad_maximum_fusion.11), channel_id=1, source_target_pairs={{0,8},{4,12},{8,0},{12,4},{1,9},{5,13},{9,1},{13,5},{2,10},{6,14},... | collective-permute-start | bytes 1572872 | tf_op jit(solution)/shard_map/ppermute | solution.py:49
  111.7 55.9 %collective-permute-start.4 = (bf16[4,2,64,2048]{3,2,1,0:T(8,128)(2,1)}, bf16[4,2,64,2048]{3,2,1,0:T(8,128)(2,1)}, u32[]{:S(2)}, u32[]{:S(2)}) collective-permute-start(bf16[4,2,64,2048]{3,2,1,0:T(8,128)(2,1)} %pad_maximum_fusion.1.refs_0_), channel_id=1, source_target_pairs={{0,16},{16,0},{1,17},{17,1},{2,18},{18,2},{3,19},{19,3},{4,20},{20... | collective-permute-start | bytes 6291464 | tf_op jit(solution)/shard_map/ppermute | solution.py:49
  167.7 470.2 %reduce-scatter.6.cloned.1.call-start = ((), (), s32[]{:S(2)}) async-start(), calls=%async_computation.6 | async-start | bytes 12582912 | tf_op jit(solution)/shard_map/reduce_scatter | solution.py:887
  237.0 47.0 %collective-permute-start.13 = (bf16[2,2,64,2048]{3,2,1,0:T(8,128)(2,1)}, bf16[2,2,64,2048]{3,2,1,0:T(8,128)(2,1)}, u32[]{:S(2)}, u32[]{:S(2)}) collective-permute-start(bf16[2,2,64,2048]{3,2,1,0:T(8,128)(2,1)} %collective-permute-done.5.refs_2_), channel_id=1, source_target_pairs={{0,16},{16,0},{1,17},{17,1},{2,18},{18,2},{3,19},{19,3},{4,20},{20... | collective-permute-start | bytes 3145736 | tf_op jit(solution)/shard_map/ppermute | solution.py:49
  244.5 37.8 %collective-permute-start.10 = (bf16[2,2,64,2048]{3,2,1,0:T(8,128)(2,1)}, bf16[2,2,64,2048]{3,2,1,0:T(8,128)(2,1)}, u32[]{:S(2)}, u32[]{:S(2)}) collective-permute-start(bf16[2,2,64,2048]{3,2,1,0:T(8,128)(2,1)} %fusion.32), channel_id=1, source_target_pairs={{0,2},{2,0},{1,3},{3,1},{4,6},{6,4},{5,7},{7,5},{8,10},{10,8},{9,1... | collective-permute-start | bytes 3145736 | tf_op jit(solution)/shard_map/ppermute | solution.py:49
  282.3 46.6 %collective-permute-start.21 = (bf16[512,2048]{1,0:T(8,128)(2,1)}, bf16[512,2048]{1,0:T(8,128)(2,1)}, u32[]{:S(2)}, u32[]{:S(2)}) collective-permute-start(bf16[512,2048]{1,0:T(8,128)(2,1)} %param.31), channel_id=1, source_target_pairs={{0,2},{2,0},{1,3},{3,1},{4,6},{6,4},{5,7},{7,5},{8,10},{10,8},{9,1... | collective-permute-start | bytes 6291464 | tf_op jit(solution)/shard_map/ppermute | solution.py:49
  304.3 54.6 %collective-permute-start.14 = (bf16[256,2048]{1,0:T(8,128)(2,1)}, bf16[256,2048]{1,0:T(8,128)(2,1)}, u32[]{:S(2)}, u32[]{:S(2)}) collective-permute-start(bf16[256,2048]{1,0:T(8,128)(2,1)} %multiply_convert_fusion.own_ref), channel_id=1, source_target_pairs={{0,4},{4,0},{8,12},{12,8},{1,5},{5,1},{9,13},{13,9},{2,6},{6,2},{1... | collective-permute-start | bytes 3145736 | tf_op jit(solution)/shard_map/ppermute | solution.py:49
  310.4 48.4 %collective-permute-start.15 = (bf16[256,2048]{1,0:T(8,128)(2,1)}, bf16[256,2048]{1,0:T(8,128)(2,1)}, u32[]{:S(2)}, u32[]{:S(2)}) collective-permute-start(bf16[256,2048]{1,0:T(8,128)(2,1)} %multiply_convert_fusion.own_ref), channel_id=1, source_target_pairs={{4,8},{8,4},{5,9},{9,5},{6,10},{10,6},{7,11},{11,7},{20,24},{24,20... | collective-permute-start | bytes 3145736 | tf_op jit(solution)/shard_map/ppermute | solution.py:49
  362.7 36.8 %collective-permute-start.16 = (bf16[256,2048]{1,0:T(8,128)(2,1)}, bf16[256,2048]{1,0:T(8,128)(2,1)}, u32[]{:S(2)}, u32[]{:S(2)}) collective-permute-start(bf16[256,2048]{1,0:T(8,128)(2,1)} %collective-permute-done.14.own_ref), channel_id=1, source_target_pairs={{4,8},{8,4},{5,9},{9,5},{6,10},{10,6},{7,11},{11,7},{20,24},{24,20... | collective-permute-start | bytes 3145736 | tf_op jit(solution)/shard_map/ppermute | solution.py:49
  364.3 32.9 %collective-permute-start.17 = (bf16[256,2048]{1,0:T(8,128)(2,1)}, bf16[256,2048]{1,0:T(8,128)(2,1)}, u32[]{:S(2)}, u32[]{:S(2)}) collective-permute-start(bf16[256,2048]{1,0:T(8,128)(2,1)} %collective-permute-done.15), channel_id=1, source_target_pairs={{4,0},{8,12},{5,1},{9,13},{6,2},{10,14},{7,3},{11,15},{20,16},{24,... | collective-permute-start | bytes 3145736 | tf_op jit(solution)/shard_map/ppermute | solution.py:49
  490.5 219.2 %reduce-scatter.4.cloned.1.call-start = ((), (), s32[]{:S(2)}) async-start(), calls=%async_computation.5 | async-start | bytes 9437184 | tf_op jit(solution)/shard_map/reduce_scatter | solution.py:893
  584.8 328.8 %reduce-scatter.8.cloned.1.call-start = ((), (), s32[]{:S(2)}) async-start(), calls=%async_computation.8 | async-start | bytes 6291456 | tf_op jit(solution)/shard_map/reduce_scatter | solution.py:887
  613.4 34.5 %collective-permute-start.39 = (bf16[1024,2048]{1,0:T(8,128)(2,1)}, bf16[1024,2048]{1,0:T(8,128)(2,1)}, u32[]{:S(2)}, u32[]{:S(2)}) collective-permute-start(bf16[1024,2048]{1,0:T(8,128)(2,1)} %convolution_convert_fusion.1), channel_id=1, source_target_pairs={{0,1},{1,0},{2,3},{3,2},{4,5},{5,4},{6,7},{7,6},{8,9},{9,8},{10,11... | collective-permute-start | bytes 12582920 | tf_op jit(solution)/shard_map/ppermute | solution.py:49
  644.6 64.8 %collective-permute-start.38 = (bf16[4,128,2048]{2,1,0:T(8,128)(2,1)}, bf16[4,128,2048]{2,1,0:T(8,128)(2,1)}, u32[]{:S(2)}, u32[]{:S(2)}) collective-permute-start(bf16[4,128,2048]{2,1,0:T(8,128)(2,1)} %dynamic-slice_bitcast_fusion), channel_id=1, source_target_pairs={{0,2},{2,0},{1,3},{3,1},{4,6},{6,4},{5,7},{7,5},{8,10},{10,8},{9,1... | collective-permute-start | bytes 6291464 | tf_op jit(solution)/shard_map/ppermute | solution.py:49
  709.4 52.5 %collective-permute-start.42 = (bf16[512,2048]{1,0:T(8,128)(2,1)}, bf16[512,2048]{1,0:T(8,128)(2,1)}, u32[]{:S(2)}, u32[]{:S(2)}) collective-permute-start(bf16[512,2048]{1,0:T(8,128)(2,1)} %slice.298), channel_id=1, source_target_pairs={{0,2},{2,0},{1,3},{3,1},{4,6},{6,4},{5,7},{7,5},{8,10},{10,8},{9,1... | collective-permute-start | bytes 6291464 | tf_op jit(solution)/shard_map/ppermute | solution.py:49
  747.0 250.3 %all-gather.9.cloned.1.call-start = ((), (), s32[]{:S(2)}) async-start(), calls=%async_computation.7 | async-start | bytes 6291456 | tf_op jit(solution)/shard_map/all_gather | solution.py:1001
  766.0 48.6 %collective-permute-start.48 = (bf16[4,64,2048]{2,1,0:T(8,128)(2,1)}, bf16[4,64,2048]{2,1,0:T(8,128)(2,1)}, u32[]{:S(2)}, u32[]{:S(2)}) collective-permute-start(bf16[4,64,2048]{2,1,0:T(8,128)(2,1)} %dynamic-slice_bitcast_fusion.3), channel_id=1, source_target_pairs={{0,16},{16,0},{1,17},{17,1},{2,18},{18,2},{3,19},{19,3},{4,20},{20... | collective-permute-start | bytes 3145736 | tf_op jit(solution)/shard_map/ppermute | solution.py:49
  785.1 73.4 %collective-permute-start.44 = (bf16[1024,1024]{1,0:T(8,128)(2,1)}, bf16[1024,1024]{1,0:T(8,128)(2,1)}, u32[]{:S(2)}, u32[]{:S(2)}) collective-permute-start(bf16[1024,1024]{1,0:T(8,128)(2,1)} %convolution_convert_fusion.6), channel_id=1, source_target_pairs={{0,1},{1,0},{2,3},{3,2},{4,5},{5,4},{6,7},{7,6},{8,9},{9,8},{10,11... | collective-permute-start | bytes 6291464 | tf_op jit(solution)/shard_map/ppermute | solution.py:49
  788.0 85.2 %collective-permute-start.46 = (bf16[512,2048]{1,0:T(8,128)(2,1)}, bf16[512,2048]{1,0:T(8,128)(2,1)}, u32[]{:S(2)}, u32[]{:S(2)}) collective-permute-start(bf16[512,2048]{1,0:T(8,128)(2,1)} %slice.250), channel_id=1, source_target_pairs={{0,2},{2,0},{1,3},{3,1},{4,6},{6,4},{5,7},{7,5},{8,10},{10,8},{9,1... | collective-permute-start | bytes 6291464 | tf_op jit(solution)/shard_map/ppermute | solution.py:49
  873.3 41.7 %collective-permute-start.47 = (bf16[512,1280]{1,0:T(8,128)(2,1)}, bf16[512,1280]{1,0:T(8,128)(2,1)}, u32[]{:S(2)}, u32[]{:S(2)}) collective-permute-start(bf16[512,1280]{1,0:T(8,128)(2,1)} %pad_maximum_fusion.5), channel_id=1, source_target_pairs={{0,2},{2,0},{1,3},{3,1},{4,6},{6,4},{5,7},{7,5},{8,10},{10,8},{9,1... | collective-permute-start | bytes 3932168 | tf_op jit(solution)/shard_map/ppermute | solution.py:49
  886.8 124.7 %all-gather.11.cloned.1.call-start = ((), (), s32[]{:S(2)}) async-start(), calls=%async_computation.9 | async-start | bytes 3145728 | tf_op jit(solution)/shard_map/all_gather | solution.py:1005
  915.1 61.3 %collective-permute-start.66 = (bf16[256,2048]{1,0:T(8,128)(2,1)S(1)}, bf16[256,2048]{1,0:T(8,128)(2,1)S(1)}, u32[]{:S(2)}, u32[]{:S(2)}) collective-permute-start(bf16[256,2048]{1,0:T(8,128)(2,1)S(1)} %dynamic-slice_bitcast_fusion.1), channel_id=1, source_target_pairs={{0,2},{2,0},{1,3},{3,1},{4,6},{6,4},{5,7},{7,5},{8,10},{10,8},{9,1... | collective-permute-start | bytes 3145736 | tf_op jit(solution)/shard_map/ppermute | solution.py:49
  (197 other events, 2349.7 us)
Sparse Core Ops, SparseCore 0:
  16.5 149.8 all-gather.4
  167.9 89.5 all-gather.6
  490.7 103.3 reduce-scatter.5
  596.3 98.8 reduce-scatter.3
  747.1 79.3 reduce-scatter.7
  886.9 86.0 all-gather.8
  977.9 33.5 all-gather.10

commit v4 on v3

--- a/solution.py
+++ b/solution.py
@@ -806,7 +806,7 @@
     projected = mm(n1, wqkv) + SCALE * mm(adapt, aup_wide)
     qkv = rope(projected, cosine, sine, 5)
     kv = qkv[:, D:].reshape(micros, rows, 2 * KVW)
-    crossing = ("x", "outer", "middle", "c")
+    crossing = ("x", "outer", "middle")
     halo = links.move(kv[:, rows - WINDOW :], *chain, crossing)
     kv_ext = jnp.concatenate([halo, kv], axis=1).reshape(micros * extent, 2 * KVW)
     launch = lambda kernel, ins, outs, args, work, **k: call(

time: 1030 us -> 1040 us (level)
  waiting for transfers between devices: 365 us -> 351 us
    ppermute x66, waiting for transfers between devices: 308 us -> 293 us  [move(): out = lax.ppermute(a, axis, pairs)]
    unnamed x328 -> x342, local copies, waits for them, and re-layouts: 38.1 us -> 46.6 us
  transfers between devices with their start and end apart: 74 -> 74, of which waited for: 38 -> 35; matrix products, arithmetic and copies ran while one was open for 21% -> 21% of each run, Pallas kernels for 20% -> 20%
where the time goes in v4:
time: 1040 us; the launch traced here: 1030 us
  waiting for transfers between devices  351 us (34%)
  Pallas kernels  226 us (22%)
  starting transfers between devices  137 us (13%)
  local copies, waits for them, and re-layouts  110 us (11%)
  matrix products  93.8 us (9%)
  other arithmetic  93.1 us (9%)
  between operations  17.1 us (2%)
    ppermute x66, waiting for transfers between devices, move(): out = lax.ppermute(a, axis, pairs)  293 us
    ppermute x66, starting transfers between devices, move(): out = lax.ppermute(a, axis, pairs)  135 us
    pallas_call x4, Pallas kernels, ffn_chunk(): pl.pallas_call(ffn_kernel, out_shape=tuple((jax.ShapeDtypeStruct(a, b) fo...  99.3 us
    pallas_call x12, Pallas kernels, call(): pl.pallas_call(body, out_shape=out_shape, grid=(count, pairs), in_specs=[...  97.7 us
    dot_general x12, matrix products, t_mm(): lax.dot_general(a, b, (((0,), (0,)), ((), ())), preferred_element_type=f32)  60.4 us
    all_gather x1, waiting for transfers between devices, per_device(): lax.all_gather(jnp.concatenate([wqkv_own, wout_own, pack], axis=1), every...  53.3 us
    unnamed x342, local copies, waits for them, and re-layouts  46.6 us
  transfers between devices with their start and end apart: 74, of which 35 were waited for; matrix products, arithmetic and copies ran while one was open for 21% of the time, Pallas kernels for 20%

profile of v4, /device:TPU:0, one launch (start us, length us, event | category | flops | bytes accessed | tf_op | source)
XLA Modules:
  0.0 1029.0 jit_solution(15118716354836437887)
XLA Ops:
  22.6 21.6 %collective-permute-done = bf16[64,4096]{1,0:T(8,128)(2,1)S(1)} collective-permute-done((bf16[64,4096]{1,0:T(8,128)(2,1)S(1)}, bf16[64,4096]{1,0:T(8,128)(2,1)S(1)}, u32[]{:S(2)}, u32[]{:S(2)}) %collective-permute-start) | collective-permute-done | bytes 524320 | tf_op jit(solution)/shard_map/ppermute | solution.py:49
  47.5 22.9 %collective-permute-done.1 = bf16[64,4096]{1,0:T(8,128)(2,1)S(1)} collective-permute-done((bf16[64,4096]{1,0:T(8,128)(2,1)S(1)}, bf16[64,4096]{1,0:T(8,128)(2,1)S(1)}, u32[]{:S(2)}, u32[]{:S(2)}) %collective-permute-start.1) | collective-permute-done | bytes 524320 | tf_op jit(solution)/shard_map/ppermute | solution.py:49
  71.4 34.3 %collective-permute-done.2 = bf16[64,4096]{1,0:T(8,128)(2,1)S(1)} collective-permute-done((bf16[64,4096]{1,0:T(8,128)(2,1)S(1)}, bf16[64,4096]{1,0:T(8,128)(2,1)S(1)}, u32[]{:S(2)}, u32[]{:S(2)}) %collective-permute-start.2) | collective-permute-done | bytes 524320 | tf_op jit(solution)/shard_map/ppermute | solution.py:49
  113.0 53.3 %all-gather.5.cloned.1.call-done = bf16[2048,5376]{1,0:T(8,128)(2,1)} async-done(((bf16[128,5376]{1,0:T(8,128)(2,1)}), bf16[2048,5376]{1,0:T(8,128)(2,1)}) %all-gather.5.cloned.1.call-update) | async-done | bytes 22020112 | tf_op jit(solution)/shard_map/all_gather | solution.py:743
  197.9 10.7 %collective-permute-start.6 = (bf16[2,64,1024]{2,1,0:T(8,128)(2,1)S(1)}, bf16[2,64,1024]{2,1,0:T(8,128)(2,1)S(1)}, u32[]{:S(2)}, u32[]{:S(2)}) collective-permute-start(bf16[2,64,1024]{2,1,0:T(8,128)(2,1)S(1)} %slice.281), channel_id=1, source_target_pairs={{0,1},{1,2},{2,3},{3,4},{4,5},{5,6},{6,7},{7,8},{8,9},{9,10},{10,1... | collective-permute-start | bytes 786440 | tf_op jit(solution)/shard_map/ppermute | solution.py:49
  222.5 14.6 %collective-permute-start.9 = (bf16[2,8,80,128]{3,2,1,0:T(8,128)(2,1)S(1)}, bf16[2,8,80,128]{3,2,1,0:T(8,128)(2,1)S(1)}, u32[]{:S(2)}, u32[]{:S(2)}) collective-permute-start(bf16[2,8,80,128]{3,2,1,0:T(8,128)(2,1)S(1)} %fusion.36), channel_id=1, source_target_pairs={{0,2},{2,0},{1,3},{3,1},{4,6},{6,4},{5,7},{7,5},{8,10},{10,8},{9,1... | collective-permute-start | bytes 983048 | tf_op jit(solution)/shard_map/ppermute | solution.py:49
  311.8 10.7 %join_gate_up.1 = bf16[4,2,2,2,64,2048]{5,4,3,2,1,0:T(8,128)(2,1)} custom-call(s32[3]{0:T(128)} %pad_add_fusion.4.at_ref, bf16[4,2,64,2048]{3,2,1,0:T(8,128)(2,1)} %pad_maximum_fusion.1.refs_0_, bf16[4,2,64,2048]{3,2,1,0:T(8,128)(2,1)} %collective-permute-done.4.refs_1_, bf16[2,2,64,2048]{3,2,1,0:T(8,128)(2,1)} %collective-permute-done.5.refs_2_, ...), custom_call_target="tpu_custom_call" | custom-call | bytes 16777216 | tf_op jit(solution)/shard_map/join_gate_up/pallas_call | solution.py:221
  333.9 24.8 %ffn_chunk.4 = (bf16[2048,1024]{1,0:T(8,128)(2,1)}, bf16[2048,2048]{1,0:T(8,128)(2,1)}, bf16[2048,2048]{1,0:T(8,128)(2,1)}, bf16[2048,2048]{1,0:T(8,128)(2,1)}, ...) custom-call(s32[2]{0:T(128)} %pad_add_fusion.3.at_ref, ...), custom_call_target="tpu_custom_call" | custom-call | flops 12884901888 | bytes 33554432 | tf_op jit(solution)/shard_map/ffn_chunk/pallas_call | solution.py:624
  366.6 24.7 %ffn_chunk.5 = (bf16[2048,1024]{1,0:T(8,128)(2,1)}, bf16[2048,2048]{1,0:T(8,128)(2,1)}, bf16[2048,2048]{1,0:T(8,128)(2,1)}, bf16[2048,2048]{1,0:T(8,128)(2,1)}, ...) custom-call(s32[2]{0:T(128)} %pad_add_fusion.2.at_ref, ...), custom_call_target="tpu_custom_call", output_to_operand_aliasing={{0}: (6, {}), {1}: (7, {}), {2}: (8, {}), {3}: (9, {}), {6}... | custom-call | flops 12884901888 | bytes 33554432 | tf_op jit(solution)/shard_map/ffn_chunk/pallas_call | solution.py:624
  401.4 24.7 %ffn_chunk.6 = (bf16[2048,1024]{1,0:T(8,128)(2,1)}, bf16[2048,2048]{1,0:T(8,128)(2,1)}, bf16[2048,2048]{1,0:T(8,128)(2,1)}, bf16[2048,2048]{1,0:T(8,128)(2,1)}, ...) custom-call(s32[2]{0:T(128)} %pad_add_fusion.1.at_ref, ...), custom_call_target="tpu_custom_call", output_to_operand_aliasing={{0}: (6, {}), {1}: (7, {}), {2}: (8, {}), {3}: (9, {}), {6}... | custom-call | flops 12884901888 | bytes 33554432 | tf_op jit(solution)/shard_map/ffn_chunk/pallas_call | solution.py:624
  432.0 25.1 %ffn_chunk.7 = (bf16[2048,1024]{1,0:T(8,128)(2,1)}, bf16[2048,2048]{1,0:T(8,128)(2,1)}, bf16[2048,2048]{1,0:T(8,128)(2,1)}, bf16[2048,2048]{1,0:T(8,128)(2,1)}, ...) custom-call(s32[2]{0:T(128)} %pad_add_fusion.at_ref, ...), custom_call_target="tpu_custom_call", output_to_operand_aliasing={{0}: (6, {}), {1}: (7, {}), {2}: (8, {}), {3}: (9, {}), {6}... | custom-call | flops 12884901888 | bytes 33554432 | tf_op jit(solution)/shard_map/ffn_chunk/pallas_call | solution.py:624
  457.1 23.8 %convolution_convert_fusion = bf16[2048,2048]{1,0:T(8,128)(2,1)} fusion(bf16[2048,2048]{1,0:T(8,128)(2,1)} %get-tuple-element.265, bf16[2048,2048]{1,0:T(8,128)(2,1)} %get-tuple-element.266), kind=kOutput, calls=%fused_computation.7 | convolution fusion | flops 17184063488 | bytes 25165824 | tf_op jit(solution)/shard_map/dot_general | solution.py:37
  501.5 22.8 %collective-permute-done.29 = bf16[256,2048]{1,0:T(8,128)(2,1)S(1)} collective-permute-done((bf16[256,2048]{1,0:T(8,128)(2,1)S(1)}, bf16[256,2048]{1,0:T(8,128)(2,1)S(1)}, u32[]{:S(2)}, u32[]{:S(2)}) %collective-permute-start.29) | collective-permute-done | bytes 1048608 | tf_op jit(solution)/shard_map/ppermute | solution.py:49
  539.2 19.7 %collective-permute-done.31 = bf16[256,2048]{1,0:T(8,128)(2,1)S(1)} collective-permute-done((bf16[256,2048]{1,0:T(8,128)(2,1)S(1)}, bf16[256,2048]{1,0:T(8,128)(2,1)S(1)}, u32[]{:S(2)}, u32[]{:S(2)}) %collective-permute-start.31) | collective-permute-done | bytes 1048608 | tf_op jit(solution)/shard_map/ppermute | solution.py:49
  562.6 11.1 %convolution_convert_fusion.3 = bf16[1024,2048]{1,0:T(8,128)(2,1)} fusion(bf16[2048,1024]{1,0:T(8,128)(2,1)S(1)} %copy-done.41, bf16[2048,2048]{1,0:T(8,128)(2,1)S(1)} %bitcast.282), kind=kOutput, calls=%fused_computation.23 | convolution fusion | flops 8592031744 | bytes 16777216 | tf_op jit(solution)/shard_map/dot_general | solution.py:37
  626.6 11.6 %attend_back_kernel.4 = (bf16[256,2048]{1,0:T(8,128)(2,1)S(1)}, f32[384,512]{1,0:T(8,128)S(1)}, f32[384,512]{1,0:T(8,128)S(1)}, f32[2,32,64,128]{3,2,1,0:T(8,128)}, f32[2,8,64,128]{3,2,1,0:T(8,128)S(1)}) custom-call(bf16[256,3072]{1,0:T(8,128)(2,1)} %rope.2.refs_0_, bf16[384,1024]{1,0:T(8,128)(2,1)S(1)} %bitcast.262, bf16[384,1024]{1,0:T(8,128)(2,1)S(1)} %bitcast.263, ...), custom_call_target="tpu_custom_call" | custom-call | flops 786432000 | bytes 4017152 | tf_op jit(solution)/shard_map/attend_back_kernel/pallas_call | solution.py:547
  654.2 11.9 %attend_back_kernel.5 = (bf16[256,2048]{1,0:T(8,128)(2,1)S(1)}, f32[384,512]{1,0:T(8,128)S(1)}, f32[384,512]{1,0:T(8,128)S(1)}, f32[2,32,64,128]{3,2,1,0:T(8,128)}, f32[2,8,64,128]{3,2,1,0:T(8,128)S(1)}) custom-call(bf16[256,3072]{1,0:T(8,128)(2,1)} %rope.2.refs_0_, ...), custom_call_target="tpu_custom_call", output_to_operand_aliasing={{0}: (12, {}), {1}: (13, {}), {2}: (14, {}), {3}: (15, {}),... | custom-call | flops 786432000 | bytes 4017152 | tf_op jit(solution)/shard_map/attend_back_kernel/pallas_call | solution.py:547
  674.4 13.7 %collective-permute-done.36 = bf16[2,8,80,128]{3,2,1,0:T(8,128)(2,1)S(1)} collective-permute-done((bf16[2,8,80,128]{3,2,1,0:T(8,128)(2,1)S(1)}, bf16[2,8,80,128]{3,2,1,0:T(8,128)(2,1)S(1)}, u32[]{:S(2)}, u32[]{:S(2)}) %collective-permute-start.36) | collective-permute-done | bytes 327712 | tf_op jit(solution)/shard_map/ppermute | solution.py:49
  698.2 11.7 %attend_back_kernel.6 = (bf16[256,2048]{1,0:T(8,128)(2,1)S(1)}, f32[384,512]{1,0:T(8,128)S(1)}, f32[384,512]{1,0:T(8,128)S(1)}, f32[2,32,64,128]{3,2,1,0:T(8,128)}, f32[2,8,64,128]{3,2,1,0:T(8,128)S(1)}) custom-call(bf16[256,3072]{1,0:T(8,128)(2,1)} %rope.2.refs_0_, ...), custom_call_target="tpu_custom_call", output_to_operand_aliasing={{0}: (12, {}), {1}: (13, {}), {2}: (14, {}), {3}: (15, {}),... | custom-call | flops 786432000 | bytes 4017152 | tf_op jit(solution)/shard_map/attend_back_kernel/pallas_call | solution.py:547
  718.1 11.8 %attend_back_kernel.7 = (bf16[256,2048]{1,0:T(8,128)(2,1)S(1)}, f32[384,512]{1,0:T(8,128)S(1)}, f32[384,512]{1,0:T(8,128)S(1)}, f32[2,32,64,128]{3,2,1,0:T(8,128)}, f32[2,8,64,128]{3,2,1,0:T(8,128)S(1)}) custom-call(bf16[256,3072]{1,0:T(8,128)(2,1)} %rope.2.refs_0_, ...), custom_call_target="tpu_custom_call", output_to_operand_aliasing={{0}: (12, {}), {1}: (13, {}), {2}: (14, {}), {3}: (15, {}),... | custom-call | flops 786432000 | bytes 4017152 | tf_op jit(solution)/shard_map/attend_back_kernel/pallas_call | solution.py:547
  831.6 19.6 %collective-permute-done.51 = bf16[64,4096]{1,0:T(8,128)(2,1)} collective-permute-done((bf16[64,4096]{1,0:T(8,128)(2,1)}, bf16[64,4096]{1,0:T(8,128)(2,1)}, u32[]{:S(2)}, u32[]{:S(2)}) %collective-permute-start.51) | collective-permute-done | bytes 524320 | tf_op jit(solution)/shard_map/ppermute | solution.py:49
  891.9 21.3 %collective-permute-done.55 = bf16[4,64,2048]{2,1,0:T(8,128)(2,1)} collective-permute-done((bf16[4,64,2048]{2,1,0:T(8,128)(2,1)}, bf16[4,64,2048]{2,1,0:T(8,128)(2,1)}, u32[]{:S(2)}, u32[]{:S(2)}) %collective-permute-start.55) | collective-permute-done | bytes 1048608 | tf_op jit(solution)/shard_map/ppermute | solution.py:49
  948.1 16.3 %collective-permute-done.57 = bf16[4,64,1280]{2,1,0:T(8,128)(2,1)S(1)} collective-permute-done((bf16[4,64,1280]{2,1,0:T(8,128)(2,1)S(1)}, bf16[4,64,1280]{2,1,0:T(8,128)(2,1)S(1)}, u32[]{:S(2)}, u32[]{:S(2)}) %collective-permute-start.57) | collective-permute-done | bytes 655392 | tf_op jit(solution)/shard_map/ppermute | solution.py:49
  1002.3 10.8 %whole_rows.1 = f32[2,64,16384]{2,1,0:T(8,128)} custom-call(bf16[2,64,16384]{2,1,0:T(8,128)(2,1)} %all-gather.9.cloned.1.call-done.in_ref), custom_call_target="tpu_custom_call" | custom-call | bytes 12582912 | tf_op jit(solution)/shard_map/whole_rows/pallas_call | solution.py:259
  (701 shorter events, 538.2 us)
Async XLA Ops:
  7.2 159.1 %all-gather.5.cloned.1.call-start = ((), (), s32[]{:S(2)}) async-start(), calls=%async_computation.3 | async-start | bytes 23396352 | tf_op jit(solution)/shard_map/all_gather | solution.py:743
  16.3 317.6 %all-gather.7.cloned.1.call-start = ((), (), s32[]{:S(2)}) async-start(), calls=%async_computation.4 | async-start | bytes 9437184 | tf_op jit(solution)/shard_map/all_gather | solution.py:818
  70.4 35.4 %collective-permute-start.2 = (bf16[64,4096]{1,0:T(8,128)(2,1)S(1)}, bf16[64,4096]{1,0:T(8,128)(2,1)S(1)}, u32[]{:S(2)}, u32[]{:S(2)}) collective-permute-start(bf16[64,4096]{1,0:T(8,128)(2,1)S(1)} %pad_maximum_fusion.11), channel_id=1, source_target_pairs={{0,8},{4,12},{8,0},{12,4},{1,9},{5,13},{9,1},{13,5},{2,10},{6,14},... | collective-permute-start | bytes 1572872 | tf_op jit(solution)/shard_map/ppermute | solution.py:49
  111.7 55.9 %collective-permute-start.4 = (bf16[4,2,64,2048]{3,2,1,0:T(8,128)(2,1)}, bf16[4,2,64,2048]{3,2,1,0:T(8,128)(2,1)}, u32[]{:S(2)}, u32[]{:S(2)}) collective-permute-start(bf16[4,2,64,2048]{3,2,1,0:T(8,128)(2,1)} %pad_maximum_fusion.1.refs_0_), channel_id=1, source_target_pairs={{0,16},{16,0},{1,17},{17,1},{2,18},{18,2},{3,19},{19,3},{4,20},{20... | collective-permute-start | bytes 6291464 | tf_op jit(solution)/shard_map/ppermute | solution.py:49
  167.7 476.5 %reduce-scatter.6.cloned.1.call-start = ((), (), s32[]{:S(2)}) async-start(), calls=%async_computation.6 | async-start | bytes 12582912 | tf_op jit(solution)/shard_map/reduce_scatter | solution.py:887
  238.4 45.6 %collective-permute-start.13 = (bf16[2,2,64,2048]{3,2,1,0:T(8,128)(2,1)}, bf16[2,2,64,2048]{3,2,1,0:T(8,128)(2,1)}, u32[]{:S(2)}, u32[]{:S(2)}) collective-permute-start(bf16[2,2,64,2048]{3,2,1,0:T(8,128)(2,1)} %collective-permute-done.5.refs_2_), channel_id=1, source_target_pairs={{0,16},{16,0},{1,17},{17,1},{2,18},{18,2},{3,19},{19,3},{4,20},{20... | collective-permute-start | bytes 3145736 | tf_op jit(solution)/shard_map/ppermute | solution.py:49
  245.8 36.6 %collective-permute-start.10 = (bf16[2,2,64,2048]{3,2,1,0:T(8,128)(2,1)}, bf16[2,2,64,2048]{3,2,1,0:T(8,128)(2,1)}, u32[]{:S(2)}, u32[]{:S(2)}) collective-permute-start(bf16[2,2,64,2048]{3,2,1,0:T(8,128)(2,1)} %fusion.32), channel_id=1, source_target_pairs={{0,2},{2,0},{1,3},{3,1},{4,6},{6,4},{5,7},{7,5},{8,10},{10,8},{9,1... | collective-permute-start | bytes 3145736 | tf_op jit(solution)/shard_map/ppermute | solution.py:49
  282.4 46.4 %collective-permute-start.21 = (bf16[512,2048]{1,0:T(8,128)(2,1)}, bf16[512,2048]{1,0:T(8,128)(2,1)}, u32[]{:S(2)}, u32[]{:S(2)}) collective-permute-start(bf16[512,2048]{1,0:T(8,128)(2,1)} %param.31), channel_id=1, source_target_pairs={{0,2},{2,0},{1,3},{3,1},{4,6},{6,4},{5,7},{7,5},{8,10},{10,8},{9,1... | collective-permute-start | bytes 6291464 | tf_op jit(solution)/shard_map/ppermute | solution.py:49
  304.3 54.4 %collective-permute-start.14 = (bf16[256,2048]{1,0:T(8,128)(2,1)}, bf16[256,2048]{1,0:T(8,128)(2,1)}, u32[]{:S(2)}, u32[]{:S(2)}) collective-permute-start(bf16[256,2048]{1,0:T(8,128)(2,1)} %multiply_convert_fusion.own_ref), channel_id=1, source_target_pairs={{0,4},{4,0},{8,12},{12,8},{1,5},{5,1},{9,13},{13,9},{2,6},{6,2},{1... | collective-permute-start | bytes 3145736 | tf_op jit(solution)/shard_map/ppermute | solution.py:49
  310.6 48.2 %collective-permute-start.15 = (bf16[256,2048]{1,0:T(8,128)(2,1)}, bf16[256,2048]{1,0:T(8,128)(2,1)S(1)}, u32[]{:S(2)}, u32[]{:S(2)}) collective-permute-start(bf16[256,2048]{1,0:T(8,128)(2,1)} %multiply_convert_fusion.own_ref), channel_id=1, source_target_pairs={{4,8},{8,4},{5,9},{9,5},{6,10},{10,6},{7,11},{11,7},{20,24},{24,20... | collective-permute-start | bytes 3145736 | tf_op jit(solution)/shard_map/ppermute | solution.py:49
  362.5 36.0 %collective-permute-start.16 = (bf16[256,2048]{1,0:T(8,128)(2,1)}, bf16[256,2048]{1,0:T(8,128)(2,1)}, u32[]{:S(2)}, u32[]{:S(2)}) collective-permute-start(bf16[256,2048]{1,0:T(8,128)(2,1)} %collective-permute-done.14.own_ref), channel_id=1, source_target_pairs={{4,8},{8,4},{5,9},{9,5},{6,10},{10,6},{7,11},{11,7},{20,24},{24,20... | collective-permute-start | bytes 3145736 | tf_op jit(solution)/shard_map/ppermute | solution.py:49
  364.2 33.0 %collective-permute-start.17 = (bf16[256,2048]{1,0:T(8,128)(2,1)}, bf16[256,2048]{1,0:T(8,128)(2,1)}, u32[]{:S(2)}, u32[]{:S(2)}) collective-permute-start(bf16[256,2048]{1,0:T(8,128)(2,1)} %copy-done.92), channel_id=1, source_target_pairs={{4,0},{8,12},{5,1},{9,13},{6,2},{10,14},{7,3},{11,15},{20,16},{24,... | collective-permute-start | bytes 3145736 | tf_op jit(solution)/shard_map/ppermute | solution.py:49
  489.2 224.8 %reduce-scatter.4.cloned.1.call-start = ((), (), s32[]{:S(2)}) async-start(), calls=%async_computation.5 | async-start | bytes 9437184 | tf_op jit(solution)/shard_map/reduce_scatter | solution.py:893
  586.2 331.8 %reduce-scatter.8.cloned.1.call-start = ((), (), s32[]{:S(2)}) async-start(), calls=%async_computation.8 | async-start | bytes 6291456 | tf_op jit(solution)/shard_map/reduce_scatter | solution.py:887
  619.7 34.4 %collective-permute-start.39 = (bf16[1024,2048]{1,0:T(8,128)(2,1)}, bf16[1024,2048]{1,0:T(8,128)(2,1)}, u32[]{:S(2)}, u32[]{:S(2)}) collective-permute-start(bf16[1024,2048]{1,0:T(8,128)(2,1)} %convolution_convert_fusion.1), channel_id=1, source_target_pairs={{0,1},{1,0},{2,3},{3,2},{4,5},{5,4},{6,7},{7,6},{8,9},{9,8},{10,11... | collective-permute-start | bytes 12582920 | tf_op jit(solution)/shard_map/ppermute | solution.py:49
  650.8 62.9 %collective-permute-start.38 = (bf16[4,128,2048]{2,1,0:T(8,128)(2,1)S(1)}, bf16[4,128,2048]{2,1,0:T(8,128)(2,1)}, u32[]{:S(2)}, u32[]{:S(2)}) collective-permute-start(bf16[4,128,2048]{2,1,0:T(8,128)(2,1)S(1)} %dynamic-slice_bitcast_fusion), channel_id=1, source_target_pairs={{0,2},{2,0},{1,3},{3,1},{4,6},{6,4},{5,7},{7,5},{8,10},{10,8},{9,1... | collective-permute-start | bytes 6291464 | tf_op jit(solution)/shard_map/ppermute | solution.py:49
  713.7 48.4 %collective-permute-start.42 = (bf16[512,2048]{1,0:T(8,128)(2,1)}, bf16[512,2048]{1,0:T(8,128)(2,1)}, u32[]{:S(2)}, u32[]{:S(2)}) collective-permute-start(bf16[512,2048]{1,0:T(8,128)(2,1)} %slice.298), channel_id=1, source_target_pairs={{0,2},{2,0},{1,3},{3,1},{4,6},{6,4},{5,7},{7,5},{8,10},{10,8},{9,1... | collective-permute-start | bytes 6291464 | tf_op jit(solution)/shard_map/ppermute | solution.py:49
  751.4 250.9 %all-gather.9.cloned.1.call-start = ((), (), s32[]{:S(2)}) async-start(), calls=%async_computation.7 | async-start | bytes 6291456 | tf_op jit(solution)/shard_map/all_gather | solution.py:1001
  770.6 48.9 %collective-permute-start.48 = (bf16[4,64,2048]{2,1,0:T(8,128)(2,1)}, bf16[4,64,2048]{2,1,0:T(8,128)(2,1)}, u32[]{:S(2)}, u32[]{:S(2)}) collective-permute-start(bf16[4,64,2048]{2,1,0:T(8,128)(2,1)} %dynamic-slice_bitcast_fusion.3), channel_id=1, source_target_pairs={{0,16},{16,0},{1,17},{17,1},{2,18},{18,2},{3,19},{19,3},{4,20},{20... | collective-permute-start | bytes 3145736 | tf_op jit(solution)/shard_map/ppermute | solution.py:49
  790.4 71.1 %collective-permute-start.44 = (bf16[1024,1024]{1,0:T(8,128)(2,1)}, bf16[1024,1024]{1,0:T(8,128)(2,1)}, u32[]{:S(2)}, u32[]{:S(2)}) collective-permute-start(bf16[1024,1024]{1,0:T(8,128)(2,1)} %convolution_convert_fusion.6), channel_id=1, source_target_pairs={{0,1},{1,0},{2,3},{3,2},{4,5},{5,4},{6,7},{7,6},{8,9},{9,8},{10,11... | collective-permute-start | bytes 6291464 | tf_op jit(solution)/shard_map/ppermute | solution.py:49
  793.2 82.4 %collective-permute-start.46 = (bf16[512,2048]{1,0:T(8,128)(2,1)}, bf16[512,2048]{1,0:T(8,128)(2,1)}, u32[]{:S(2)}, u32[]{:S(2)}) collective-permute-start(bf16[512,2048]{1,0:T(8,128)(2,1)} %slice.250), channel_id=1, source_target_pairs={{0,2},{2,0},{1,3},{3,1},{4,6},{6,4},{5,7},{7,5},{8,10},{10,8},{9,1... | collective-permute-start | bytes 6291464 | tf_op jit(solution)/shard_map/ppermute | solution.py:49
  875.8 46.1 %collective-permute-start.47 = (bf16[512,1280]{1,0:T(8,128)(2,1)}, bf16[512,1280]{1,0:T(8,128)(2,1)}, u32[]{:S(2)}, u32[]{:S(2)}) collective-permute-start(bf16[512,1280]{1,0:T(8,128)(2,1)} %pad_maximum_fusion.5), channel_id=1, source_target_pairs={{0,2},{2,0},{1,3},{3,1},{4,6},{6,4},{5,7},{7,5},{8,10},{10,8},{9,1... | collective-permute-start | bytes 3932168 | tf_op jit(solution)/shard_map/ppermute | solution.py:49
  889.2 128.4 %all-gather.11.cloned.1.call-start = ((), (), s32[]{:S(2)}) async-start(), calls=%async_computation.9 | async-start | bytes 3145728 | tf_op jit(solution)/shard_map/all_gather | solution.py:1005
  921.9 60.2 %collective-permute-start.66 = (bf16[256,2048]{1,0:T(8,128)(2,1)S(1)}, bf16[256,2048]{1,0:T(8,128)(2,1)S(1)}, u32[]{:S(2)}, u32[]{:S(2)}) collective-permute-start(bf16[256,2048]{1,0:T(8,128)(2,1)S(1)} %dynamic-slice_bitcast_fusion.1), channel_id=1, source_target_pairs={{0,2},{2,0},{1,3},{3,1},{4,6},{6,4},{5,7},{7,5},{8,10},{10,8},{9,1... | collective-permute-start | bytes 3145736 | tf_op jit(solution)/shard_map/ppermute | solution.py:49
  (204 other events, 2449.9 us)
Sparse Core Ops, SparseCore 0:
  16.5 149.8 all-gather.4
  167.9 89.4 all-gather.6
  489.4 105.4 reduce-scatter.5
  597.1 96.6 reduce-scatter.3
  751.5 80.1 reduce-scatter.7
  889.3 86.3 all-gather.8
  983.6 33.8 all-gather.10
